TPU v7x, 512 devices: a whole 4x8x8 slice. The times are simulated.
512 devices in a mesh: ctx: 32 (over z_hi, y, core), tp: 16 (over x, z_lo).
Axes of the slice: x: 4, y: 8, z: 8 (z_hi: 2, z_lo: 4; z = z_hi * 4 + z_lo), core: 2. Of those that a mesh axis runs over, the one named last changes fastest.
Arguments:
- residual: bfloat16 [4352, 8192], P('ctx', 'tp'), may hold values from -64 to 64
- gate_first: bfloat16 [4352, 8192], P('ctx', 'tp'), may hold values from -6 to 6
- gate_second: bfloat16 [4352, 8192], P('ctx', 'tp'), may hold values from -6 to 6
- hyena_value: bfloat16 [4352, 8192], P('ctx', 'tp'), may hold values from -6 to 6
- short_taps: float32 [3, 3, 8192], P(None, None, 'tp'), may hold values from -3.5 to 3.5
- long_taps: bfloat16 [128, 8192], P(None, 'tp'), may hold values from -0.5 to 0.5
- norm_gain: float32 [8192], P('tp'), may hold values from 0.1 to 1.9
- queries: bfloat16 [4352, 8192], P('ctx', 'tp'), may hold values from -8 to 8
- attn_keys: bfloat16 [4352, 8192], P('ctx', 'tp'), may hold values from -8 to 8
Outputs:
- stream: bfloat16 [4352, 8192], P('ctx', 'tp')
- attended: bfloat16 [4352, 8192], P('ctx', 'tp')
All inputs are finite; a program needn't handle non-finite values.
Results may differ from a plain program's by a relative error of at most 0.007.
Values may be sent and summed in bfloat16 or wider, within the bound.
No kernel may reach another device: no remote copies, remote signals or barrier semaphores. Data moves between devices by JAX's collectives and lax.ppermute only.
A program may use at most 64 MiB of HBM per device.

v0:
```python
import math

import jax
import jax.numpy as jnp
from jax import lax
from jax.sharding import PartitionSpec as P

HD = 128


def shifted(value, axis, steps):
    count = lax.axis_size(axis)
    first, last = (max(0, -steps), min(count, count - steps))
    return lax.ppermute(value, axis, [(source, source + steps) for source in range(first, last)])


def featurize(extended, tap_weights, count):
    taps_total = tap_weights.shape[0]
    result = jnp.zeros((count, extended.shape[1]), jnp.float32)
    for lag_index in range(taps_total):
        begin = taps_total - 1 - lag_index
        result = result + tap_weights[lag_index] * extended[begin : begin + count].astype(
            jnp.float32
        )
    return result


def long_filter(extended, long_taps, count):
    filter_len = long_taps.shape[0]
    padded = extended.astype(jnp.float32)
    tap_table = long_taps.astype(jnp.float32)

    def tap_group(group_index, running):
        for inner_index in range(8):
            lag_index = group_index * 8 + inner_index
            window = lax.dynamic_slice_in_dim(padded, filter_len - 1 - lag_index, count, 0)
            running = (
                running + lax.dynamic_index_in_dim(tap_table, lag_index, 0, keepdims=False) * window
            )
        return running

    return lax.fori_loop(
        0, filter_len // 8, tap_group, jnp.zeros((count, extended.shape[1]), jnp.float32)
    )


def shards(
    residual,
    gate_first,
    gate_second,
    hyena_value,
    short_taps,
    long_taps,
    norm_gain,
    queries,
    attn_keys,
):
    rows = residual.shape[0]
    chans = residual.shape[1]
    filter_len = long_taps.shape[0]
    reach = short_taps.shape[1]
    prev_first, prev_second, prev_value = shifted(
        (
            gate_first[rows - reach + 1 :],
            gate_second[rows - reach + 1 :],
            hyena_value[rows - reach + 1 :],
        ),
        "ctx",
        1,
    )
    feat_first = featurize(jnp.concatenate([prev_first, gate_first], axis=0), short_taps[0], rows)
    feat_second = featurize(
        jnp.concatenate([prev_second, gate_second], axis=0), short_taps[1], rows
    )
    feat_value = featurize(jnp.concatenate([prev_value, hyena_value], axis=0), short_taps[2], rows)
    product = (feat_first * feat_value).astype(jnp.bfloat16)
    prev_product = shifted(product[rows - filter_len + 1 :], "ctx", 1)
    extended = jnp.concatenate([prev_product, product], axis=0)
    filtered = long_filter(extended, long_taps, rows)
    stream = (residual.astype(jnp.float32) + feat_second * filtered).astype(jnp.bfloat16)
    stream_f = stream.astype(jnp.float32)
    row_squares = jnp.sum(stream_f * stream_f, axis=1)
    row_totals = lax.psum(row_squares, "tp")
    inverse = 1.0 / jnp.sqrt(row_totals / (chans * lax.axis_size("tp")) + 1e-06)
    heads = chans // HD
    scale = 1.0 / math.sqrt(HD)
    my_index = lax.axis_index("ctx")
    query_pos = my_index * rows + jnp.arange(rows)
    last_query = my_index * rows + rows - 1
    query_heads = queries.reshape(rows, heads, HD)
    init_state = (
        jnp.full((heads, rows), -1e30, jnp.float32),
        jnp.zeros((heads, rows), jnp.float32),
        jnp.zeros((rows, heads, HD), jnp.float32),
    )
    values = (stream_f * inverse[:, None] * norm_gain).astype(jnp.bfloat16)
    key_piece = lax.all_gather(attn_keys, "ctx", axis=0, tiled=True)
    raw_piece = lax.all_gather(values, "ctx", axis=0, tiled=True)
    piece_rows = key_piece.shape[0]
    block = math.gcd(piece_rows, 1536)

    def block_step(block_index, state):
        offset = block_index * block
        key_block = lax.dynamic_slice_in_dim(key_piece, offset, block, 0)
        raw_block = lax.dynamic_slice_in_dim(raw_piece, offset, block, 0)

        def update(current):
            running_max, running_sum, accum = current
            scores = (
                jnp.einsum(
                    "shd,phd->hsp",
                    query_heads,
                    key_block.reshape(block, heads, HD),
                    preferred_element_type=jnp.float32,
                )
                * scale
            )
            key_pos = offset + jnp.arange(block)
            allowed = (key_pos[None, :] <= query_pos[:, None])[None]
            masked = jnp.where(allowed, scores, -1e30)
            new_max = jnp.maximum(running_max, jnp.max(masked, axis=2))
            factor = jnp.exp(running_max - new_max)
            expo = jnp.where(allowed, jnp.exp(scores - new_max[:, :, None]), 0.0)
            new_sum = running_sum * factor + jnp.sum(expo, axis=2)
            weights = expo.astype(jnp.bfloat16)
            contrib = jnp.einsum(
                "hsp,phd->shd",
                weights,
                raw_block.reshape(block, heads, HD),
                preferred_element_type=jnp.float32,
            )
            new_accum = accum * factor.T[:, :, None] + contrib
            return (new_max, new_sum, new_accum)

        def keep_state(current):
            return current

        return lax.cond(offset <= last_query, update, keep_state, state)

    final_state = lax.fori_loop(0, piece_rows // block, block_step, init_state)
    running_sum = final_state[1]
    accum = final_state[2]
    attended = (accum / running_sum.T[:, :, None]).reshape(rows, chans).astype(jnp.bfloat16)
    return (stream, attended)


def solution(mesh):
    placed = (
        P("ctx", "tp"),
        P("ctx", "tp"),
        P("ctx", "tp"),
        P("ctx", "tp"),
        P(None, None, "tp"),
        P(None, "tp"),
        P("tp"),
        P("ctx", "tp"),
        P("ctx", "tp"),
    )
    return jax.shard_map(
        shards,
        mesh=mesh,
        in_specs=placed,
        out_specs=(P("ctx", "tp"), P("ctx", "tp")),
        check_vma=False,
    )
```

profile of v0, /device:TPU:443, one launch (start us, length us, event | category | flops | bytes accessed | tf_op | source)
XLA Modules:
  0.0 276.9 jit_solution(2932315413179396833)
XLA Ops:
  21.2 8.7 %while.36 = (s32[]{:T(128)}, f32[136,512]{1,0:T(8,128)S(1)}, f32[128,512]{1,0:T(8,128)S(1)}, f32[263,512]{1,0:T(8,128)S(1)}, s32[]{:T(128)}, /*index=5*/s32[]{:T...) while((s32[]{:T(128)}, f32[136,512]{1,0:T(8,128)S(1)}, ...), condition=%wide.region_1.2_spmd.clone, body=%wide.region_0.1_spmd.clone.sunk | while | flops 1183811 | bytes 2835447 | solution.py:42
  30.1 25.8 %psum.7 = f32[136]{0:T(256)S(1)} all-reduce(f32[136]{0:T(256)S(1)} %get-tuple-element.512), channel_id=1, replica_groups=mesh['ctx'=32,'tp'=16] {'tp'}, use_global_device_ids=true, to_apply=%region_3.4 | all-reduce | flops 136 | bytes 1088 | tf_op jit(solution)/shard_map/psum | solution.py:83
  56.8 58.0 %all-gather.3.cloned.1.call-done = bf16[4352,512]{1,0:T(8,128)(2,1)} async-done(((bf16[136,512]{1,0:T(8,128)(2,1)}), bf16[4352,512]{1,0:T(8,128)(2,1)}) %all-gather.3.cloned.1.call-update) | async-done | bytes 4456464 | tf_op jit(solution)/shard_map/all_gather | solution.py:97
  114.8 6.4 %copy.20 = bf16[4352,512]{0,1:T(8,128)(2,1)} copy(bf16[4352,512]{1,0:T(8,128)(2,1)} %all-gather.3.cloned.1.call-done) | data formatting | bytes 8912896
  121.2 100.1 %all-gather.5.cloned.1.call-done = bf16[4352,512]{1,0:T(8,128)(2,1)} async-done(((bf16[136,512]{1,0:T(8,128)(2,1)}), bf16[4352,512]{1,0:T(8,128)(2,1)}) %all-gather.5.cloned.1.call-update) | async-done | bytes 4456464 | tf_op jit(solution)/shard_map/all_gather | solution.py:98
  221.4 6.6 %copy.22 = bf16[4352,512]{0,1:T(8,128)(2,1)} copy(bf16[4352,512]{1,0:T(8,128)(2,1)} %all-gather.5.cloned.1.call-done) | data formatting | bytes 8912896
  228.0 41.2 %while.35 = (s32[]{:T(128)}, f32[4,136]{1,0:T(4,128)S(1)}, f32[4,136]{1,0:T(4,128)S(1)}, f32[136,4,128]{2,0,1:T(8,128)S(1)}, s32[]{:T(128)}, /*index=5*/bf16[435...) while((s32[]{:T(128)}, f32[4,136]{1,0:T(4,128)S(1)}, ...), condition=%wide.region_9.10_spmd.clone, body=%wide.region_4.9_spmd.clone.sunk | while | flops 72732656 | bytes 4118965 | solution.py:140
  228.0 2.4 conditional.3
  230.4 2.4 conditional.3
  232.9 2.4 conditional.3
  235.3 2.4 conditional.3
  237.7 2.4 conditional.3
  240.1 2.4 conditional.3
  242.6 2.4 conditional.3
  245.0 2.4 conditional.3
  247.4 2.4 conditional.3
  249.8 2.4 conditional.3
  252.3 2.4 conditional.3
  254.7 2.4 conditional.3
  257.1 2.4 conditional.3
  259.5 2.4 conditional.3
  262.0 2.4 conditional.3
  264.4 2.4 conditional.3
  266.8 2.4 conditional.3
  (258 shorter events, 61.5 us)
Async XLA Ops:
  7.2 49.6 %copy-start = (bf16[136,512]{1,0:T(8,128)(2,1)S(1)}, bf16[136,512]{1,0:T(8,128)(2,1)}, u32[]{:S(2)}) copy-start(bf16[136,512]{1,0:T(8,128)(2,1)} %param.22) | copy-start | bytes 417796
  7.2 107.6 %all-gather.3.cloned.1.call-start = ((), (), s32[]{:S(2)}) async-start(), calls=%async_computation | async-start | bytes 4595712 | tf_op jit(solution)/shard_map/all_gather | solution.py:97
  7.9 213.5 %all-gather.5.cloned.1.call-start = ((), (), s32[]{:S(2)}) async-start(), calls=%async_computation.1 | async-start | bytes 4595712 | tf_op jit(solution)/shard_map/all_gather | solution.py:98
  8.7 4.2 %collective-permute-start.1 = (bf16[2,512]{1,0:T(2,128)(2,1)S(1)}, bf16[2,512]{1,0:T(2,128)(2,1)S(1)}, u32[]{:S(2)}, u32[]{:S(2)}) collective-permute-start(bf16[2,512]{1,0:T(2,128)(2,1)S(1)} %slice.86), channel_id=1, source_target_pairs={{0,16},{16,32},{32,48},{48,64},{64,80},{80,96},{96,112},{112,128},... | collective-permute-start | bytes 6152 | tf_op jit(solution)/shard_map/ppermute | solution.py:14
  10.7 3.8 %collective-permute-start.2 = (bf16[2,512]{1,0:T(2,128)(2,1)S(1)}, bf16[2,512]{1,0:T(2,128)(2,1)S(1)}, u32[]{:S(2)}, u32[]{:S(2)}) collective-permute-start(bf16[2,512]{1,0:T(2,128)(2,1)S(1)} %slice.92), channel_id=1, source_target_pairs={{0,16},{16,32},{32,48},{48,64},{64,80},{80,96},{96,112},{112,128},... | collective-permute-start | bytes 6152 | tf_op jit(solution)/shard_map/ppermute | solution.py:14
  16.0 5.1 %collective-permute-start.3 = (bf16[127,512]{1,0:T(8,128)(2,1)S(1)}, bf16[127,512]{1,0:T(8,128)(2,1)S(1)}, u32[]{:S(2)}, u32[]{:S(2)}) collective-permute-start(bf16[127,512]{1,0:T(8,128)(2,1)S(1)} %slice.103), channel_id=1, source_target_pairs={{0,16},{16,32},{32,48},{48,64},{64,80},{80,96},{96,112},{112,128},... | collective-permute-start | bytes 390152 | tf_op jit(solution)/shard_map/ppermute | solution.py:14
  18.0 11.9 %collective-permute-start = (bf16[2,512]{1,0:T(2,128)(2,1)S(1)}, bf16[2,512]{1,0:T(2,128)(2,1)S(1)}, u32[]{:S(2)}, u32[]{:S(2)}) collective-permute-start(bf16[2,512]{1,0:T(2,128)(2,1)S(1)} %slice.80), channel_id=1, source_target_pairs={{0,16},{16,32},{32,48},{48,64},{64,80},{80,96},{96,112},{112,128},... | collective-permute-start | bytes 6152 | tf_op jit(solution)/shard_map/ppermute | solution.py:14
  21.2 8.7 %copy-start.2 = (bf16[136,512]{1,0:T(8,128)(2,1)S(1)}, bf16[136,512]{1,0:T(8,128)(2,1)}, u32[]{:S(2)}) copy-start(bf16[136,512]{1,0:T(8,128)(2,1)} %param.17) | copy-start | bytes 417796
  21.2 8.7 %copy-start.3 = (bf16[136,512]{1,0:T(8,128)(2,1)S(1)}, bf16[136,512]{1,0:T(8,128)(2,1)}, u32[]{:S(2)}) copy-start(bf16[136,512]{1,0:T(8,128)(2,1)} %param.15) | copy-start | bytes 417796
  21.2 34.8 %copy-start.4 = (f32[512]{0:T(512)S(1)}, f32[512]{0:T(512)}, u32[]{:S(2)}) copy-start(f32[512]{0:T(512)} %param.21) | copy-start | bytes 6148
  30.1 91.1 %copy-start.1 = (bf16[136,512]{1,0:T(8,128)(2,1)}, bf16[136,512]{1,0:T(8,128)(2,1)S(1)}, u32[]{:S(2)}) copy-start(bf16[136,512]{1,0:T(8,128)(2,1)S(1)} %get-tuple-element.513) | copy-start | bytes 417796
Sparse Core Ops, SparseCore 0:
  11.4 103.3 all-gather.2
  118.8 102.5 all-gather.4
where the time goes:
time: 278 us; the launch traced here: 277 us
  waiting for transfers between devices  161 us (58%)
  local copies, waits for them, and re-layouts  35 us (13%)
  blocking collectives  25.8 us (9%)
  other arithmetic  18.4 us (7%)
  between operations  14.2 us (5%)
  matrix products  12.7 us (5%)
  starting transfers between devices  5.21 us (2%)
  loops' own time  4.14 us (1%)
    all_gather x1, waiting for transfers between devices, shards(): raw_piece = lax.all_gather(values, 'ctx', axis=0, tiled=True)  100 us
    all_gather x1, waiting for transfers between devices, shards(): key_piece = lax.all_gather(attn_keys, 'ctx', axis=0, tiled=True)  58 us
    psum x1, blocking collectives, shards(): row_totals = lax.psum(row_squares, 'tp')  25.8 us
    dynamic_slice x17, local copies, waits for them, and re-layouts, block_step(): raw_block = lax.dynamic_slice_in_dim(raw_piece, offset, block, 0)  18.3 us
    unnamed x13, local copies, waits for them, and re-layouts  13 us
    dot_general x17, matrix products, update(): jnp.einsum('shd,phd->hsp', query_heads, key_block.reshape(block, heads, H...  6.99 us
    reduce_sum x17, other arithmetic, update(): new_sum = running_sum * factor + jnp.sum(expo, axis=2)  6.31 us
    dot_general x17, matrix products, update(): jnp.einsum('hsp,phd->shd', weights, raw_block.reshape(block, heads, HD),...  5.74 us
  transfers between devices with their start and end apart: 6, of which 4 were waited for; matrix products, arithmetic and copies ran while one was open for 7% of the time, Pallas kernels for 0%

commit v1 on v0

v1 whole, which is shorter than its diff:
```python
import functools
import math

import jax
import jax.numpy as jnp
from jax import lax
from jax.experimental import pallas as pl
from jax.experimental.pallas import tpu as pltpu
from jax.sharding import Mesh, PartitionSpec as P

HD = 128
ROWS_AXES = ("zh", "s", "h", "c")
CHAN_AXES = ("x", "zl")
PEERS = ("zh", "s", "h")
HIGHEST = lax.Precision.HIGHEST


def front_kernel(gf, gs, hv, res, halo, taps, long_taps, stream, packed, squares, ext, prod, copies):
    rows = gf.shape[0]
    lanes = gf.shape[1]

    def extended(own, prev):
        ext[0:rows, :] = prev.astype(jnp.float32)
        ext[rows : 2 * rows, :] = own.astype(jnp.float32)

    def featurize(index, begin, count):
        total = taps[index, 0:1, :] * ext[begin : begin + count, :]
        total = total + taps[index, 1:2, :] * ext[begin - 1 : begin - 1 + count, :]
        return total + taps[index, 2:3, :] * ext[begin - 2 : begin - 2 + count, :]

    span = 2 * rows - 8
    extended(gf[...], halo[0:rows, :])
    prod[8:, :] = featurize(0, 8, span)
    extended(hv[...], halo[rows : 2 * rows, :])
    value = (prod[8:, :] * featurize(2, 8, span)).astype(jnp.bfloat16)
    prod[0:8, :] = jnp.zeros((8, lanes), jnp.float32)
    prod[8:, :] = value.astype(jnp.float32)
    for lag in range(8):
        copies[lag, 8:, :] = prod[8 - lag : 2 * rows - lag, :]

    tiles = rows // 8

    def lag_group(group, totals):
        weights = long_taps[pl.ds(pl.multiple_of(group * 8, 8), 8), :].astype(jnp.float32)
        base = rows - group * 8
        totals = list(totals)
        for lag in range(8):
            weight = jnp.broadcast_to(weights[lag : lag + 1, :], (8, lanes))
            for tile in range(tiles):
                window = copies[lag, pl.ds(pl.multiple_of(base + tile * 8, 8), 8), :]
                totals[tile] = totals[tile] + weight * window
        return tuple(totals)

    zero = jnp.zeros((8, lanes), jnp.float32)
    totals = lax.fori_loop(0, long_taps.shape[0] // 8, lag_group, (zero,) * tiles)
    filtered = jnp.concatenate(totals, axis=0)

    ext[rows - 8 : rows, :] = halo[2 * rows : 2 * rows + 8, :].astype(jnp.float32)
    ext[rows : 2 * rows, :] = gs[...].astype(jnp.float32)
    out = (res[...].astype(jnp.float32) + featurize(1, rows, rows) * filtered).astype(jnp.bfloat16)
    stream[...] = out
    for copy in range(packed.shape[0]):
        packed[copy, 0] = out
    wide = out.astype(jnp.float32)
    part = lax.dot_general(
        jnp.ones((squares.shape[0], lanes), jnp.float32),
        wide * wide,
        (((1,), (1,)), ((), ())),
        precision=HIGHEST,
        preferred_element_type=jnp.float32,
    )

    @pl.when(pl.program_id(0) == 0)
    def _():
        squares[...] = part

    @pl.when(pl.program_id(0) > 0)
    def _():
        squares[...] = squares[...] + part


def front(gf, gs, hv, res, halo, taps, long_taps):
    rows, chans = gf.shape
    heads = chans // HD
    column = lambda n: pl.BlockSpec((n, HD), lambda i: (0, i))
    return pl.pallas_call(
        front_kernel,
        grid=(heads,),
        in_specs=[
            column(rows),
            column(rows),
            column(rows),
            column(rows),
            column(halo.shape[0]),
            pl.BlockSpec((3, 3, HD), lambda i: (0, 0, i)),
            column(long_taps.shape[0]),
        ],
        out_specs=[
            column(rows),
            pl.BlockSpec((4, 1, rows, HD), lambda i: (0, i, 0, 0)),
            pl.BlockSpec((16, rows), lambda i: (0, 0)),
        ],
        out_shape=[
            jax.ShapeDtypeStruct((rows, chans), jnp.bfloat16),
            jax.ShapeDtypeStruct((4, heads, rows, HD), jnp.bfloat16),
            jax.ShapeDtypeStruct((16, rows), jnp.float32),
        ],
        scratch_shapes=[
            pltpu.VMEM((2 * rows, HD), jnp.float32),
            pltpu.VMEM((2 * rows, HD), jnp.float32),
            pltpu.VMEM((8, 2 * rows, HD), jnp.float32),
        ],
        compiler_params=pltpu.CompilerParams(vmem_limit_bytes=32 << 20),
        cost_estimate=pl.CostEstimate(flops=40_000_000, bytes_accessed=2_000_000, transcendentals=0),
        name="front",
    )(gf, gs, hv, res, halo, taps, long_taps)


def score_kernel(place, q, k_own, k_other, weights, denom, scores):
    rows = q.shape[1]
    keys = k_own.shape[0]
    unit = math.log2(math.e) / math.sqrt(HD)
    chunks = [(begin, min(256, keys - begin)) for begin in range(0, keys, 256)]

    def query_block(index, carry):
        query = q[index]
        query_pos = place[0] + index * 2 * rows + lax.broadcasted_iota(jnp.int32, (rows, 1), 0)
        top = None
        for half, ref in enumerate((k_own, k_other)):
            for begin, width in chunks:
                score = lax.dot_general(
                    query,
                    ref[begin : begin + width, :],
                    (((1,), (1,)), ((), ())),
                    preferred_element_type=jnp.float32,
                )
                lane = begin + lax.broadcasted_iota(jnp.int32, (1, width), 1)
                key_pos = place[1 + half] + lane
                for edge in range(rows, keys, rows):
                    if edge < begin + width:
                        key_pos = key_pos + jnp.where(lane >= edge, rows, 0)
                score = jnp.where(key_pos <= query_pos, score * unit, -1e30)
                scores[:, half * keys + begin : half * keys + begin + width] = score
                for part in range(0, width, 128):
                    piece = score[:, part : part + 128]
                    top = piece if top is None else jnp.maximum(top, piece)
        top = jnp.max(top, axis=1, keepdims=True)
        total = jnp.zeros((rows, 128), jnp.float32)
        for begin in range(0, 2 * keys, 128):
            expo = jnp.exp2(scores[:, begin : begin + 128] - top)
            total = total + expo
            weights[index, :, begin : begin + 128] = expo.astype(jnp.bfloat16)
        total = jnp.sum(total, axis=1, keepdims=True)
        denom[index] = jnp.broadcast_to(total, (rows, 128))
        return carry

    lax.fori_loop(0, q.shape[0], query_block, 0)


def score(place, q, k_own, k_other):
    blocks, rows, _ = q.shape
    keys = k_own.shape[0]
    vmem = pl.BlockSpec(memory_space=pltpu.VMEM)
    return pl.pallas_call(
        score_kernel,
        in_specs=[pl.BlockSpec(memory_space=pltpu.SMEM), vmem, vmem, vmem],
        out_specs=[vmem, vmem],
        out_shape=[
            jax.ShapeDtypeStruct((blocks, rows, 2 * keys), jnp.bfloat16),
            jax.ShapeDtypeStruct((blocks, rows, 128), jnp.float32),
        ],
        scratch_shapes=[pltpu.VMEM((rows, 2 * keys), jnp.float32)],
        compiler_params=pltpu.CompilerParams(vmem_limit_bytes=32 << 20),
        cost_estimate=pl.CostEstimate(
            flops=2 * blocks * rows * 2 * keys * HD,
            bytes_accessed=8_000_000,
            transcendentals=blocks * rows * 2 * keys,
        ),
        name="score",
    )(place, q, k_own, k_other)


def attend_kernel(weights, denom, v_own, v_other, inv_own, inv_other, gain, out, values):
    blocks, rows, _ = out.shape
    keys = v_own.shape[0] * rows
    for half, (v, inv) in enumerate(((v_own, inv_own), (v_other, inv_other))):
        for block in range(v.shape[0]):
            scaled = v[block].astype(jnp.float32) * inv[:, block : block + 1] * gain[...]
            begin = half * keys + block * rows
            values[begin : begin + rows, :] = scaled.astype(jnp.bfloat16)

    def query_block(index, carry):
        total = jnp.dot(weights[index], values[...], preferred_element_type=jnp.float32)
        out[index] = (total / denom[index]).astype(jnp.bfloat16)
        return carry

    lax.fori_loop(0, blocks, query_block, 0)


def attend(weights, denom, v_own, v_other, inv_own, inv_other, gain):
    blocks, rows, keys = weights.shape
    vmem = pl.BlockSpec(memory_space=pltpu.VMEM)
    return pl.pallas_call(
        attend_kernel,
        in_specs=[vmem] * 7,
        out_specs=vmem,
        out_shape=jax.ShapeDtypeStruct((blocks, rows, HD), jnp.bfloat16),
        scratch_shapes=[pltpu.VMEM((keys, HD), jnp.bfloat16)],
        compiler_params=pltpu.CompilerParams(vmem_limit_bytes=32 << 20),
        cost_estimate=pl.CostEstimate(
            flops=2 * blocks * rows * keys * HD, bytes_accessed=7_000_000, transcendentals=0
        ),
        name="attend",
    )(weights, denom, v_own, v_other, inv_own, inv_other, gain)


def exchange(value, axes):
    return lax.all_to_all(value, axes, 0, 0, tiled=True)


def swap_cores(value):
    return lax.ppermute(value, "c", [(0, 1), (1, 0)])


def shards(residual, gate_first, gate_second, hyena_value, short_taps, long_taps, norm_gain, queries, attn_keys):
    rows, chans = residual.shape
    heads = chans // HD
    count = 32
    width = chans * 16

    halo = lax.ppermute(
        jnp.concatenate([gate_first, hyena_value, gate_second[rows - 8 :]], axis=0),
        ROWS_AXES,
        [(source, source + 1) for source in range(count - 1)],
    )
    keys_by_head = attn_keys.reshape(rows, heads, HD).transpose(1, 0, 2)
    keys_own = exchange(jnp.concatenate([keys_by_head] * 4, axis=0), PEERS)
    queries_own = exchange(queries.reshape(rows, heads, HD).transpose(1, 0, 2), "h")

    stream, packed, squares = front(gate_first, gate_second, hyena_value, residual, halo, short_taps, long_taps)
    values_own = exchange(packed.reshape(16, rows, HD), PEERS)
    totals = jnp.sum(exchange(squares, CHAN_AXES), axis=0)
    inverse = 1.0 / jnp.sqrt(totals / width + 1e-06)
    inverse_own = exchange(jnp.broadcast_to(inverse, (16, rows)), PEERS)

    keys_other = swap_cores(keys_own)
    values_other = swap_cores(values_own)
    inverse_other = swap_cores(inverse_own)

    core = lax.axis_index("c")
    block = lax.axis_index("zh") * 16 + lax.axis_index("s") * 8 + core
    place = jnp.stack([block * rows, core * rows, (1 - core) * rows]).astype(jnp.int32)
    weights, denom = score(
        place, queries_own, keys_own.reshape(16 * rows, HD), keys_other.reshape(16 * rows, HD)
    )
    gain = lax.dynamic_slice_in_dim(norm_gain, lax.axis_index("h") * HD, HD, 0).reshape(1, HD)
    result = attend(weights, denom, values_own, values_other, inverse_own.T, inverse_other.T, gain)
    attended = exchange(result, "h").transpose(1, 0, 2).reshape(rows, chans)
    return stream, attended


def solution(mesh):
    inner = Mesh(mesh.devices.reshape(2, 2, 4, 2, 4, 4), ROWS_AXES + CHAN_AXES)
    both = P(ROWS_AXES, CHAN_AXES)
    return jax.shard_map(
        shards,
        mesh=inner,
        in_specs=(both, both, both, both, P(None, None, CHAN_AXES), P(None, CHAN_AXES), P(CHAN_AXES), both, both),
        out_specs=(both, both),
        check_vma=False,
    )
```

time: 278 us -> 139 us (0.50)
  the two profiles are of different devices: /device:TPU:443 before, /device:TPU:1 now
where the time goes in v1:
time: 139 us; the launch traced here: 138 us
  starting transfers between devices  45.8 us (33%)
  blocking collectives  38.8 us (28%)
  waiting for transfers between devices  28.5 us (21%)
  Pallas kernels  13.8 us (10%)
  local copies, waits for them, and re-layouts  9.5 us (7%)
    all_to_all x2, blocking collectives, exchange(): return lax.all_to_all(value, axes, 0, 0, tiled=True)  38.8 us
    all_to_all x4, waiting for transfers between devices, exchange(): return lax.all_to_all(value, axes, 0, 0, tiled=True)  23.9 us
    ppermute x3, starting transfers between devices, swap_cores(): return lax.ppermute(value, 'c', [(0, 1), (1, 0)])  21.5 us
    all_to_all x4, starting transfers between devices, exchange(): return lax.all_to_all(value, axes, 0, 0, tiled=True)  19.7 us
    pallas_call x1, Pallas kernels, front(): pl.pallas_call(front_kernel, grid=(heads,), in_specs=[column(rows), colum...  5.92 us
    unnamed x16, local copies, waits for them, and re-layouts  5.28 us
    pallas_call x1, Pallas kernels, score(): pl.pallas_call(score_kernel, in_specs=[pl.BlockSpec(memory_space=pltpu.SM...  5.14 us
    ppermute x1, starting transfers between devices, shards(): lax.ppermute(jnp.concatenate([gate_first, hyena_value, gate_second[rows -...  4.59 us
  transfers between devices with their start and end apart: 8, of which 5 were waited for; matrix products, arithmetic and copies ran while one was open for 2% of the time, Pallas kernels for 4%

profile of v1, /device:TPU:1, one launch (start us, length us, event | category | flops | bytes accessed | tf_op | source)
XLA Modules:
  0.0 138.3 jit_solution(359203752277618058)
XLA Ops:
  1.4 1.0 pad_maximum_fusion.1
  2.4 4.6 %collective-permute-start = (bf16[280,512]{1,0:T(8,128)(2,1)S(1)}, bf16[280,512]{1,0:T(8,128)(2,1)S(1)}, u32[]{:S(2)}, u32[]{:S(2)}) collective-permute-start(bf16[280,512]{1,0:T(8,128)(2,1)S(1)} %pad_maximum_fusion.1), channel_id=1, source_target_pairs={{0,16},{16,32},{32,48},{48,64},{64,80},{80,96},{96,112},{112,128},... | collective-permute-start | bytes 860168 | tf_op jit(solution)/shard_map/ppermute | solution.py:231
  7.0 4.6 %collective-permute-done.halo = bf16[280,512]{1,0:T(8,128)(2,1)S(1)} collective-permute-done((bf16[280,512]{1,0:T(8,128)(2,1)S(1)}, bf16[280,512]{1,0:T(8,128)(2,1)S(1)}, u32[]{:S(2)}, u32[]{:S(2)}) %collective-permute-start) | collective-permute-done | bytes 286752 | tf_op jit(solution)/shard_map/ppermute | solution.py:231
  11.6 0.9 copy-done.1
  12.5 0.9 copy-done.2
  13.4 0.9 copy-done.3
  14.3 0.9 copy-done.4
  15.2 0.9 copy-done.5
  16.9 5.9 %front.1 = (bf16[136,512]{1,0:T(8,128)(2,1)}, bf16[4,4,136,128]{3,2,1,0:T(8,128)(2,1)}, f32[16,136]{1,0:T(8,128)S(1)}) custom-call(bf16[136,512]{1,0:T(8,128)(2,1)S(1)} %copy-done.1, bf16[136,512]{1,0:T(8,128)(2,1)S(1)} %copy-done.3, bf16[136,512]{1,0:T(8,128)(2,1)S(1)} %copy-done.2, bf16[136,512]{1,0:T(8,128)(2,1)S(1)} %copy-done.4, ...), custom_call_target="tpu_custom_call" | custom-call | flops 40000000 | bytes 2000000 | tf_op jit(solution)/shard_map/front/pallas_call | solution.py:86
  23.4 8.5 %all-to-all-start.3 = ((f32[16,1,136]{2,1,0:T(1,128)}), f32[16,1,136]{2,1,0:T(1,128)S(1)}, u32[]{:S(2)}, u32[]{:S(2)}) async-start(f32[16,1,136]{2,1,0:T(1,128)} %copy.17), calls=%async_computation.3 | async-start | bytes 32768 | tf_op jit(solution)/shard_map/all_to_all | solution.py:218
  32.0 6.7 %all-to-all-done.3 = f32[16,1,136]{2,1,0:T(1,128)S(1)} async-done(((f32[16,1,136]{2,1,0:T(1,128)}), f32[16,1,136]{2,1,0:T(1,128)S(1)}, u32[]{:S(2)}, u32[]{:S(2)}) %all-to-all-start.3) | async-done | bytes 8736 | tf_op jit(solution)/shard_map/all_to_all | solution.py:218
  38.7 29.1 %all_to_all.38 = bf16[16,136,128]{2,1,0:T(8,128)(2,1)S(1)} all-to-all(bf16[16,136,128]{2,1,0:T(8,128)(2,1)S(1)} %pad_maximum_fusion), channel_id=1, replica_groups=mesh['zh'=2,'s'=2,'h'=4,'c'=2,'x'=4,'zl'=4] {'zh','s','h'}, dimensions={0} | all-to-all | bytes 1114112 | tf_op jit(solution)/shard_map/all_to_all | solution.py:218
  67.9 3.6 %all-to-all-start.2 = ((bf16[16,136,128]{2,1,0:T(8,128)(2,1)}), bf16[16,136,128]{2,1,0:T(8,128)(2,1)S(1)}, u32[]{:S(2)}, u32[]{:S(2)}) async-start(bf16[16,136,128]{2,1,0:T(8,128)(2,1)} %bitcast.7), calls=%async_computation.2 | async-start | bytes 1114112 | tf_op jit(solution)/shard_map/all_to_all | solution.py:218
  71.5 8.6 %collective-permute-start.1 = (bf16[16,136,128]{2,1,0:T(8,128)(2,1)S(1)}, bf16[16,136,128]{2,1,0:T(8,128)(2,1)S(1)}, u32[]{:S(2)}, u32[]{:S(2)}) collective-permute-start(bf16[16,136,128]{2,1,0:T(8,128)(2,1)S(1)} %all_to_all.38), channel_id=1, source_target_pairs={{0,16},{16,0},{1,17},{17,1},{2,18},{18,2},{3,19},{19,3},{4,20},{20... | collective-permute-start | bytes 1671176 | tf_op jit(solution)/shard_map/ppermute | solution.py:222
  80.1 6.1 %all-to-all-done.2.v_own = bf16[16,136,128]{2,1,0:T(8,128)(2,1)S(1)} async-done(((bf16[16,136,128]{2,1,0:T(8,128)(2,1)}), bf16[16,136,128]{2,1,0:T(8,128)(2,1)S(1)}, u32[]{:S(2)}, u32[]{:S(2)}) %all-to-all-start.2) | async-done | bytes 557088 | tf_op jit(solution)/shard_map/all_to_all | solution.py:218
  86.2 9.5 %collective-permute-start.2 = (bf16[16,136,128]{2,1,0:T(8,128)(2,1)S(1)}, bf16[16,136,128]{2,1,0:T(8,128)(2,1)S(1)}, u32[]{:S(2)}, u32[]{:S(2)}) collective-permute-start(bf16[16,136,128]{2,1,0:T(8,128)(2,1)S(1)} %all-to-all-done.2.v_own), channel_id=1, source_target_pairs={{0,16},{16,0},{1,17},{17,1},{2,18},{18,2},{3,19},{19,3},{4,20},{20... | collective-permute-start | bytes 1671176 | tf_op jit(solution)/shard_map/ppermute | solution.py:222
  96.3 4.3 %all-to-all-start.4 = ((f32[16,1,136]{2,1,0:T(1,128)}), f32[16,1,136]{2,1,0:T(1,128)S(1)}, u32[]{:S(2)}, u32[]{:S(2)}) async-start(f32[16,1,136]{2,1,0:T(1,128)} %broadcast_in_dim.3), calls=%async_computation.4 | async-start | bytes 32768 | tf_op jit(solution)/shard_map/all_to_all | solution.py:218
  101.4 10.5 %all-to-all-done.4 = f32[16,1,136]{2,1,0:T(1,128)S(1)} async-done(((f32[16,1,136]{2,1,0:T(1,128)}), f32[16,1,136]{2,1,0:T(1,128)S(1)}, u32[]{:S(2)}, u32[]{:S(2)}) %all-to-all-start.4) | async-done | bytes 8736 | tf_op jit(solution)/shard_map/all_to_all | solution.py:218
  111.9 3.3 %all-to-all-start = ((bf16[4,136,128]{2,1,0:T(8,128)(2,1)}), bf16[4,136,128]{2,1,0:T(8,128)(2,1)S(1)}, u32[]{:S(2)}, u32[]{:S(2)}) async-start(bf16[4,136,128]{2,1,0:T(8,128)(2,1)} %bitcast_bitcast_fusion.1), calls=%async_computation | async-start | bytes 278528 | tf_op jit(solution)/shard_map/all_to_all | solution.py:218
  115.3 0.8 dynamic-slice_bitcast_fusion.gain
  116.2 3.3 %collective-permute-start.3 = (f32[16,136]{0,1:T(8,128)S(1)}, f32[16,136]{0,1:T(8,128)S(1)}, u32[]{:S(2)}, u32[]{:S(2)}) collective-permute-start(f32[16,136]{0,1:T(8,128)S(1)} %bitcast.34), channel_id=1, source_target_pairs={{0,16},{16,0},{1,17},{17,1},{2,18},{18,2},{3,19},{19,3},{4,20},{20... | collective-permute-start | bytes 26120 | tf_op jit(solution)/shard_map/ppermute | solution.py:222
  120.1 5.1 %score.1 = (bf16[4,136,4352]{2,1,0:T(8,128)(2,1)S(1)}, f32[4,136,128]{2,1,0:T(8,128)S(1)}) custom-call(s32[3]{0:T(128)S(1)} %pad_add_fusion.place, bf16[4,136,128]{2,1,0:T(8,128)(2,1)S(1)} %all-to-all-done.q, bf16[2176,128]{1,0:T(8,128)(2,1)S(1)} %bitcast.33, bf16[2176,128]{1,0:T(8,128)(2,1)S(1)} %bitcast.38), custom_call_target="tpu_custom_call" | custom-call | flops 606076928 | bytes 8000000 | tf_op jit(solution)/shard_map/score/pallas_call | solution.py:164
  125.2 2.7 %attend.1 = bf16[4,136,128]{2,1,0:T(8,128)(2,1)S(1)} custom-call(bf16[4,136,4352]{2,1,0:T(8,128)(2,1)S(1)} %get-tuple-element.8.weights, f32[4,136,128]{2,1,0:T(8,128)S(1)} %get-tuple-element.9.denom, bf16[16,136,128]{2,1,0:T(8,128)(2,1)S(1)} %all-to-all-done.2.v_own, bf16[16,136,128]{2,1,0:T(8,128)(2,1)S(1)} %collective-permute-done.2.v_other, ...), custom_call_target="tpu_custom_call" | custom-call | flops 606076928 | bytes 7000000 | tf_op jit(solution)/shard_map/attend/pallas_call | solution.py:203
  127.9 9.7 %all_to_all.39 = bf16[4,136,128]{2,1,0:T(8,128)(2,1)S(1)} all-to-all(bf16[4,136,128]{2,1,0:T(8,128)(2,1)S(1)} %attend.1), channel_id=1, replica_groups=mesh['zh'=2,'s'=2,'h'=4,'c'=2,'x'=4,'zl'=4] {'h'}, dimensions={0} | all-to-all | bytes 278528 | tf_op jit(solution)/shard_map/all_to_all | solution.py:218
  (26 shorter events, 4.9 us)
Async XLA Ops:
  0.6 6.4 %copy-start = (bf16[136,512]{1,0:T(8,128)(2,1)S(1)}, bf16[136,512]{1,0:T(8,128)(2,1)}, u32[]{:S(2)}) copy-start(bf16[136,512]{1,0:T(8,128)(2,1)} %param.17) | copy-start | bytes 417796
  0.6 100.0 %copy-start.7 = (bf16[136,512]{1,0:T(8,128)(2,1)S(1)}, bf16[136,512]{1,0:T(8,128)(2,1)}, u32[]{:S(2)}) copy-start(bf16[136,512]{1,0:T(8,128)(2,1)} %param.16) | copy-start | bytes 417796
  2.4 9.2 %collective-permute-start = (bf16[280,512]{1,0:T(8,128)(2,1)S(1)}, bf16[280,512]{1,0:T(8,128)(2,1)S(1)}, u32[]{:S(2)}, u32[]{:S(2)}) collective-permute-start(bf16[280,512]{1,0:T(8,128)(2,1)S(1)} %pad_maximum_fusion.1), channel_id=1, source_target_pairs={{0,16},{16,32},{32,48},{48,64},{64,80},{80,96},{96,112},{112,128},... | collective-permute-start | bytes 860168 | tf_op jit(solution)/shard_map/ppermute | solution.py:231
  11.6 0.9 copy-start.1
  12.5 0.9 copy-start.2
  13.4 0.9 copy-start.3
  14.3 0.9 copy-start.4
  15.2 0.9 copy-start.5
  16.1 0.7 copy-start.6
  23.4 15.3 %all-to-all-start.3 = ((f32[16,1,136]{2,1,0:T(1,128)}), f32[16,1,136]{2,1,0:T(1,128)S(1)}, u32[]{:S(2)}, u32[]{:S(2)}) async-start(f32[16,1,136]{2,1,0:T(1,128)} %copy.17), calls=%async_computation.3 | async-start | bytes 32768 | tf_op jit(solution)/shard_map/all_to_all | solution.py:218
  67.9 18.4 %all-to-all-start.2 = ((bf16[16,136,128]{2,1,0:T(8,128)(2,1)}), bf16[16,136,128]{2,1,0:T(8,128)(2,1)S(1)}, u32[]{:S(2)}, u32[]{:S(2)}) async-start(bf16[16,136,128]{2,1,0:T(8,128)(2,1)} %bitcast.7), calls=%async_computation.2 | async-start | bytes 1114112 | tf_op jit(solution)/shard_map/all_to_all | solution.py:218
  71.5 48.6 %collective-permute-start.1 = (bf16[16,136,128]{2,1,0:T(8,128)(2,1)S(1)}, bf16[16,136,128]{2,1,0:T(8,128)(2,1)S(1)}, u32[]{:S(2)}, u32[]{:S(2)}) collective-permute-start(bf16[16,136,128]{2,1,0:T(8,128)(2,1)S(1)} %all_to_all.38), channel_id=1, source_target_pairs={{0,16},{16,0},{1,17},{17,1},{2,18},{18,2},{3,19},{19,3},{4,20},{20... | collective-permute-start | bytes 1671176 | tf_op jit(solution)/shard_map/ppermute | solution.py:222
  86.2 39.0 %collective-permute-start.2 = (bf16[16,136,128]{2,1,0:T(8,128)(2,1)S(1)}, bf16[16,136,128]{2,1,0:T(8,128)(2,1)S(1)}, u32[]{:S(2)}, u32[]{:S(2)}) collective-permute-start(bf16[16,136,128]{2,1,0:T(8,128)(2,1)S(1)} %all-to-all-done.2.v_own), channel_id=1, source_target_pairs={{0,16},{16,0},{1,17},{17,1},{2,18},{18,2},{3,19},{19,3},{4,20},{20... | collective-permute-start | bytes 1671176 | tf_op jit(solution)/shard_map/ppermute | solution.py:222
  96.3 15.6 %all-to-all-start.4 = ((f32[16,1,136]{2,1,0:T(1,128)}), f32[16,1,136]{2,1,0:T(1,128)S(1)}, u32[]{:S(2)}, u32[]{:S(2)}) async-start(f32[16,1,136]{2,1,0:T(1,128)} %broadcast_in_dim.3), calls=%async_computation.4 | async-start | bytes 32768 | tf_op jit(solution)/shard_map/all_to_all | solution.py:218
  111.9 8.1 %all-to-all-start = ((bf16[4,136,128]{2,1,0:T(8,128)(2,1)}), bf16[4,136,128]{2,1,0:T(8,128)(2,1)S(1)}, u32[]{:S(2)}, u32[]{:S(2)}) async-start(bf16[4,136,128]{2,1,0:T(8,128)(2,1)} %bitcast_bitcast_fusion.1), calls=%async_computation | async-start | bytes 278528 | tf_op jit(solution)/shard_map/all_to_all | solution.py:218
  116.2 9.0 %collective-permute-start.3 = (f32[16,136]{0,1:T(8,128)S(1)}, f32[16,136]{0,1:T(8,128)S(1)}, u32[]{:S(2)}, u32[]{:S(2)}) collective-permute-start(f32[16,136]{0,1:T(8,128)S(1)} %bitcast.34), channel_id=1, source_target_pairs={{0,16},{16,0},{1,17},{17,1},{2,18},{18,2},{3,19},{19,3},{4,20},{20... | collective-permute-start | bytes 26120 | tf_op jit(solution)/shard_map/ppermute | solution.py:222

commit v2 on v1

v2 whole, which is shorter than its diff:
```python
import functools
import math

import jax
import jax.numpy as jnp
from jax import lax
from jax.experimental import pallas as pl
from jax.experimental.pallas import tpu as pltpu
from jax.sharding import Mesh, PartitionSpec as P

HD = 128
ROWS_AXES = ("zh", "s", "h", "c")
CHAN_AXES = ("x", "zl")
PEERS = ("zh", "s", "h")
HIGHEST = lax.Precision.HIGHEST


def shift_copies(prod, copies):
    length = prod.shape[0]
    for lag in range(8):
        copies[lag, 8:length, :] = prod[8 - lag : length - lag, :]


def lag_sums(weights, copies, base, pairs):
    totals = {}
    for group in range(weights.shape[0] // 8):
        wanted = [tile for tile, other in pairs if other == group]
        rows = weights[group * 8 : group * 8 + 8, :].astype(jnp.float32)
        for lag in range(8):
            weight = jnp.broadcast_to(rows[lag : lag + 1, :], rows.shape)
            for tile in wanted:
                begin = base + 8 * (tile - group)
                term = weight * copies[lag, begin : begin + 8, :]
                totals[tile] = totals[tile] + term if tile in totals else term
    return [totals[tile] for tile in sorted(totals)]


def featurize(taps, index, ext, begin, count):
    total = taps[index, 0:1, :] * ext[begin : begin + count, :]
    total = total + taps[index, 1:2, :] * ext[begin - 1 : begin - 1 + count, :]
    return total + taps[index, 2:3, :] * ext[begin - 2 : begin - 2 + count, :]


def head_lanes(head):
    return pl.ds(pl.multiple_of(head * HD, HD), HD)


def early_kernel(
    packed, gs, res, taps_in, long_in, keys, partial, feat, res_out, edge, taps_out, long_out, keys_out,
    gs_v, ext, prod, copies, sems,
):
    rows, chans = gs.shape
    loads = [(taps_in, taps_out), (long_in, long_out), (gs, gs_v), (res, res_out)]
    moves = [pltpu.make_async_copy(src, dst, sems.at[i]) for i, (src, dst) in enumerate(loads)]
    for copy in range(keys_out.shape[0]):
        for head in range(keys_out.shape[1]):
            src = keys.at[:, head * HD : (head + 1) * HD]
            moves.append(pltpu.make_async_copy(src, keys_out.at[copy, head], sems.at[len(moves)]))
    for move in moves:
        move.start()
    for move in moves[:4]:
        move.wait()
    tiles = rows // 8
    pairs = [(tile, group) for group in range(long_in.shape[0] // 8) for tile in range(group, tiles)]
    top = lax.broadcasted_iota(jnp.int32, (rows, HD), 0) < 2
    ext[0:8, :] = jnp.zeros((8, HD), jnp.float32)
    prod[0:8, :] = jnp.zeros((8, HD), jnp.float32)

    def one_head(head, carry):
        lanes = head_lanes(head)
        taps = taps_out[:, :, lanes]

        def feature(index, raw):
            wide = raw.astype(jnp.float32)
            ext[8:, :] = wide
            edge[index, :, lanes] = wide[0:8, :]
            return featurize(taps, index, ext, 8, rows)

        first = feature(0, packed[0:rows, lanes])
        product = (first * feature(2, packed[rows : 2 * rows, lanes])).astype(jnp.bfloat16).astype(jnp.float32)
        feat[:, lanes] = feature(1, gs_v[:, lanes])
        prod[8:, :] = jnp.where(top, 0.0, product)
        shift_copies(prod, copies)
        totals = lag_sums(long_out[:, lanes], copies, 8, pairs)
        partial[:, lanes] = jnp.concatenate(totals, axis=0)
        return carry

    lax.fori_loop(0, chans // HD, one_head, 0)
    for move in moves[4:]:
        move.wait()


def in_hbm(*arrays):
    return [pltpu.with_memory_space_constraint(array, pltpu.HBM) for array in arrays]


def early(packed, gs, res, taps, long_taps, keys):
    rows, chans = gs.shape
    heads = chans // HD
    hbm = pl.BlockSpec(memory_space=pltpu.HBM)
    vmem = pl.BlockSpec(memory_space=pltpu.VMEM)
    return pl.pallas_call(
        early_kernel,
        in_specs=[vmem] + [hbm] * 5,
        out_specs=[vmem] * 7,
        out_shape=[
            jax.ShapeDtypeStruct((rows, chans), jnp.float32),
            jax.ShapeDtypeStruct((rows, chans), jnp.float32),
            jax.ShapeDtypeStruct((rows, chans), jnp.bfloat16),
            jax.ShapeDtypeStruct((3, 8, chans), jnp.float32),
            jax.ShapeDtypeStruct(taps.shape, jnp.float32),
            jax.ShapeDtypeStruct(long_taps.shape, jnp.bfloat16),
            jax.ShapeDtypeStruct((2, heads, rows, HD), jnp.bfloat16),
        ],
        scratch_shapes=[
            pltpu.VMEM((rows, chans), jnp.bfloat16),
            pltpu.VMEM((rows + 8, HD), jnp.float32),
            pltpu.VMEM((rows + 8, HD), jnp.float32),
            pltpu.VMEM((8, rows + 8, HD), jnp.float32),
            pltpu.SemaphoreType.DMA((4 + 2 * heads,)),
        ],
        compiler_params=pltpu.CompilerParams(vmem_limit_bytes=32 << 20),
        cost_estimate=pl.CostEstimate(flops=6_000_000_000, bytes_accessed=2_000_000, transcendentals=0),
        name="early",
    )(packed, *in_hbm(gs, res, taps, long_taps, keys))


def late_kernel(halo, partial, feat, res, edge, taps_in, long_in, stream, squares, ext, prod, copies):
    rows, chans = res.shape
    tiles = rows // 8
    pairs = [(tile, group) for group in range(long_in.shape[0] // 8) for tile in range(min(group + 2, tiles))]
    inside = lax.broadcasted_iota(jnp.int32, (rows, HD), 0) < rows - 6
    first_row = (lax.broadcasted_iota(jnp.int32, (8, HD), 0) == 0).astype(jnp.float32)
    prod[0:8, :] = jnp.zeros((8, HD), jnp.float32)
    prod[rows + 8 :, :] = jnp.zeros((8, HD), jnp.float32)
    squares[...] = jnp.zeros_like(squares)

    def one_head(head, carry):
        lanes = head_lanes(head)
        taps = taps_in[:, :, lanes]

        def feature(index, begin):
            ext[0:rows, :] = halo[begin : begin + rows, lanes].astype(jnp.float32)
            ext[rows : rows + 8, :] = edge[index, :, lanes]
            return featurize(taps, index, ext, 8, rows)

        first = feature(0, 0)
        product = (first * feature(2, rows)).astype(jnp.bfloat16).astype(jnp.float32)
        prod[8 : rows + 8, :] = jnp.where(inside, product, 0.0)
        shift_copies(prod, copies)
        totals = lag_sums(long_in[:, lanes], copies, rows, pairs)
        filtered = partial[:, lanes] + jnp.concatenate(totals, axis=0)
        ext[0:8, :] = halo[2 * rows : 2 * rows + 8, lanes].astype(jnp.float32)
        ext[8:16, :] = edge[1, :, lanes]
        gate = jnp.concatenate([featurize(taps, 1, ext, 8, 8), feat[8:, lanes]], axis=0)
        out = (res[:, lanes].astype(jnp.float32) + gate * filtered).astype(jnp.bfloat16)
        stream[:, lanes] = out
        wide = out.astype(jnp.float32)
        squares[...] += lax.dot_general(
            first_row,
            wide * wide,
            (((1,), (1,)), ((), ())),
            precision=HIGHEST,
            preferred_element_type=jnp.float32,
        )
        return carry

    lax.fori_loop(0, chans // HD, one_head, 0)


def late(halo, partial, feat, res, edge, taps, long_taps):
    rows, chans = res.shape
    vmem = pl.BlockSpec(memory_space=pltpu.VMEM)
    return pl.pallas_call(
        late_kernel,
        in_specs=[vmem] * 7,
        out_specs=[vmem] * 2,
        out_shape=[
            jax.ShapeDtypeStruct((rows, chans), jnp.bfloat16),
            jax.ShapeDtypeStruct((8, rows), jnp.float32),
        ],
        scratch_shapes=[
            pltpu.VMEM((rows + 8, HD), jnp.float32),
            pltpu.VMEM((rows + 16, HD), jnp.float32),
            pltpu.VMEM((8, rows + 16, HD), jnp.float32),
        ],
        compiler_params=pltpu.CompilerParams(vmem_limit_bytes=32 << 20),
        cost_estimate=pl.CostEstimate(flops=30_000_000_000, bytes_accessed=2_000_000, transcendentals=0),
        name="late",
    )(halo, partial, feat, res, edge, taps, long_taps)


def pack_kernel(gf, hv, gs, out, sems):
    rows = gf.shape[0]
    moves = [
        pltpu.make_async_copy(gf, out.at[0:rows], sems.at[0]),
        pltpu.make_async_copy(hv, out.at[rows : 2 * rows], sems.at[1]),
        pltpu.make_async_copy(gs.at[rows - 8 : rows], out.at[2 * rows : 2 * rows + 8], sems.at[2]),
    ]
    for move in moves:
        move.start()
    for move in moves:
        move.wait()


def pack(gf, hv, gs):
    rows, chans = gf.shape
    return pl.pallas_call(
        pack_kernel,
        in_specs=[pl.BlockSpec(memory_space=pltpu.HBM)] * 3,
        out_specs=pl.BlockSpec(memory_space=pltpu.VMEM),
        out_shape=jax.ShapeDtypeStruct((2 * rows + 8, chans), jnp.bfloat16),
        scratch_shapes=[pltpu.SemaphoreType.DMA((3,))],
        compiler_params=pltpu.CompilerParams(vmem_limit_bytes=16 << 20),
        cost_estimate=pl.CostEstimate(flops=0, bytes_accessed=600_000, transcendentals=0),
        name="pack",
    )(*in_hbm(gf, hv, gs))


def normalize_kernel(width, gathered, stream, gain, packed):
    parts = gathered.shape[0]
    total = lax.dot_general(
        gathered[...],
        jnp.ones((parts, HD), jnp.float32),
        (((0,), (0,)), ((), ())),
        precision=HIGHEST,
        preferred_element_type=jnp.float32,
    )
    inverse = 1.0 / jnp.sqrt(total / width + 1e-06)
    for head in range(packed.shape[1]):
        lanes = slice(head * HD, (head + 1) * HD)
        value = stream[:, lanes].astype(jnp.float32) * inverse * gain[:, lanes]
        value = value.astype(jnp.bfloat16)
        for copy in range(packed.shape[0]):
            packed[copy, head] = value


def normalize(width, gathered, stream, gain):
    rows, chans = stream.shape
    vmem = pl.BlockSpec(memory_space=pltpu.VMEM)
    return pl.pallas_call(
        functools.partial(normalize_kernel, width),
        in_specs=[vmem] * 3,
        out_specs=vmem,
        out_shape=jax.ShapeDtypeStruct((4, chans // HD, rows, HD), jnp.bfloat16),
        cost_estimate=pl.CostEstimate(flops=1_000_000, bytes_accessed=800_000, transcendentals=20_000),
        name="normalize",
    )(gathered, stream, gain)


def score_kernel(place, q0, q1, q2, q3, k0, k1, k2, k3, out, denom, scores, weights, sems):
    rows = q0.shape[0]
    keys = k0.shape[0]
    unit = math.log2(math.e) / math.sqrt(HD)
    chunks = [(begin, min(256, keys - begin)) for begin in range(0, keys, 256)]
    for index, query_ref in enumerate((q0, q1, q2, q3)):
        query = query_ref[...]
        query_pos = place[4 + index] + lax.broadcasted_iota(jnp.int32, (rows, 1), 0)
        top = None
        for part, ref in enumerate((k0, k1, k2, k3)):
            for begin, width in chunks:
                score = lax.dot_general(
                    query,
                    ref[begin : begin + width, :],
                    (((1,), (1,)), ((), ())),
                    preferred_element_type=jnp.float32,
                )
                lane = begin + lax.broadcasted_iota(jnp.int32, (1, width), 1)
                key_pos = place[part] + lane
                for edge in range(rows, keys, rows):
                    if edge < begin + width:
                        key_pos = key_pos + jnp.where(lane >= edge, rows, 0)
                score = jnp.where(key_pos <= query_pos, score * unit, -1e30)
                scores[:, part * keys + begin : part * keys + begin + width] = score
                for piece in range(0, width, 128):
                    piece = score[:, piece : min(piece + 128, width)]
                    if piece.shape[1] < 128:
                        piece = jnp.concatenate(
                            [piece, jnp.full((rows, 128 - piece.shape[1]), -1e30, jnp.float32)], axis=1
                        )
                    top = piece if top is None else jnp.maximum(top, piece)
        top = jnp.max(top, axis=1, keepdims=True)
        total = jnp.zeros((rows, 128), jnp.float32)
        for begin in range(0, 4 * keys, 128):
            expo = jnp.exp2(scores[:, begin : begin + 128] - top)
            total = total + expo
            weights[index, :, begin : begin + 128] = expo.astype(jnp.bfloat16)
        total = jnp.sum(total, axis=1, keepdims=True)
        denom[index] = jnp.broadcast_to(total, (rows, 128))
        pltpu.make_async_copy(weights.at[index], out.at[index], sems.at[index]).start()
    for index in range(4):
        pltpu.make_async_copy(weights.at[index], out.at[index], sems.at[index]).wait()


def score(place, queries, keys):
    rows = queries[0].shape[0]
    blocks = len(queries)
    count = sum(part.shape[0] for part in keys)
    vmem = pl.BlockSpec(memory_space=pltpu.VMEM)
    return pl.pallas_call(
        score_kernel,
        in_specs=[pl.BlockSpec(memory_space=pltpu.SMEM)] + [vmem] * 8,
        out_specs=[pl.BlockSpec(memory_space=pltpu.HBM), vmem],
        out_shape=[
            pltpu.HBM((blocks, rows, count), jnp.bfloat16),
            jax.ShapeDtypeStruct((blocks, rows, 128), jnp.float32),
        ],
        scratch_shapes=[
            pltpu.VMEM((rows, count), jnp.float32),
            pltpu.VMEM((blocks, rows, count), jnp.bfloat16),
            pltpu.SemaphoreType.DMA((blocks,)),
        ],
        compiler_params=pltpu.CompilerParams(vmem_limit_bytes=32 << 20),
        cost_estimate=pl.CostEstimate(
            flops=2 * blocks * rows * count * HD,
            bytes_accessed=8_000_000,
            transcendentals=blocks * rows * count,
        ),
        name="score",
    )(place, *queries, *keys)


def attend_kernel(place, weights_in, denom, v_own, v_other, out, weights, sems):
    blocks, rows, _ = out.shape
    half = v_own.shape[0] // 2
    moves = [
        pltpu.make_async_copy(weights_in.at[index], weights.at[index], sems.at[index]) for index in range(blocks)
    ]
    for move in moves:
        move.start()
    for index, move in enumerate(moves):
        move.wait()
        total = jnp.zeros((rows, HD), jnp.float32)
        for part in range(4):
            begin = pl.multiple_of(place[12 + part // 2] * half, 16)
            ref = v_other if part % 2 else v_own
            total = total + jnp.dot(
                weights[index, :, part * half : (part + 1) * half],
                ref[pl.ds(begin, half), :],
                preferred_element_type=jnp.float32,
            )
        out[place[8 + index]] = (total / denom[index]).astype(jnp.bfloat16)


def attend(place, weights, denom, v_own, v_other):
    blocks, rows, keys = weights.shape
    vmem = pl.BlockSpec(memory_space=pltpu.VMEM)
    return pl.pallas_call(
        attend_kernel,
        in_specs=[pl.BlockSpec(memory_space=pltpu.SMEM), pl.BlockSpec(memory_space=pltpu.HBM), vmem, vmem, vmem],
        out_specs=vmem,
        out_shape=jax.ShapeDtypeStruct((blocks, rows, HD), jnp.bfloat16),
        scratch_shapes=[pltpu.VMEM((blocks, rows, keys), jnp.bfloat16), pltpu.SemaphoreType.DMA((blocks,))],
        compiler_params=pltpu.CompilerParams(vmem_limit_bytes=16 << 20),
        cost_estimate=pl.CostEstimate(
            flops=2 * blocks * rows * keys * HD, bytes_accessed=7_000_000, transcendentals=0
        ),
        name="attend",
    )(place, *in_hbm(weights), denom, v_own, v_other)


def exchange(value, axes):
    return lax.all_to_all(value, axes, 0, 0, tiled=True)


def swap_cores(value):
    return lax.ppermute(value, "c", [(0, 1), (1, 0)])


def shards(residual, gate_first, gate_second, hyena_value, short_taps, long_taps, norm_gain, queries, attn_keys):
    rows, chans = residual.shape
    heads = chans // HD
    count = 32
    width = chans * 16

    core = lax.axis_index("c")
    head = lax.axis_index("h")
    side = lax.axis_index("zh")
    group = side * 16 + lax.axis_index("s") * 8 + core
    owners = [head ^ flip for flip in range(heads)]
    place = [side * 16 + core, side * 16 + 1 - core, (1 - side) * 16 + core, (1 - side) * 16 + 1 - core]
    place = place + [group + owner * 2 for owner in owners]
    place = jnp.concatenate([jnp.stack(place) * rows, jnp.stack(owners + [side, 1 - side])]).astype(jnp.int32)

    last = pack(gate_first, hyena_value, gate_second)
    halo = lax.ppermute(
        last,
        ROWS_AXES,
        [(source, source + 1) for source in range(count - 1)],
    )
    *early_parts, keys_by_head = early(
        last, gate_second, residual, short_taps, long_taps, attn_keys
    )
    keys_near = exchange(keys_by_head.reshape(8, rows, HD), ("s", "h"))

    stream, squares = late(halo, *early_parts)
    gathered = lax.all_gather(squares, CHAN_AXES, axis=0, tiled=True)
    packed = normalize(width, gathered, stream, norm_gain.reshape(1, chans))
    keys_near, packed = lax.optimization_barrier((keys_near, packed))
    values_own = exchange(packed.reshape(16, rows, HD), PEERS)

    keys_far = lax.ppermute(keys_near, "zh", [(0, 1)])
    parts = [keys_near, swap_cores(keys_near), keys_far, swap_cores(keys_far)]
    blocks = []
    for flip, owner in enumerate(owners):
        block = lax.dynamic_slice_in_dim(queries, owner * HD, HD, 1)
        if flip:
            block = lax.ppermute(block, "h", [(source, source ^ flip) for source in range(heads)])
        blocks.append(block)
    weights, denom = score(place, blocks, [part.reshape(8 * rows, HD) for part in parts])
    values_own, denom = lax.optimization_barrier((values_own, denom))
    values_other = swap_cores(values_own)
    result = attend(
        place, weights, denom, values_own.reshape(16 * rows, HD), values_other.reshape(16 * rows, HD)
    )
    attended = exchange(result, "h").transpose(1, 0, 2).reshape(rows, chans)
    return stream, attended


def solution(mesh):
    inner = Mesh(mesh.devices.reshape(2, 2, 4, 2, 4, 4), ROWS_AXES + CHAN_AXES)
    both = P(ROWS_AXES, CHAN_AXES)
    return jax.shard_map(
        shards,
        mesh=inner,
        in_specs=(both, both, both, both, P(None, None, CHAN_AXES), P(None, CHAN_AXES), P(CHAN_AXES), both, both),
        out_specs=(both, both),
        check_vma=False,
    )
```

time: 139 us -> 136 us (0.978)
  waiting for transfers between devices: 28.5 us -> 5.59 us
  starting transfers between devices: 45.8 us -> 60.2 us
  local copies, waits for them, and re-layouts: 9.5 us -> 0.88 us
  blocking collectives: 38.8 us -> 46.9 us
  Pallas kernels: 13.8 us -> 20.3 us
    all_gather x0 -> x1, blocking collectives: none -> 38.7 us  [shards(): gathered = lax.all_gather(squares, CHAN_AXES, axis=0, tiled=True)]
    all_to_all x2 -> x1, blocking collectives: 38.8 us -> 8.27 us  [exchange(): return lax.all_to_all(value, axes, 0, 0, tiled=True)]
    all_to_all x4 -> x2, waiting for transfers between devices: 23.9 us -> 0.01 us  [exchange(): return lax.all_to_all(value, axes, 0, 0, tiled=True)]
    ppermute x1 -> x5, starting transfers between devices: 4.59 us -> 21.1 us  [the longest x3 9.27 us: shards(): lax.ppermute(block, 'h', [(source, source ^ flip) for source in range(hea...]
    pallas_call x2 -> x5, Pallas kernels: 8.62 us -> 14.2 us  [the longest x1 4.25 us: attend(): pl.pallas_call(attend_kernel, in_specs=[pl.BlockSpec(memory_space=pltpu.S...]
    unnamed x16 -> x2, local copies, waits for them, and re-layouts: 5.28 us -> 0.01 us
    ppermute x3, starting transfers between devices: 21.5 us -> 18.4 us  [swap_cores(): return lax.ppermute(value, 'c', [(0, 1), (1, 0)])]
    ppermute x3, waiting for transfers between devices: 0.01 us -> 1.57 us  [swap_cores(): return lax.ppermute(value, 'c', [(0, 1), (1, 0)])]
  transfers between devices with their start and end apart: 8 -> 10, of which waited for: 5 -> 3; matrix products, arithmetic and copies ran while one was open for 2% -> 0% of each run, Pallas kernels for 4% -> 11%
where the time goes in v2:
time: 136 us; the launch traced here: 135 us
  starting transfers between devices  60.2 us (44%)
  blocking collectives  46.9 us (34%)
  Pallas kernels  20.3 us (15%)
  waiting for transfers between devices  5.59 us (4%)
    all_gather x1, blocking collectives, shards(): gathered = lax.all_gather(squares, CHAN_AXES, axis=0, tiled=True)  38.7 us
    all_to_all x2, starting transfers between devices, exchange(): return lax.all_to_all(value, axes, 0, 0, tiled=True)  20.7 us
    ppermute x3, starting transfers between devices, swap_cores(): return lax.ppermute(value, 'c', [(0, 1), (1, 0)])  18.4 us
    ppermute x3, starting transfers between devices, shards(): lax.ppermute(block, 'h', [(source, source ^ flip) for source in range(hea...  9.27 us
    all_to_all x1, blocking collectives, exchange(): return lax.all_to_all(value, axes, 0, 0, tiled=True)  8.27 us
    ppermute x1, starting transfers between devices, shards(): keys_far = lax.ppermute(keys_near, 'zh', [(0, 1)])  7.19 us
    pallas_call x1, Pallas kernels, score(): pl.pallas_call(score_kernel, in_specs=[pl.BlockSpec(memory_space=pltpu.SM...  6.06 us
    ppermute x1, starting transfers between devices, shards(): lax.ppermute(last, ROWS_AXES, [(source, source + 1) for source in range(c...  4.59 us
  transfers between devices with their start and end apart: 10, of which 3 were waited for; matrix products, arithmetic and copies ran while one was open for 0% of the time, Pallas kernels for 11%

profile of v2, /device:TPU:1, one launch (start us, length us, event | category | flops | bytes accessed | tf_op | source)
XLA Modules:
  0.0 134.8 jit_solution(12984512212930395588)
XLA Ops:
  0.6 1.0 pack.1.packed
  1.6 4.6 %collective-permute-start = (bf16[280,512]{1,0:T(8,128)(2,1)S(1)}, bf16[280,512]{1,0:T(8,128)(2,1)S(1)}, u32[]{:S(2)}, u32[]{:S(2)}) collective-permute-start(bf16[280,512]{1,0:T(8,128)(2,1)S(1)} %pack.1.packed), channel_id=1, source_target_pairs={{0,16},{16,32},{32,48},{48,64},{64,80},{80,96},{96,112},{112,128},... | collective-permute-start | bytes 860168 | tf_op jit(solution)/shard_map/ppermute | solution.py:386
  6.2 3.5 %early.1 = (f32[136,512]{1,0:T(8,128)S(1)}, f32[136,512]{1,0:T(8,128)S(1)}, bf16[136,512]{1,0:T(8,128)(2,1)S(1)}, f32[3,8,512]{2,1,0:T(8,128)S(1)}, f32[3,3,512]...) custom-call(bf16[280,512]{1,0:T(8,128)(2,1)S(1)} %pack.1.packed, ...), custom_call_target="tpu_custom_call" | custom-call | flops 6000000000 | bytes 2000000 | tf_op jit(solution)/shard_map/early/pallas_call | solution.py:102
  9.8 11.1 %all-to-all-start = ((bf16[8,136,128]{2,1,0:T(8,128)(2,1)}), bf16[8,136,128]{2,1,0:T(8,128)(2,1)S(1)}, u32[]{:S(2)}, u32[]{:S(2)}) async-start(bf16[8,136,128]{2,1,0:T(8,128)(2,1)} %bitcast.14), calls=%async_computation | async-start | bytes 557056 | tf_op jit(solution)/shard_map/all_to_all | solution.py:363
  20.9 3.3 %late.1 = (bf16[136,512]{1,0:T(8,128)(2,1)}, f32[8,136]{1,0:T(8,128)S(1)}) custom-call(bf16[280,512]{1,0:T(8,128)(2,1)S(1)} %collective-permute-done.halo, f32[136,512]{1,0:T(8,128)S(1)} %get-tuple-element.17.partial, f32[136,512]{1,0:T(8,128)S(1)} %get-tuple-element.18.feat, bf16[136,512]{1,0:T(8,128)(2,1)S(1)} %get-tuple-element.19.res, ...), custom_call_target="tpu_custom_call" | custom-call | flops 30000001024 | bytes 2000000 | tf_op jit(solution)/shard_map/late/pallas_call | solution.py:174
  24.2 38.7 %all_gather.3.gathered = f32[128,136]{1,0:T(8,128)} all-gather(f32[8,136]{1,0:T(8,128)S(1)} %get-tuple-element.25), channel_id=1, replica_groups=mesh['zh'=2,'s'=2,'h'=4,'c'=2,'x'=4,'zl'=4] {'x','zl'}, dimensions={0}, use_global_device_ids=true | all-gather | bytes 73984 | tf_op jit(solution)/shard_map/all_gather | solution.py:397
  62.9 2.1 %normalize.1 = bf16[4,4,136,128]{3,2,1,0:T(8,128)(2,1)} custom-call(f32[128,136]{1,0:T(8,128)} %all_gather.3.gathered, bf16[136,512]{1,0:T(8,128)(2,1)} %get-tuple-element.15.stream, f32[1,512]{1,0:T(1,128)} %bitcast.36), custom_call_target="tpu_custom_call" | custom-call | flops 1000000 | bytes 800000 | tf_op jit(solution)/shard_map/normalize/pallas_call | solution.py:241
  65.0 9.6 %all-to-all-start.1 = ((bf16[16,136,128]{2,1,0:T(8,128)(2,1)}), bf16[16,136,128]{2,1,0:T(8,128)(2,1)S(1)}, u32[]{:S(2)}, u32[]{:S(2)}) async-start(bf16[16,136,128]{2,1,0:T(8,128)(2,1)} %bitcast.35), calls=%async_computation.1 | async-start | bytes 1114112 | tf_op jit(solution)/shard_map/all_to_all | solution.py:363
  74.7 7.2 %collective-permute-start.5 = (bf16[8,136,128]{2,1,0:T(8,128)(2,1)S(1)}, bf16[8,136,128]{2,1,0:T(8,128)(2,1)S(1)}, u32[]{:S(2)}, u32[]{:S(2)}) collective-permute-start(bf16[8,136,128]{2,1,0:T(8,128)(2,1)S(1)} %all-to-all-done), channel_id=1, source_target_pairs={{0,256},{1,257},{2,258},{3,259},{4,260},{5,261},{6,262},{7,263},{8... | collective-permute-start | bytes 835592 | tf_op jit(solution)/shard_map/ppermute | solution.py:402
  81.9 10.4 %collective-permute-start.4 = (bf16[8,136,128]{2,1,0:T(8,128)(2,1)S(1)}, bf16[8,136,128]{2,1,0:T(8,128)(2,1)S(1)}, u32[]{:S(2)}, u32[]{:S(2)}) collective-permute-start(bf16[8,136,128]{2,1,0:T(8,128)(2,1)S(1)} %all-to-all-done), channel_id=1, source_target_pairs={{0,16},{16,0},{1,17},{17,1},{2,18},{18,2},{3,19},{19,3},{4,20},{20... | collective-permute-start | bytes 835592 | tf_op jit(solution)/shard_map/ppermute | solution.py:367
  92.2 2.1 %collective-permute-done.5 = bf16[8,136,128]{2,1,0:T(8,128)(2,1)S(1)} collective-permute-done((bf16[8,136,128]{2,1,0:T(8,128)(2,1)S(1)}, bf16[8,136,128]{2,1,0:T(8,128)(2,1)S(1)}, u32[]{:S(2)}, u32[]{:S(2)}) %collective-permute-start.5) | collective-permute-done | bytes 278560 | tf_op jit(solution)/shard_map/ppermute | solution.py:402
  94.4 4.1 %collective-permute-start.6 = (bf16[8,136,128]{2,1,0:T(8,128)(2,1)S(1)}, bf16[8,136,128]{2,1,0:T(8,128)(2,1)S(1)}, u32[]{:S(2)}, u32[]{:S(2)}) collective-permute-start(bf16[8,136,128]{2,1,0:T(8,128)(2,1)S(1)} %collective-permute-done.5), channel_id=1, source_target_pairs={{0,16},{16,0},{1,17},{17,1},{2,18},{18,2},{3,19},{19,3},{4,20},{20... | collective-permute-start | bytes 835592 | tf_op jit(solution)/shard_map/ppermute | solution.py:367
  98.5 3.8 %collective-permute-start.3 = (bf16[136,128]{1,0:T(8,128)(2,1)S(1)}, bf16[136,128]{1,0:T(8,128)(2,1)S(1)}, u32[]{:S(2)}, u32[]{:S(2)}) collective-permute-start(bf16[136,128]{1,0:T(8,128)(2,1)S(1)} %get-tuple-element.32), channel_id=1, source_target_pairs={{0,96},{32,64},{64,32},{96,0},{1,97},{33,65},{65,33},{97,1},{2,98}... | collective-permute-start | bytes 104456 | tf_op jit(solution)/shard_map/ppermute | solution.py:408
  102.4 2.0 %collective-permute-start.1 = (bf16[136,128]{1,0:T(8,128)(2,1)S(1)}, bf16[136,128]{1,0:T(8,128)(2,1)S(1)}, u32[]{:S(2)}, u32[]{:S(2)}) collective-permute-start(bf16[136,128]{1,0:T(8,128)(2,1)S(1)} %get-tuple-element.33), channel_id=1, source_target_pairs={{0,32},{32,0},{64,96},{96,64},{1,33},{33,1},{65,97},{97,65},{2,34}... | collective-permute-start | bytes 104456 | tf_op jit(solution)/shard_map/ppermute | solution.py:408
  104.3 3.5 %collective-permute-start.2 = (bf16[136,128]{1,0:T(8,128)(2,1)S(1)}, bf16[136,128]{1,0:T(8,128)(2,1)S(1)}, u32[]{:S(2)}, u32[]{:S(2)}) collective-permute-start(bf16[136,128]{1,0:T(8,128)(2,1)S(1)} %get-tuple-element.35), channel_id=1, source_target_pairs={{0,64},{32,96},{64,0},{96,32},{1,65},{33,97},{65,1},{97,33},{2,66}... | collective-permute-start | bytes 104456 | tf_op jit(solution)/shard_map/ppermute | solution.py:408
  107.8 0.1 stack.53
  107.9 0.1 concatenate.3.place
  108.0 1.9 %collective-permute-done.2.q2 = bf16[136,128]{1,0:T(8,128)(2,1)S(1)} collective-permute-done((bf16[136,128]{1,0:T(8,128)(2,1)S(1)}, bf16[136,128]{1,0:T(8,128)(2,1)S(1)}, u32[]{:S(2)}, u32[]{:S(2)}) %collective-permute-start.2) | collective-permute-done | bytes 34848 | tf_op jit(solution)/shard_map/ppermute | solution.py:408
  109.9 6.1 %score.1 = (bf16[4,136,4352]{2,1,0:T(8,128)(2,1)}, f32[4,136,128]{2,1,0:T(8,128)S(1)}) custom-call(s32[14]{0:T(128)S(1)} %concatenate.3.place, bf16[136,128]{1,0:T(8,128)(2,1)S(1)} %get-tuple-element.34.q0, bf16[136,128]{1,0:T(8,128)(2,1)S(1)} %collective-permute-done.1.q1, bf16[136,128]{1,0:T(8,128)(2,1)S(1)} %collective-permute-done.2.q2, ...), custom_call_target="tpu_custom_call" | custom-call | flops 606076928 | bytes 8000000 | tf_op jit(solution)/shard_map/score/pallas_call | solution.py:300
  116.0 4.0 %collective-permute-start.7 = (bf16[16,136,128]{2,1,0:T(8,128)(2,1)S(1)}, bf16[16,136,128]{2,1,0:T(8,128)(2,1)S(1)}, u32[]{:S(2)}, u32[]{:S(2)}) collective-permute-start(bf16[16,136,128]{2,1,0:T(8,128)(2,1)S(1)} %all-to-all-done.1), channel_id=1, source_target_pairs={{0,16},{16,0},{1,17},{17,1},{2,18},{18,2},{3,19},{19,3},{4,20},{20... | collective-permute-start | bytes 1671176 | tf_op jit(solution)/shard_map/ppermute | solution.py:367
  120.0 1.6 %collective-permute-done.7 = bf16[16,136,128]{2,1,0:T(8,128)(2,1)S(1)} collective-permute-done((bf16[16,136,128]{2,1,0:T(8,128)(2,1)S(1)}, bf16[16,136,128]{2,1,0:T(8,128)(2,1)S(1)}, u32[]{:S(2)}, u32[]{:S(2)}) %collective-permute-start.7) | collective-permute-done | bytes 557088 | tf_op jit(solution)/shard_map/ppermute | solution.py:367
  121.6 4.2 %attend.1 = bf16[4,136,128]{2,1,0:T(8,128)(2,1)S(1)} custom-call(s32[14]{0:T(128)S(1)} %concatenate.3.place, bf16[4,136,4352]{2,1,0:T(8,128)(2,1)} %get-tuple-element.27.weights_in, f32[4,136,128]{2,1,0:T(8,128)S(1)} %get-tuple-element.30.denom, bf16[2176,128]{1,0:T(8,128)(2,1)S(1)} %bitcast.29, bf16[2176,128]{1,0:T(8,128)(2,1)S(1)} %bitcast.30), custom_call_target="tpu_custom_call" | custom-call | flops 606076928 | bytes 7000000 | tf_op jit(solution)/shard_map/attend/pallas_call | solution.py:348
  125.8 8.3 %all_to_all.15 = bf16[4,136,128]{2,1,0:T(8,128)(2,1)S(1)} all-to-all(bf16[4,136,128]{2,1,0:T(8,128)(2,1)S(1)} %attend.1), channel_id=1, replica_groups=mesh['zh'=2,'s'=2,'h'=4,'c'=2,'x'=4,'zl'=4] {'h'}, dimensions={0} | all-to-all | bytes 278528 | tf_op jit(solution)/shard_map/all_to_all | solution.py:363
  134.1 0.7 copy_bitcast_fusion
  (11 shorter events, 0.1 us)
Async XLA Ops:
  1.6 19.3 %collective-permute-start = (bf16[280,512]{1,0:T(8,128)(2,1)S(1)}, bf16[280,512]{1,0:T(8,128)(2,1)S(1)}, u32[]{:S(2)}, u32[]{:S(2)}) collective-permute-start(bf16[280,512]{1,0:T(8,128)(2,1)S(1)} %pack.1.packed), channel_id=1, source_target_pairs={{0,16},{16,32},{32,48},{48,64},{64,80},{80,96},{96,112},{112,128},... | collective-permute-start | bytes 860168 | tf_op jit(solution)/shard_map/ppermute | solution.py:386
  9.8 55.2 %all-to-all-start = ((bf16[8,136,128]{2,1,0:T(8,128)(2,1)}), bf16[8,136,128]{2,1,0:T(8,128)(2,1)S(1)}, u32[]{:S(2)}, u32[]{:S(2)}) async-start(bf16[8,136,128]{2,1,0:T(8,128)(2,1)} %bitcast.14), calls=%async_computation | async-start | bytes 557056 | tf_op jit(solution)/shard_map/all_to_all | solution.py:363
  20.9 77.6 %copy-start = (bf16[136,512]{1,0:T(8,128)(2,1)S(1)}, bf16[136,512]{1,0:T(8,128)(2,1)}, u32[]{:S(2)}) copy-start(bf16[136,512]{1,0:T(8,128)(2,1)} %param.16) | copy-start | bytes 417796
  65.0 51.0 %all-to-all-start.1 = ((bf16[16,136,128]{2,1,0:T(8,128)(2,1)}), bf16[16,136,128]{2,1,0:T(8,128)(2,1)S(1)}, u32[]{:S(2)}, u32[]{:S(2)}) async-start(bf16[16,136,128]{2,1,0:T(8,128)(2,1)} %bitcast.35), calls=%async_computation.1 | async-start | bytes 1114112 | tf_op jit(solution)/shard_map/all_to_all | solution.py:363
  74.7 19.7 %collective-permute-start.5 = (bf16[8,136,128]{2,1,0:T(8,128)(2,1)S(1)}, bf16[8,136,128]{2,1,0:T(8,128)(2,1)S(1)}, u32[]{:S(2)}, u32[]{:S(2)}) collective-permute-start(bf16[8,136,128]{2,1,0:T(8,128)(2,1)S(1)} %all-to-all-done), channel_id=1, source_target_pairs={{0,256},{1,257},{2,258},{3,259},{4,260},{5,261},{6,262},{7,263},{8... | collective-permute-start | bytes 835592 | tf_op jit(solution)/shard_map/ppermute | solution.py:402
  81.9 28.0 %collective-permute-start.4 = (bf16[8,136,128]{2,1,0:T(8,128)(2,1)S(1)}, bf16[8,136,128]{2,1,0:T(8,128)(2,1)S(1)}, u32[]{:S(2)}, u32[]{:S(2)}) collective-permute-start(bf16[8,136,128]{2,1,0:T(8,128)(2,1)S(1)} %all-to-all-done), channel_id=1, source_target_pairs={{0,16},{16,0},{1,17},{17,1},{2,18},{18,2},{3,19},{19,3},{4,20},{20... | collective-permute-start | bytes 835592 | tf_op jit(solution)/shard_map/ppermute | solution.py:367
  94.4 15.6 %collective-permute-start.6 = (bf16[8,136,128]{2,1,0:T(8,128)(2,1)S(1)}, bf16[8,136,128]{2,1,0:T(8,128)(2,1)S(1)}, u32[]{:S(2)}, u32[]{:S(2)}) collective-permute-start(bf16[8,136,128]{2,1,0:T(8,128)(2,1)S(1)} %collective-permute-done.5), channel_id=1, source_target_pairs={{0,16},{16,0},{1,17},{17,1},{2,18},{18,2},{3,19},{19,3},{4,20},{20... | collective-permute-start | bytes 835592 | tf_op jit(solution)/shard_map/ppermute | solution.py:367
  98.5 9.5 %collective-permute-start.3 = (bf16[136,128]{1,0:T(8,128)(2,1)S(1)}, bf16[136,128]{1,0:T(8,128)(2,1)S(1)}, u32[]{:S(2)}, u32[]{:S(2)}) collective-permute-start(bf16[136,128]{1,0:T(8,128)(2,1)S(1)} %get-tuple-element.32), channel_id=1, source_target_pairs={{0,96},{32,64},{64,32},{96,0},{1,97},{33,65},{65,33},{97,1},{2,98}... | collective-permute-start | bytes 104456 | tf_op jit(solution)/shard_map/ppermute | solution.py:408
  102.4 5.7 %collective-permute-start.1 = (bf16[136,128]{1,0:T(8,128)(2,1)S(1)}, bf16[136,128]{1,0:T(8,128)(2,1)S(1)}, u32[]{:S(2)}, u32[]{:S(2)}) collective-permute-start(bf16[136,128]{1,0:T(8,128)(2,1)S(1)} %get-tuple-element.33), channel_id=1, source_target_pairs={{0,32},{32,0},{64,96},{96,64},{1,33},{33,1},{65,97},{97,65},{2,34}... | collective-permute-start | bytes 104456 | tf_op jit(solution)/shard_map/ppermute | solution.py:408
  104.3 5.6 %collective-permute-start.2 = (bf16[136,128]{1,0:T(8,128)(2,1)S(1)}, bf16[136,128]{1,0:T(8,128)(2,1)S(1)}, u32[]{:S(2)}, u32[]{:S(2)}) collective-permute-start(bf16[136,128]{1,0:T(8,128)(2,1)S(1)} %get-tuple-element.35), channel_id=1, source_target_pairs={{0,64},{32,96},{64,0},{96,32},{1,65},{33,97},{65,1},{97,33},{2,66}... | collective-permute-start | bytes 104456 | tf_op jit(solution)/shard_map/ppermute | solution.py:408
  116.0 5.6 %collective-permute-start.7 = (bf16[16,136,128]{2,1,0:T(8,128)(2,1)S(1)}, bf16[16,136,128]{2,1,0:T(8,128)(2,1)S(1)}, u32[]{:S(2)}, u32[]{:S(2)}) collective-permute-start(bf16[16,136,128]{2,1,0:T(8,128)(2,1)S(1)} %all-to-all-done.1), channel_id=1, source_target_pairs={{0,16},{16,0},{1,17},{17,1},{2,18},{18,2},{3,19},{19,3},{4,20},{20... | collective-permute-start | bytes 1671176 | tf_op jit(solution)/shard_map/ppermute | solution.py:367

commit v3 on v2

--- a/solution.py
+++ b/solution.py
@@ -46,19 +46,15 @@
 
 
 def early_kernel(
-    packed, gs, res, taps_in, long_in, keys, partial, feat, res_out, edge, taps_out, long_out, keys_out,
+    packed, gs, res, taps_in, long_in, partial, feat, res_out, edge, taps_out, long_out,
     gs_v, ext, prod, copies, sems,
 ):
     rows, chans = gs.shape
     loads = [(taps_in, taps_out), (long_in, long_out), (gs, gs_v), (res, res_out)]
     moves = [pltpu.make_async_copy(src, dst, sems.at[i]) for i, (src, dst) in enumerate(loads)]
-    for copy in range(keys_out.shape[0]):
-        for head in range(keys_out.shape[1]):
-            src = keys.at[:, head * HD : (head + 1) * HD]
-            moves.append(pltpu.make_async_copy(src, keys_out.at[copy, head], sems.at[len(moves)]))
     for move in moves:
         move.start()
-    for move in moves[:4]:
+    for move in moves:
         move.wait()
     tiles = rows // 8
     pairs = [(tile, group) for group in range(long_in.shape[0] // 8) for tile in range(group, tiles)]
@@ -86,23 +82,20 @@
         return carry
 
     lax.fori_loop(0, chans // HD, one_head, 0)
-    for move in moves[4:]:
-        move.wait()
 
 
 def in_hbm(*arrays):
     return [pltpu.with_memory_space_constraint(array, pltpu.HBM) for array in arrays]
 
 
-def early(packed, gs, res, taps, long_taps, keys):
+def early(packed, gs, res, taps, long_taps):
     rows, chans = gs.shape
-    heads = chans // HD
     hbm = pl.BlockSpec(memory_space=pltpu.HBM)
     vmem = pl.BlockSpec(memory_space=pltpu.VMEM)
     return pl.pallas_call(
         early_kernel,
-        in_specs=[vmem] + [hbm] * 5,
-        out_specs=[vmem] * 7,
+        in_specs=[vmem] + [hbm] * 4,
+        out_specs=[vmem] * 6,
         out_shape=[
             jax.ShapeDtypeStruct((rows, chans), jnp.float32),
             jax.ShapeDtypeStruct((rows, chans), jnp.float32),
@@ -110,19 +103,18 @@
             jax.ShapeDtypeStruct((3, 8, chans), jnp.float32),
             jax.ShapeDtypeStruct(taps.shape, jnp.float32),
             jax.ShapeDtypeStruct(long_taps.shape, jnp.bfloat16),
-            jax.ShapeDtypeStruct((2, heads, rows, HD), jnp.bfloat16),
         ],
         scratch_shapes=[
             pltpu.VMEM((rows, chans), jnp.bfloat16),
             pltpu.VMEM((rows + 8, HD), jnp.float32),
             pltpu.VMEM((rows + 8, HD), jnp.float32),
             pltpu.VMEM((8, rows + 8, HD), jnp.float32),
-            pltpu.SemaphoreType.DMA((4 + 2 * heads,)),
+            pltpu.SemaphoreType.DMA((4,)),
         ],
         compiler_params=pltpu.CompilerParams(vmem_limit_bytes=32 << 20),
         cost_estimate=pl.CostEstimate(flops=6_000_000_000, bytes_accessed=2_000_000, transcendentals=0),
         name="early",
-    )(packed, *in_hbm(gs, res, taps, long_taps, keys))
+    )(packed, *in_hbm(gs, res, taps, long_taps))
 
 
 def late_kernel(halo, partial, feat, res, edge, taps_in, long_in, stream, squares, ext, prod, copies):
@@ -130,12 +122,11 @@
     tiles = rows // 8
     pairs = [(tile, group) for group in range(long_in.shape[0] // 8) for tile in range(min(group + 2, tiles))]
     inside = lax.broadcasted_iota(jnp.int32, (rows, HD), 0) < rows - 6
-    first_row = (lax.broadcasted_iota(jnp.int32, (8, HD), 0) == 0).astype(jnp.float32)
     prod[0:8, :] = jnp.zeros((8, HD), jnp.float32)
     prod[rows + 8 :, :] = jnp.zeros((8, HD), jnp.float32)
-    squares[...] = jnp.zeros_like(squares)
-
-    def one_head(head, carry):
+    total = jnp.zeros((8, rows), jnp.float32)
+
+    def one_head(head, total):
         lanes = head_lanes(head)
         taps = taps_in[:, :, lanes]
 
@@ -156,16 +147,18 @@
         out = (res[:, lanes].astype(jnp.float32) + gate * filtered).astype(jnp.bfloat16)
         stream[:, lanes] = out
         wide = out.astype(jnp.float32)
-        squares[...] += lax.dot_general(
-            first_row,
+        total = total + lax.dot_general(
+            jnp.ones((8, HD), jnp.float32),
             wide * wide,
             (((1,), (1,)), ((), ())),
             precision=HIGHEST,
             preferred_element_type=jnp.float32,
         )
-        return carry
-
-    lax.fori_loop(0, chans // HD, one_head, 0)
+        return total
+
+    total = lax.fori_loop(0, chans // HD, one_head, total)
+    for peer in range(squares.shape[0]):
+        squares[peer] = total[0:1, :]
 
 
 def late(halo, partial, feat, res, edge, taps, long_taps):
@@ -177,7 +170,7 @@
         out_specs=[vmem] * 2,
         out_shape=[
             jax.ShapeDtypeStruct((rows, chans), jnp.bfloat16),
-            jax.ShapeDtypeStruct((8, rows), jnp.float32),
+            jax.ShapeDtypeStruct((16, 1, rows), jnp.float32),
         ],
         scratch_shapes=[
             pltpu.VMEM((rows + 8, HD), jnp.float32),
@@ -190,38 +183,55 @@
     )(halo, partial, feat, res, edge, taps, long_taps)
 
 
-def pack_kernel(gf, hv, gs, out, sems):
+def pack_kernel(gf, hv, gs, keys, queries, halo, keys_out, queries_out, sems):
     rows = gf.shape[0]
-    moves = [
-        pltpu.make_async_copy(gf, out.at[0:rows], sems.at[0]),
-        pltpu.make_async_copy(hv, out.at[rows : 2 * rows], sems.at[1]),
-        pltpu.make_async_copy(gs.at[rows - 8 : rows], out.at[2 * rows : 2 * rows + 8], sems.at[2]),
+    pairs = []
+    for copy in range(keys_out.shape[0]):
+        for head in range(keys_out.shape[1]):
+            pairs.append((keys.at[:, head * HD : (head + 1) * HD], keys_out.at[copy, head]))
+    pairs += [
+        (gf, halo.at[0:rows]),
+        (hv, halo.at[rows : 2 * rows]),
+        (gs.at[rows - 8 : rows], halo.at[2 * rows : 2 * rows + 8]),
+        (queries, queries_out.at[0:rows]),
+        (queries, queries_out.at[rows : 2 * rows]),
     ]
+    moves = [pltpu.make_async_copy(src, dst, sems.at[i]) for i, (src, dst) in enumerate(pairs)]
     for move in moves:
         move.start()
     for move in moves:
         move.wait()
 
 
-def pack(gf, hv, gs):
+def pack(gf, hv, gs, keys, queries):
     rows, chans = gf.shape
+    heads = chans // HD
+    vmem = pl.BlockSpec(memory_space=pltpu.VMEM)
+    hbm = pl.BlockSpec(memory_space=pltpu.HBM)
     return pl.pallas_call(
         pack_kernel,
-        in_specs=[pl.BlockSpec(memory_space=pltpu.HBM)] * 3,
-        out_specs=pl.BlockSpec(memory_space=pltpu.VMEM),
-        out_shape=jax.ShapeDtypeStruct((2 * rows + 8, chans), jnp.bfloat16),
-        scratch_shapes=[pltpu.SemaphoreType.DMA((3,))],
+        in_specs=[hbm] * 5,
+        out_specs=[vmem, vmem, hbm],
+        out_shape=[
+            jax.ShapeDtypeStruct((2 * rows + 8, chans), jnp.bfloat16),
+            jax.ShapeDtypeStruct((2, heads, rows, HD), jnp.bfloat16),
+            pltpu.HBM((2 * rows, chans), jnp.bfloat16),
+        ],
+        scratch_shapes=[pltpu.SemaphoreType.DMA((2 * heads + 5,))],
         compiler_params=pltpu.CompilerParams(vmem_limit_bytes=16 << 20),
         cost_estimate=pl.CostEstimate(flops=0, bytes_accessed=600_000, transcendentals=0),
         name="pack",
-    )(*in_hbm(gf, hv, gs))
+    )(*in_hbm(gf, hv, gs, keys, queries))
 
 
 def normalize_kernel(width, gathered, stream, gain, packed):
-    parts = gathered.shape[0]
+    total = gathered[0]
+    for peer in range(1, gathered.shape[0]):
+        total = total + gathered[peer]
+    total = jnp.broadcast_to(total, (8, total.shape[1]))
     total = lax.dot_general(
-        gathered[...],
-        jnp.ones((parts, HD), jnp.float32),
+        jnp.where(lax.broadcasted_iota(jnp.int32, total.shape, 0) == 0, total, 0.0),
+        jnp.ones((8, HD), jnp.float32),
         (((0,), (0,)), ((), ())),
         precision=HIGHEST,
         preferred_element_type=jnp.float32,
@@ -248,13 +258,23 @@
     )(gathered, stream, gain)
 
 
-def score_kernel(place, q0, q1, q2, q3, k0, k1, k2, k3, out, denom, scores, weights, sems):
-    rows = q0.shape[0]
+def score_kernel(place, gathered, k0, k1, k2, k3, out, denom, scores, weights, q, sems):
+    rows = q.shape[1]
     keys = k0.shape[0]
     unit = math.log2(math.e) / math.sqrt(HD)
     chunks = [(begin, min(256, keys - begin)) for begin in range(0, keys, 256)]
-    for index, query_ref in enumerate((q0, q1, q2, q3)):
-        query = query_ref[...]
+    blocks = q.shape[0]
+    begin = pl.multiple_of(place[8] * HD, HD)
+    moves = []
+    for index in range(blocks):
+        src = gathered.at[index * 2 * rows : index * 2 * rows + rows, pl.ds(begin, HD)]
+        moves.append(pltpu.make_async_copy(src, q.at[index], sems.at[index]))
+    for move in moves:
+        move.start()
+    for move in moves:
+        move.wait()
+    for index in range(blocks):
+        query = q[index]
         query_pos = place[4 + index] + lax.broadcasted_iota(jnp.int32, (rows, 1), 0)
         top = None
         for part, ref in enumerate((k0, k1, k2, k3)):
@@ -288,18 +308,18 @@
         total = jnp.sum(total, axis=1, keepdims=True)
         denom[index] = jnp.broadcast_to(total, (rows, 128))
         pltpu.make_async_copy(weights.at[index], out.at[index], sems.at[index]).start()
-    for index in range(4):
+    for index in range(blocks):
         pltpu.make_async_copy(weights.at[index], out.at[index], sems.at[index]).wait()
 
 
-def score(place, queries, keys):
-    rows = queries[0].shape[0]
-    blocks = len(queries)
+def score(place, gathered, keys):
+    rows = keys[0].shape[0] // 8
+    blocks = gathered.shape[0] // (2 * rows)
     count = sum(part.shape[0] for part in keys)
     vmem = pl.BlockSpec(memory_space=pltpu.VMEM)
     return pl.pallas_call(
         score_kernel,
-        in_specs=[pl.BlockSpec(memory_space=pltpu.SMEM)] + [vmem] * 8,
+        in_specs=[pl.BlockSpec(memory_space=pltpu.SMEM), pl.BlockSpec(memory_space=pltpu.HBM)] + [vmem] * 4,
         out_specs=[pl.BlockSpec(memory_space=pltpu.HBM), vmem],
         out_shape=[
             pltpu.HBM((blocks, rows, count), jnp.bfloat16),
@@ -308,6 +328,7 @@
         scratch_shapes=[
             pltpu.VMEM((rows, count), jnp.float32),
             pltpu.VMEM((blocks, rows, count), jnp.bfloat16),
+            pltpu.VMEM((blocks, rows, HD), jnp.bfloat16),
             pltpu.SemaphoreType.DMA((blocks,)),
         ],
         compiler_params=pltpu.CompilerParams(vmem_limit_bytes=32 << 20),
@@ -317,7 +338,7 @@
             transcendentals=blocks * rows * count,
         ),
         name="score",
-    )(place, *queries, *keys)
+    )(place, *in_hbm(gathered), *keys)
 
 
 def attend_kernel(place, weights_in, denom, v_own, v_other, out, weights, sems):
@@ -332,14 +353,14 @@
         move.wait()
         total = jnp.zeros((rows, HD), jnp.float32)
         for part in range(4):
-            begin = pl.multiple_of(place[12 + part // 2] * half, 16)
+            begin = pl.multiple_of(place[9 + part // 2] * half, 16)
             ref = v_other if part % 2 else v_own
             total = total + jnp.dot(
                 weights[index, :, part * half : (part + 1) * half],
                 ref[pl.ds(begin, half), :],
                 preferred_element_type=jnp.float32,
             )
-        out[place[8 + index]] = (total / denom[index]).astype(jnp.bfloat16)
+        out[index] = (total / denom[index]).astype(jnp.bfloat16)
 
 
 def attend(place, weights, denom, v_own, v_other):
@@ -377,37 +398,24 @@
     head = lax.axis_index("h")
     side = lax.axis_index("zh")
     group = side * 16 + lax.axis_index("s") * 8 + core
-    owners = [head ^ flip for flip in range(heads)]
     place = [side * 16 + core, side * 16 + 1 - core, (1 - side) * 16 + core, (1 - side) * 16 + 1 - core]
-    place = place + [group + owner * 2 for owner in owners]
-    place = jnp.concatenate([jnp.stack(place) * rows, jnp.stack(owners + [side, 1 - side])]).astype(jnp.int32)
-
-    last = pack(gate_first, hyena_value, gate_second)
-    halo = lax.ppermute(
-        last,
-        ROWS_AXES,
-        [(source, source + 1) for source in range(count - 1)],
-    )
-    *early_parts, keys_by_head = early(
-        last, gate_second, residual, short_taps, long_taps, attn_keys
-    )
+    place = place + [group + owner * 2 for owner in range(heads)]
+    place = jnp.concatenate([jnp.stack(place) * rows, jnp.stack([head, side, 1 - side])]).astype(jnp.int32)
+
+    last, keys_by_head, queries_twice = pack(gate_first, hyena_value, gate_second, attn_keys, queries)
     keys_near = exchange(keys_by_head.reshape(8, rows, HD), ("s", "h"))
-
+    queries_all = lax.all_gather(queries_twice, "h", axis=0, tiled=True)
+    halo = lax.ppermute(last, ROWS_AXES, [(source, source + 1) for source in range(count - 1)])
+    early_parts = early(last, gate_second, residual, short_taps, long_taps)
     stream, squares = late(halo, *early_parts)
-    gathered = lax.all_gather(squares, CHAN_AXES, axis=0, tiled=True)
+    keys_near, squares = lax.optimization_barrier((keys_near, squares))
+    gathered = exchange(squares, CHAN_AXES)
     packed = normalize(width, gathered, stream, norm_gain.reshape(1, chans))
-    keys_near, packed = lax.optimization_barrier((keys_near, packed))
     values_own = exchange(packed.reshape(16, rows, HD), PEERS)
 
     keys_far = lax.ppermute(keys_near, "zh", [(0, 1)])
     parts = [keys_near, swap_cores(keys_near), keys_far, swap_cores(keys_far)]
-    blocks = []
-    for flip, owner in enumerate(owners):
-        block = lax.dynamic_slice_in_dim(queries, owner * HD, HD, 1)
-        if flip:
-            block = lax.ppermute(block, "h", [(source, source ^ flip) for source in range(heads)])
-        blocks.append(block)
-    weights, denom = score(place, blocks, [part.reshape(8 * rows, HD) for part in parts])
+    weights, denom = score(place, queries_all, [part.reshape(8 * rows, HD) for part in parts])
     values_own, denom = lax.optimization_barrier((values_own, denom))
     values_other = swap_cores(values_own)
     result = attend(

time: 136 us -> 127 us (0.934)
  the two profiles are of different devices: /device:TPU:1 before, /device:TPU:64 now
where the time goes in v3:
time: 127 us; the launch traced here: 126 us
  starting transfers between devices  32.2 us (25%)
  Pallas kernels  29.7 us (23%)
  blocking collectives  26.7 us (21%)
  waiting for transfers between devices  22.5 us (18%)
  between operations  14.2 us (11%)
    all_to_all x2, blocking collectives, exchange(): return lax.all_to_all(value, axes, 0, 0, tiled=True)  26.7 us
    all_to_all x2, starting transfers between devices, exchange(): return lax.all_to_all(value, axes, 0, 0, tiled=True)  16.8 us
    ppermute x1, waiting for transfers between devices, shards(): keys_far = lax.ppermute(keys_near, 'zh', [(0, 1)])  14.4 us
    pallas_call x1, Pallas kernels, pack(): pl.pallas_call(pack_kernel, in_specs=[hbm] * 5, out_specs=[vmem, vmem, hb...  10.4 us
    ppermute x1, starting transfers between devices, shards(): keys_far = lax.ppermute(keys_near, 'zh', [(0, 1)])  7.75 us
    pallas_call x1, Pallas kernels, score(): pl.pallas_call(score_kernel, in_specs=[pl.BlockSpec(memory_space=pltpu.SM...  6.93 us
    ppermute x3, starting transfers between devices, swap_cores(): return lax.ppermute(value, 'c', [(0, 1), (1, 0)])  5.87 us
    all_to_all x2, waiting for transfers between devices, exchange(): return lax.all_to_all(value, axes, 0, 0, tiled=True)  4.8 us
  transfers between devices with their start and end apart: 8, of which 4 were waited for; matrix products, arithmetic and copies ran while one was open for 0% of the time, Pallas kernels for 12%

profile of v3, /device:TPU:64, one launch (start us, length us, event | category | flops | bytes accessed | tf_op | source)
XLA Modules:
  0.0 126.1 jit_solution(17710450105792367873)
XLA Ops:
  7.2 0.0 all-gather.2.cloned.1.call-start
  7.2 10.4 %pack.1 = (bf16[280,512]{1,0:T(8,128)(2,1)S(1)}, bf16[2,4,136,128]{3,2,1,0:T(8,128)(2,1)}, bf16[272,512]{1,0:T(8,128)(2,1)}) custom-call(bf16[136,512]{1,0:T(8,128)(2,1)} %gf.1, bf16[136,512]{1,0:T(8,128)(2,1)} %hv.1, bf16[136,512]{1,0:T(8,128)(2,1)} %gs.3, bf16[136,512]{1,0:T(8,128)(2,1)} %keys.1, bf16[136,512]{1,0:T(8,128)(2,1)} %queries.1), custom_call_target="tpu_custom_call" | custom-call | bytes 600000 | tf_op jit(solution)/shard_map/pack/pallas_call | solution.py:211
  17.6 1.8 %collective-permute-start = (bf16[280,512]{1,0:T(8,128)(2,1)S(1)}, bf16[280,512]{1,0:T(8,128)(2,1)S(1)}, u32[]{:S(2)}, u32[]{:S(2)}) collective-permute-start(bf16[280,512]{1,0:T(8,128)(2,1)S(1)} %get-tuple-element.19.packed), channel_id=1, source_target_pairs={{0,16},{16,32},{32,48},{48,64},{64,80},{80,96},{96,112},{112,128},... | collective-permute-start | bytes 860168 | tf_op jit(solution)/shard_map/ppermute | solution.py:408
  19.3 0.0 all-gather.2.cloned.1.call-update
  19.4 7.3 %all-to-all-start = ((bf16[8,136,128]{2,1,0:T(8,128)(2,1)}), bf16[8,136,128]{2,1,0:T(8,128)(2,1)S(1)}, u32[]{:S(2)}, u32[]{:S(2)}) async-start(bf16[8,136,128]{2,1,0:T(8,128)(2,1)} %bitcast.11), calls=%async_computation | async-start | bytes 557056 | tf_op jit(solution)/shard_map/all_to_all | solution.py:384
  26.6 2.8 %early.1 = (f32[136,512]{1,0:T(8,128)S(1)}, f32[136,512]{1,0:T(8,128)S(1)}, bf16[136,512]{1,0:T(8,128)(2,1)S(1)}, f32[3,8,512]{2,1,0:T(8,128)S(1)}, f32[3,3,512]...) custom-call(bf16[280,512]{1,0:T(8,128)(2,1)S(1)} %get-tuple-element.19.packed, bf16[136,512]{1,0:T(8,128)(2,1)} %gs.3, ...), custom_call_target="tpu_custom_call" | custom-call | flops 6000000000 | bytes 2000000 | tf_op jit(solution)/shard_map/early/pallas_call | solution.py:95
  29.4 3.3 %late.1 = (bf16[136,512]{1,0:T(8,128)(2,1)}, f32[16,1,136]{2,1,0:T(1,128)S(1)}) custom-call(bf16[280,512]{1,0:T(8,128)(2,1)S(1)} %collective-permute-done.halo, f32[136,512]{1,0:T(8,128)S(1)} %get-tuple-element.20.partial, f32[136,512]{1,0:T(8,128)S(1)} %get-tuple-element.21.feat, bf16[136,512]{1,0:T(8,128)(2,1)S(1)} %get-tuple-element.22.res, ...), custom_call_target="tpu_custom_call" | custom-call | flops 30000001024 | bytes 2000000 | tf_op jit(solution)/shard_map/late/pallas_call | solution.py:167
  32.7 4.8 %all-to-all-done = bf16[8,136,128]{2,1,0:T(8,128)(2,1)S(1)} async-done(((bf16[8,136,128]{2,1,0:T(8,128)(2,1)}), bf16[8,136,128]{2,1,0:T(8,128)(2,1)S(1)}, u32[]{:S(2)}, u32[]{:S(2)}) %all-to-all-start) | async-done | bytes 278560 | tf_op jit(solution)/shard_map/all_to_all | solution.py:384
  37.5 16.4 %all_to_all.20.gathered = f32[16,1,136]{2,1,0:T(1,128)} all-to-all(f32[16,1,136]{2,1,0:T(1,128)S(1)} %get-tuple-element.32), channel_id=1, replica_groups=mesh['zh'=2,'s'=2,'h'=4,'c'=2,'x'=4,'zl'=4] {'x','zl'}, dimensions={0} | all-to-all | bytes 17408 | tf_op jit(solution)/shard_map/all_to_all | solution.py:384
  53.9 2.1 %normalize.1 = bf16[4,4,136,128]{3,2,1,0:T(8,128)(2,1)} custom-call(f32[16,1,136]{2,1,0:T(1,128)} %all_to_all.20.gathered, bf16[136,512]{1,0:T(8,128)(2,1)} %get-tuple-element.17.stream, f32[1,512]{1,0:T(1,128)} %bitcast.33), custom_call_target="tpu_custom_call" | custom-call | flops 1000000 | bytes 800000 | tf_op jit(solution)/shard_map/normalize/pallas_call | solution.py:251
  56.0 9.6 %all-to-all-start.2 = ((bf16[16,136,128]{2,1,0:T(8,128)(2,1)}), bf16[16,136,128]{2,1,0:T(8,128)(2,1)S(1)}, u32[]{:S(2)}, u32[]{:S(2)}) async-start(bf16[16,136,128]{2,1,0:T(8,128)(2,1)} %bitcast.32), calls=%async_computation.2 | async-start | bytes 1114112 | tf_op jit(solution)/shard_map/all_to_all | solution.py:384
  65.6 7.7 %collective-permute-start.2 = (bf16[8,136,128]{2,1,0:T(8,128)(2,1)S(1)}, bf16[8,136,128]{2,1,0:T(8,128)(2,1)S(1)}, u32[]{:S(2)}, u32[]{:S(2)}) collective-permute-start(bf16[8,136,128]{2,1,0:T(8,128)(2,1)S(1)} %all-to-all-done), channel_id=1, source_target_pairs={{0,256},{1,257},{2,258},{3,259},{4,260},{5,261},{6,262},{7,263},{8... | collective-permute-start | bytes 835592 | tf_op jit(solution)/shard_map/ppermute | solution.py:416
  73.3 0.1 stack.44
  73.4 1.9 %collective-permute-start.1 = (bf16[8,136,128]{2,1,0:T(8,128)(2,1)S(1)}, bf16[8,136,128]{2,1,0:T(8,128)(2,1)S(1)}, u32[]{:S(2)}, u32[]{:S(2)}) collective-permute-start(bf16[8,136,128]{2,1,0:T(8,128)(2,1)S(1)} %all-to-all-done), channel_id=1, source_target_pairs={{0,16},{16,0},{1,17},{17,1},{2,18},{18,2},{3,19},{19,3},{4,20},{20... | collective-permute-start | bytes 835592 | tf_op jit(solution)/shard_map/ppermute | solution.py:388
  75.3 14.4 %collective-permute-done.2 = bf16[8,136,128]{2,1,0:T(8,128)(2,1)S(1)} collective-permute-done((bf16[8,136,128]{2,1,0:T(8,128)(2,1)S(1)}, bf16[8,136,128]{2,1,0:T(8,128)(2,1)S(1)}, u32[]{:S(2)}, u32[]{:S(2)}) %collective-permute-start.2) | collective-permute-done | bytes 278560 | tf_op jit(solution)/shard_map/ppermute | solution.py:416
  89.8 1.9 %collective-permute-start.3 = (bf16[8,136,128]{2,1,0:T(8,128)(2,1)S(1)}, bf16[8,136,128]{2,1,0:T(8,128)(2,1)S(1)}, u32[]{:S(2)}, u32[]{:S(2)}) collective-permute-start(bf16[8,136,128]{2,1,0:T(8,128)(2,1)S(1)} %collective-permute-done.2), channel_id=1, source_target_pairs={{0,16},{16,0},{1,17},{17,1},{2,18},{18,2},{3,19},{19,3},{4,20},{20... | collective-permute-start | bytes 835592 | tf_op jit(solution)/shard_map/ppermute | solution.py:388
  91.7 0.1 pad_add_fusion.place
  91.8 1.4 %collective-permute-done.3 = bf16[8,136,128]{2,1,0:T(8,128)(2,1)S(1)} collective-permute-done((bf16[8,136,128]{2,1,0:T(8,128)(2,1)S(1)}, bf16[8,136,128]{2,1,0:T(8,128)(2,1)S(1)}, u32[]{:S(2)}, u32[]{:S(2)}) %collective-permute-start.3) | collective-permute-done | bytes 278560 | tf_op jit(solution)/shard_map/ppermute | solution.py:388
  93.2 6.9 %score.1 = (bf16[4,136,4352]{2,1,0:T(8,128)(2,1)}, f32[4,136,128]{2,1,0:T(8,128)S(1)}) custom-call(s32[11]{0:T(128)S(1)} %pad_add_fusion.place, bf16[1088,512]{1,0:T(8,128)(2,1)} %all-gather.2.cloned.1.call-done.gathered, bf16[1088,128]{1,0:T(8,128)(2,1)S(1)} %bitcast.28, bf16[1088,128]{1,0:T(8,128)(2,1)S(1)} %bitcast.30, bf16[1088,128]{1,0:T(8,128)(2,1)S(1)} %bitcast.29, ...), custom_call_target="tpu_custom_call" | custom-call | flops 606076928 | bytes 8000000 | tf_op jit(solution)/shard_map/score/pallas_call | solution.py:320
  100.2 2.0 %collective-permute-start.4 = (bf16[16,136,128]{2,1,0:T(8,128)(2,1)S(1)}, bf16[16,136,128]{2,1,0:T(8,128)(2,1)S(1)}, u32[]{:S(2)}, u32[]{:S(2)}) collective-permute-start(bf16[16,136,128]{2,1,0:T(8,128)(2,1)S(1)} %all-to-all-done.2), channel_id=1, source_target_pairs={{0,16},{16,0},{1,17},{17,1},{2,18},{18,2},{3,19},{19,3},{4,20},{20... | collective-permute-start | bytes 1671176 | tf_op jit(solution)/shard_map/ppermute | solution.py:388
  102.2 1.8 %collective-permute-done.4 = bf16[16,136,128]{2,1,0:T(8,128)(2,1)S(1)} collective-permute-done((bf16[16,136,128]{2,1,0:T(8,128)(2,1)S(1)}, bf16[16,136,128]{2,1,0:T(8,128)(2,1)S(1)}, u32[]{:S(2)}, u32[]{:S(2)}) %collective-permute-start.4) | collective-permute-done | bytes 557088 | tf_op jit(solution)/shard_map/ppermute | solution.py:388
  104.0 4.3 %attend.1 = bf16[4,136,128]{2,1,0:T(8,128)(2,1)S(1)} custom-call(s32[11]{0:T(128)S(1)} %pad_add_fusion.place, bf16[4,136,4352]{2,1,0:T(8,128)(2,1)} %get-tuple-element.31.weights_in, f32[4,136,128]{2,1,0:T(8,128)S(1)} %get-tuple-element.34.denom, bf16[2176,128]{1,0:T(8,128)(2,1)S(1)} %bitcast.26, bf16[2176,128]{1,0:T(8,128)(2,1)S(1)} %bitcast.27), custom_call_target="tpu_custom_call" | custom-call | flops 606076928 | bytes 7000000 | tf_op jit(solution)/shard_map/attend/pallas_call | solution.py:369
  108.3 10.3 %all_to_all.21 = bf16[4,136,128]{2,1,0:T(8,128)(2,1)S(1)} all-to-all(bf16[4,136,128]{2,1,0:T(8,128)(2,1)S(1)} %attend.1), channel_id=1, replica_groups=mesh['zh'=2,'s'=2,'h'=4,'c'=2,'x'=4,'zl'=4] {'h'}, dimensions={0} | all-to-all | bytes 278528 | tf_op jit(solution)/shard_map/all_to_all | solution.py:384
  118.6 0.7 copy_bitcast_fusion
  (5 shorter events, 0.0 us)
Async XLA Ops:
  7.2 86.1 %all-gather.2.cloned.1.call-start = ((), (), s32[]{:S(2)}) async-start(), calls=%async_computation.4 | async-start | bytes 1392640 | tf_op jit(solution)/shard_map/all_gather | solution.py:407
  17.6 11.8 %collective-permute-start = (bf16[280,512]{1,0:T(8,128)(2,1)S(1)}, bf16[280,512]{1,0:T(8,128)(2,1)S(1)}, u32[]{:S(2)}, u32[]{:S(2)}) collective-permute-start(bf16[280,512]{1,0:T(8,128)(2,1)S(1)} %get-tuple-element.19.packed), channel_id=1, source_target_pairs={{0,16},{16,32},{32,48},{48,64},{64,80},{80,96},{96,112},{112,128},... | collective-permute-start | bytes 860168 | tf_op jit(solution)/shard_map/ppermute | solution.py:408
  19.4 18.1 %all-to-all-start = ((bf16[8,136,128]{2,1,0:T(8,128)(2,1)}), bf16[8,136,128]{2,1,0:T(8,128)(2,1)S(1)}, u32[]{:S(2)}, u32[]{:S(2)}) async-start(bf16[8,136,128]{2,1,0:T(8,128)(2,1)} %bitcast.11), calls=%async_computation | async-start | bytes 557056 | tf_op jit(solution)/shard_map/all_to_all | solution.py:384
  56.0 44.2 %all-to-all-start.2 = ((bf16[16,136,128]{2,1,0:T(8,128)(2,1)}), bf16[16,136,128]{2,1,0:T(8,128)(2,1)S(1)}, u32[]{:S(2)}, u32[]{:S(2)}) async-start(bf16[16,136,128]{2,1,0:T(8,128)(2,1)} %bitcast.32), calls=%async_computation.2 | async-start | bytes 1114112 | tf_op jit(solution)/shard_map/all_to_all | solution.py:384
  65.6 24.2 %collective-permute-start.2 = (bf16[8,136,128]{2,1,0:T(8,128)(2,1)S(1)}, bf16[8,136,128]{2,1,0:T(8,128)(2,1)S(1)}, u32[]{:S(2)}, u32[]{:S(2)}) collective-permute-start(bf16[8,136,128]{2,1,0:T(8,128)(2,1)S(1)} %all-to-all-done), channel_id=1, source_target_pairs={{0,256},{1,257},{2,258},{3,259},{4,260},{5,261},{6,262},{7,263},{8... | collective-permute-start | bytes 835592 | tf_op jit(solution)/shard_map/ppermute | solution.py:416
  73.4 18.4 %collective-permute-start.1 = (bf16[8,136,128]{2,1,0:T(8,128)(2,1)S(1)}, bf16[8,136,128]{2,1,0:T(8,128)(2,1)S(1)}, u32[]{:S(2)}, u32[]{:S(2)}) collective-permute-start(bf16[8,136,128]{2,1,0:T(8,128)(2,1)S(1)} %all-to-all-done), channel_id=1, source_target_pairs={{0,16},{16,0},{1,17},{17,1},{2,18},{18,2},{3,19},{19,3},{4,20},{20... | collective-permute-start | bytes 835592 | tf_op jit(solution)/shard_map/ppermute | solution.py:388
  89.8 3.4 %collective-permute-start.3 = (bf16[8,136,128]{2,1,0:T(8,128)(2,1)S(1)}, bf16[8,136,128]{2,1,0:T(8,128)(2,1)S(1)}, u32[]{:S(2)}, u32[]{:S(2)}) collective-permute-start(bf16[8,136,128]{2,1,0:T(8,128)(2,1)S(1)} %collective-permute-done.2), channel_id=1, source_target_pairs={{0,16},{16,0},{1,17},{17,1},{2,18},{18,2},{3,19},{19,3},{4,20},{20... | collective-permute-start | bytes 835592 | tf_op jit(solution)/shard_map/ppermute | solution.py:388
  100.2 3.9 %collective-permute-start.4 = (bf16[16,136,128]{2,1,0:T(8,128)(2,1)S(1)}, bf16[16,136,128]{2,1,0:T(8,128)(2,1)S(1)}, u32[]{:S(2)}, u32[]{:S(2)}) collective-permute-start(bf16[16,136,128]{2,1,0:T(8,128)(2,1)S(1)} %all-to-all-done.2), channel_id=1, source_target_pairs={{0,16},{16,0},{1,17},{17,1},{2,18},{18,2},{3,19},{19,3},{4,20},{20... | collective-permute-start | bytes 1671176 | tf_op jit(solution)/shard_map/ppermute | solution.py:388
Sparse Core Ops, SparseCore 0:
  19.5 41.6 all-gather.1

commit v4 on v3

--- a/solution.py
+++ b/solution.py
@@ -183,7 +183,7 @@
     )(halo, partial, feat, res, edge, taps, long_taps)
 
 
-def pack_kernel(gf, hv, gs, keys, queries, halo, keys_out, queries_out, sems):
+def pack_kernel(gf, hv, gs, keys, halo, keys_out, sems):
     rows = gf.shape[0]
     pairs = []
     for copy in range(keys_out.shape[0]):
@@ -193,8 +193,6 @@
         (gf, halo.at[0:rows]),
         (hv, halo.at[rows : 2 * rows]),
         (gs.at[rows - 8 : rows], halo.at[2 * rows : 2 * rows + 8]),
-        (queries, queries_out.at[0:rows]),
-        (queries, queries_out.at[rows : 2 * rows]),
     ]
     moves = [pltpu.make_async_copy(src, dst, sems.at[i]) for i, (src, dst) in enumerate(pairs)]
     for move in moves:
@@ -203,25 +201,24 @@
         move.wait()
 
 
-def pack(gf, hv, gs, keys, queries):
+def pack(gf, hv, gs, keys):
     rows, chans = gf.shape
     heads = chans // HD
     vmem = pl.BlockSpec(memory_space=pltpu.VMEM)
     hbm = pl.BlockSpec(memory_space=pltpu.HBM)
     return pl.pallas_call(
         pack_kernel,
-        in_specs=[hbm] * 5,
-        out_specs=[vmem, vmem, hbm],
+        in_specs=[hbm] * 4,
+        out_specs=[vmem, vmem],
         out_shape=[
             jax.ShapeDtypeStruct((2 * rows + 8, chans), jnp.bfloat16),
             jax.ShapeDtypeStruct((2, heads, rows, HD), jnp.bfloat16),
-            pltpu.HBM((2 * rows, chans), jnp.bfloat16),
-        ],
-        scratch_shapes=[pltpu.SemaphoreType.DMA((2 * heads + 5,))],
+        ],
+        scratch_shapes=[pltpu.SemaphoreType.DMA((2 * heads + 3,))],
         compiler_params=pltpu.CompilerParams(vmem_limit_bytes=16 << 20),
         cost_estimate=pl.CostEstimate(flops=0, bytes_accessed=600_000, transcendentals=0),
         name="pack",
-    )(*in_hbm(gf, hv, gs, keys, queries))
+    )(*in_hbm(gf, hv, gs, keys))
 
 
 def normalize_kernel(width, gathered, stream, gain, packed):
@@ -258,23 +255,13 @@
     )(gathered, stream, gain)
 
 
-def score_kernel(place, gathered, k0, k1, k2, k3, out, denom, scores, weights, q, sems):
-    rows = q.shape[1]
+def score_kernel(place, q0, q1, q2, q3, k0, k1, k2, k3, out, denom, scores, weights, sems):
+    rows = q0.shape[0]
     keys = k0.shape[0]
     unit = math.log2(math.e) / math.sqrt(HD)
     chunks = [(begin, min(256, keys - begin)) for begin in range(0, keys, 256)]
-    blocks = q.shape[0]
-    begin = pl.multiple_of(place[8] * HD, HD)
-    moves = []
-    for index in range(blocks):
-        src = gathered.at[index * 2 * rows : index * 2 * rows + rows, pl.ds(begin, HD)]
-        moves.append(pltpu.make_async_copy(src, q.at[index], sems.at[index]))
-    for move in moves:
-        move.start()
-    for move in moves:
-        move.wait()
-    for index in range(blocks):
-        query = q[index]
+    for index, query_ref in enumerate((q0, q1, q2, q3)):
+        query = query_ref[...]
         query_pos = place[4 + index] + lax.broadcasted_iota(jnp.int32, (rows, 1), 0)
         top = None
         for part, ref in enumerate((k0, k1, k2, k3)):
@@ -308,18 +295,18 @@
         total = jnp.sum(total, axis=1, keepdims=True)
         denom[index] = jnp.broadcast_to(total, (rows, 128))
         pltpu.make_async_copy(weights.at[index], out.at[index], sems.at[index]).start()
-    for index in range(blocks):
+    for index in range(4):
         pltpu.make_async_copy(weights.at[index], out.at[index], sems.at[index]).wait()
 
 
-def score(place, gathered, keys):
-    rows = keys[0].shape[0] // 8
-    blocks = gathered.shape[0] // (2 * rows)
+def score(place, queries, keys):
+    rows = queries[0].shape[0]
+    blocks = len(queries)
     count = sum(part.shape[0] for part in keys)
     vmem = pl.BlockSpec(memory_space=pltpu.VMEM)
     return pl.pallas_call(
         score_kernel,
-        in_specs=[pl.BlockSpec(memory_space=pltpu.SMEM), pl.BlockSpec(memory_space=pltpu.HBM)] + [vmem] * 4,
+        in_specs=[pl.BlockSpec(memory_space=pltpu.SMEM)] + [vmem] * 8,
         out_specs=[pl.BlockSpec(memory_space=pltpu.HBM), vmem],
         out_shape=[
             pltpu.HBM((blocks, rows, count), jnp.bfloat16),
@@ -328,7 +315,6 @@
         scratch_shapes=[
             pltpu.VMEM((rows, count), jnp.float32),
             pltpu.VMEM((blocks, rows, count), jnp.bfloat16),
-            pltpu.VMEM((blocks, rows, HD), jnp.bfloat16),
             pltpu.SemaphoreType.DMA((blocks,)),
         ],
         compiler_params=pltpu.CompilerParams(vmem_limit_bytes=32 << 20),
@@ -338,7 +324,7 @@
             transcendentals=blocks * rows * count,
         ),
         name="score",
-    )(place, *in_hbm(gathered), *keys)
+    )(place, *queries, *keys)
 
 
 def attend_kernel(place, weights_in, denom, v_own, v_other, out, weights, sems):
@@ -353,14 +339,14 @@
         move.wait()
         total = jnp.zeros((rows, HD), jnp.float32)
         for part in range(4):
-            begin = pl.multiple_of(place[9 + part // 2] * half, 16)
+            begin = pl.multiple_of(place[12 + part // 2] * half, 16)
             ref = v_other if part % 2 else v_own
             total = total + jnp.dot(
                 weights[index, :, part * half : (part + 1) * half],
                 ref[pl.ds(begin, half), :],
                 preferred_element_type=jnp.float32,
             )
-        out[index] = (total / denom[index]).astype(jnp.bfloat16)
+        out[place[8 + index]] = (total / denom[index]).astype(jnp.bfloat16)
 
 
 def attend(place, weights, denom, v_own, v_other):
@@ -398,24 +384,30 @@
     head = lax.axis_index("h")
     side = lax.axis_index("zh")
     group = side * 16 + lax.axis_index("s") * 8 + core
+    owners = [head ^ flip for flip in range(heads)]
     place = [side * 16 + core, side * 16 + 1 - core, (1 - side) * 16 + core, (1 - side) * 16 + 1 - core]
-    place = place + [group + owner * 2 for owner in range(heads)]
-    place = jnp.concatenate([jnp.stack(place) * rows, jnp.stack([head, side, 1 - side])]).astype(jnp.int32)
-
-    last, keys_by_head, queries_twice = pack(gate_first, hyena_value, gate_second, attn_keys, queries)
+    place = place + [group + owner * 2 for owner in owners]
+    place = jnp.concatenate([jnp.stack(place) * rows, jnp.stack(owners + [side, 1 - side])]).astype(jnp.int32)
+
+    last, keys_by_head = pack(gate_first, hyena_value, gate_second, attn_keys)
     keys_near = exchange(keys_by_head.reshape(8, rows, HD), ("s", "h"))
-    queries_all = lax.all_gather(queries_twice, "h", axis=0, tiled=True)
     halo = lax.ppermute(last, ROWS_AXES, [(source, source + 1) for source in range(count - 1)])
     early_parts = early(last, gate_second, residual, short_taps, long_taps)
     stream, squares = late(halo, *early_parts)
-    keys_near, squares = lax.optimization_barrier((keys_near, squares))
+
+    blocks = [lax.dynamic_slice_in_dim(queries, owner * HD, HD, 1) for owner in owners]
+    blocks, squares = lax.optimization_barrier((blocks, squares))
+    for flip in range(1, heads):
+        blocks[flip] = lax.ppermute(blocks[flip], "h", [(source, source ^ flip) for source in range(heads)])
+    keys_near, blocks, squares = lax.optimization_barrier((keys_near, blocks, squares))
+    keys_far = lax.ppermute(keys_near, "zh", [(0, 1)])
     gathered = exchange(squares, CHAN_AXES)
     packed = normalize(width, gathered, stream, norm_gain.reshape(1, chans))
+    packed, keys_far = lax.optimization_barrier((packed, keys_far))
     values_own = exchange(packed.reshape(16, rows, HD), PEERS)
 
-    keys_far = lax.ppermute(keys_near, "zh", [(0, 1)])
     parts = [keys_near, swap_cores(keys_near), keys_far, swap_cores(keys_far)]
-    weights, denom = score(place, queries_all, [part.reshape(8 * rows, HD) for part in parts])
+    weights, denom = score(place, blocks, [part.reshape(8 * rows, HD) for part in parts])
     values_own, denom = lax.optimization_barrier((values_own, denom))
     values_other = swap_cores(values_own)
     result = attend(

time: 127 us -> 108 us (0.85)
  the two profiles are of different devices: /device:TPU:64 before, /device:TPU:1 now
where the time goes in v4:
time: 108 us
  starting transfers between devices  54.6 us (51%)
  blocking collectives  21.9 us (20%)
  Pallas kernels  20.4 us (19%)
  waiting for transfers between devices  9.19 us (9%)
    all_to_all x2, blocking collectives, exchange(): return lax.all_to_all(value, axes, 0, 0, tiled=True)  21.9 us
    ppermute x3, starting transfers between devices, swap_cores(): return lax.ppermute(value, 'c', [(0, 1), (1, 0)])  17.1 us
    all_to_all x2, starting transfers between devices, exchange(): return lax.all_to_all(value, axes, 0, 0, tiled=True)  12.5 us
    ppermute x1, starting transfers between devices, shards(): keys_far = lax.ppermute(keys_near, 'zh', [(0, 1)])  9.6 us
    ppermute x3, starting transfers between devices, shards(): lax.ppermute(blocks[flip], 'h', [(source, source ^ flip) for source in ra...  9.26 us
    ppermute x1, starting transfers between devices, shards(): lax.ppermute(last, ROWS_AXES, [(source, source + 1) for source in range(c...  6.2 us
    pallas_call x1, Pallas kernels, score(): pl.pallas_call(score_kernel, in_specs=[pl.BlockSpec(memory_space=pltpu.SM...  6.08 us
    ppermute x3, waiting for transfers between devices, shards(): lax.ppermute(blocks[flip], 'h', [(source, source ^ flip) for source in ra...  4.53 us
  transfers between devices with their start and end apart: 10, of which 4 were waited for; matrix products, arithmetic and copies ran while one was open for 0% of the time, Pallas kernels for 13%

profile of v4, /device:TPU:1, one launch (start us, length us, event | category | flops | bytes accessed | tf_op | source)
XLA Modules:
  0.0 107.8 jit_solution(4594109766027884089)
XLA Ops:
  0.6 1.9 %pack.1 = (bf16[280,512]{1,0:T(8,128)(2,1)S(1)}, bf16[2,4,136,128]{3,2,1,0:T(8,128)(2,1)}) custom-call(bf16[136,512]{1,0:T(8,128)(2,1)} %gf.1, bf16[136,512]{1,0:T(8,128)(2,1)} %hv.1, bf16[136,512]{1,0:T(8,128)(2,1)} %gs.3, bf16[136,512]{1,0:T(8,128)(2,1)} %keys.1), custom_call_target="tpu_custom_call" | custom-call | bytes 600000 | tf_op jit(solution)/shard_map/pack/pallas_call | solution.py:209
  2.6 7.7 %all-to-all-start = ((bf16[8,136,128]{2,1,0:T(8,128)(2,1)}), bf16[8,136,128]{2,1,0:T(8,128)(2,1)S(1)}, u32[]{:S(2)}, u32[]{:S(2)}) async-start(bf16[8,136,128]{2,1,0:T(8,128)(2,1)} %bitcast.14), calls=%async_computation | async-start | bytes 557056 | tf_op jit(solution)/shard_map/all_to_all | solution.py:370
  10.2 6.2 %collective-permute-start = (bf16[280,512]{1,0:T(8,128)(2,1)S(1)}, bf16[280,512]{1,0:T(8,128)(2,1)S(1)}, u32[]{:S(2)}, u32[]{:S(2)}) collective-permute-start(bf16[280,512]{1,0:T(8,128)(2,1)S(1)} %get-tuple-element.29.packed), channel_id=1, source_target_pairs={{0,16},{16,32},{32,48},{48,64},{64,80},{80,96},{96,112},{112,128},... | collective-permute-start | bytes 860168 | tf_op jit(solution)/shard_map/ppermute | solution.py:394
  16.5 2.8 %early.1 = (f32[136,512]{1,0:T(8,128)S(1)}, f32[136,512]{1,0:T(8,128)S(1)}, bf16[136,512]{1,0:T(8,128)(2,1)S(1)}, f32[3,8,512]{2,1,0:T(8,128)S(1)}, f32[3,3,512]...) custom-call(bf16[280,512]{1,0:T(8,128)(2,1)S(1)} %get-tuple-element.29.packed, bf16[136,512]{1,0:T(8,128)(2,1)} %gs.3, ...), custom_call_target="tpu_custom_call" | custom-call | flops 6000000000 | bytes 2000000 | tf_op jit(solution)/shard_map/early/pallas_call | solution.py:95
  19.3 1.8 %collective-permute-done.halo = bf16[280,512]{1,0:T(8,128)(2,1)S(1)} collective-permute-done((bf16[280,512]{1,0:T(8,128)(2,1)S(1)}, bf16[280,512]{1,0:T(8,128)(2,1)S(1)}, u32[]{:S(2)}, u32[]{:S(2)}) %collective-permute-start) | collective-permute-done | bytes 286752 | tf_op jit(solution)/shard_map/ppermute | solution.py:394
  21.1 3.3 %late.1 = (bf16[136,512]{1,0:T(8,128)(2,1)}, f32[16,1,136]{2,1,0:T(1,128)S(1)}) custom-call(bf16[280,512]{1,0:T(8,128)(2,1)S(1)} %collective-permute-done.halo, f32[136,512]{1,0:T(8,128)S(1)} %get-tuple-element.30.partial, f32[136,512]{1,0:T(8,128)S(1)} %get-tuple-element.31.feat, bf16[136,512]{1,0:T(8,128)(2,1)S(1)} %get-tuple-element.32.res, ...), custom_call_target="tpu_custom_call" | custom-call | flops 30000001024 | bytes 2000000 | tf_op jit(solution)/shard_map/late/pallas_call | solution.py:167
  24.4 2.5 %collective-permute-start.1 = (bf16[136,128]{1,0:T(8,128)(2,1)S(1)}, bf16[136,128]{1,0:T(8,128)(2,1)S(1)}, u32[]{:S(2)}, u32[]{:S(2)}) collective-permute-start(bf16[136,128]{1,0:T(8,128)(2,1)S(1)} %get-tuple-element.40), channel_id=1, source_target_pairs={{0,32},{32,0},{64,96},{96,64},{1,33},{33,1},{65,97},{97,65},{2,34}... | collective-permute-start | bytes 104456 | tf_op jit(solution)/shard_map/ppermute | solution.py:401
  26.9 4.7 %collective-permute-start.2 = (bf16[136,128]{1,0:T(8,128)(2,1)S(1)}, bf16[136,128]{1,0:T(8,128)(2,1)S(1)}, u32[]{:S(2)}, u32[]{:S(2)}) collective-permute-start(bf16[136,128]{1,0:T(8,128)(2,1)S(1)} %get-tuple-element.41), channel_id=1, source_target_pairs={{0,64},{32,96},{64,0},{96,32},{1,65},{33,97},{65,1},{97,33},{2,66}... | collective-permute-start | bytes 104456 | tf_op jit(solution)/shard_map/ppermute | solution.py:401
  31.6 2.0 %collective-permute-start.3 = (bf16[136,128]{1,0:T(8,128)(2,1)S(1)}, bf16[136,128]{1,0:T(8,128)(2,1)S(1)}, u32[]{:S(2)}, u32[]{:S(2)}) collective-permute-start(bf16[136,128]{1,0:T(8,128)(2,1)S(1)} %get-tuple-element.42), channel_id=1, source_target_pairs={{0,96},{32,64},{64,32},{96,0},{1,97},{33,65},{65,33},{97,1},{2,98}... | collective-permute-start | bytes 104456 | tf_op jit(solution)/shard_map/ppermute | solution.py:401
  33.7 4.5 %collective-permute-done.3.q3 = bf16[136,128]{1,0:T(8,128)(2,1)S(1)} collective-permute-done((bf16[136,128]{1,0:T(8,128)(2,1)S(1)}, bf16[136,128]{1,0:T(8,128)(2,1)S(1)}, u32[]{:S(2)}, u32[]{:S(2)}) %collective-permute-start.3) | collective-permute-done | bytes 34848 | tf_op jit(solution)/shard_map/ppermute | solution.py:401
  38.2 9.6 %collective-permute-start.5 = (bf16[8,136,128]{2,1,0:T(8,128)(2,1)S(1)}, bf16[8,136,128]{2,1,0:T(8,128)(2,1)S(1)}, u32[]{:S(2)}, u32[]{:S(2)}) collective-permute-start(bf16[8,136,128]{2,1,0:T(8,128)(2,1)S(1)} %all-to-all-done), channel_id=1, source_target_pairs={{0,256},{1,257},{2,258},{3,259},{4,260},{5,261},{6,262},{7,263},{8... | collective-permute-start | bytes 835592 | tf_op jit(solution)/shard_map/ppermute | solution.py:403
  47.8 13.8 %all_to_all.20.gathered = f32[16,1,136]{2,1,0:T(1,128)} all-to-all(f32[16,1,136]{2,1,0:T(1,128)S(1)} %get-tuple-element.49), channel_id=1, replica_groups=mesh['zh'=2,'s'=2,'h'=4,'c'=2,'x'=4,'zl'=4] {'x','zl'}, dimensions={0} | all-to-all | bytes 17408 | tf_op jit(solution)/shard_map/all_to_all | solution.py:370
  61.6 2.1 %normalize.1 = bf16[4,4,136,128]{3,2,1,0:T(8,128)(2,1)} custom-call(f32[16,1,136]{2,1,0:T(1,128)} %all_to_all.20.gathered, bf16[136,512]{1,0:T(8,128)(2,1)} %get-tuple-element.27.stream, f32[1,512]{1,0:T(1,128)} %bitcast.36), custom_call_target="tpu_custom_call" | custom-call | flops 1000000 | bytes 800000 | tf_op jit(solution)/shard_map/normalize/pallas_call | solution.py:248
  63.6 4.8 %all-to-all-start.2 = ((bf16[16,136,128]{2,1,0:T(8,128)(2,1)}), bf16[16,136,128]{2,1,0:T(8,128)(2,1)S(1)}, u32[]{:S(2)}, u32[]{:S(2)}) async-start(bf16[16,136,128]{2,1,0:T(8,128)(2,1)} %bitcast.35), calls=%async_computation.2 | async-start | bytes 1114112 | tf_op jit(solution)/shard_map/all_to_all | solution.py:370
  68.5 9.0 %collective-permute-start.4 = (bf16[8,136,128]{2,1,0:T(8,128)(2,1)S(1)}, bf16[8,136,128]{2,1,0:T(8,128)(2,1)S(1)}, u32[]{:S(2)}, u32[]{:S(2)}) collective-permute-start(bf16[8,136,128]{2,1,0:T(8,128)(2,1)S(1)} %all-to-all-done), channel_id=1, source_target_pairs={{0,16},{16,0},{1,17},{17,1},{2,18},{18,2},{3,19},{19,3},{4,20},{20... | collective-permute-start | bytes 835592 | tf_op jit(solution)/shard_map/ppermute | solution.py:374
  77.5 1.9 %collective-permute-start.6 = (bf16[8,136,128]{2,1,0:T(8,128)(2,1)S(1)}, bf16[8,136,128]{2,1,0:T(8,128)(2,1)S(1)}, u32[]{:S(2)}, u32[]{:S(2)}) collective-permute-start(bf16[8,136,128]{2,1,0:T(8,128)(2,1)S(1)} %collective-permute-done.5), channel_id=1, source_target_pairs={{0,16},{16,0},{1,17},{17,1},{2,18},{18,2},{3,19},{19,3},{4,20},{20... | collective-permute-start | bytes 835592 | tf_op jit(solution)/shard_map/ppermute | solution.py:374
  79.6 0.1 concatenate.3.place
  79.7 1.3 %collective-permute-done.6 = bf16[8,136,128]{2,1,0:T(8,128)(2,1)S(1)} collective-permute-done((bf16[8,136,128]{2,1,0:T(8,128)(2,1)S(1)}, bf16[8,136,128]{2,1,0:T(8,128)(2,1)S(1)}, u32[]{:S(2)}, u32[]{:S(2)}) %collective-permute-start.6) | collective-permute-done | bytes 278560 | tf_op jit(solution)/shard_map/ppermute | solution.py:374
  81.0 6.1 %score.1 = (bf16[4,136,4352]{2,1,0:T(8,128)(2,1)}, f32[4,136,128]{2,1,0:T(8,128)S(1)}) custom-call(s32[14]{0:T(128)S(1)} %concatenate.3.place, bf16[136,128]{1,0:T(8,128)(2,1)S(1)} %get-tuple-element.44.q0, bf16[136,128]{1,0:T(8,128)(2,1)S(1)} %collective-permute-done.1.q1, bf16[136,128]{1,0:T(8,128)(2,1)S(1)} %collective-permute-done.2.q2, ...), custom_call_target="tpu_custom_call" | custom-call | flops 606076928 | bytes 8000000 | tf_op jit(solution)/shard_map/score/pallas_call | solution.py:307
  87.1 6.1 %collective-permute-start.7 = (bf16[16,136,128]{2,1,0:T(8,128)(2,1)S(1)}, bf16[16,136,128]{2,1,0:T(8,128)(2,1)S(1)}, u32[]{:S(2)}, u32[]{:S(2)}) collective-permute-start(bf16[16,136,128]{2,1,0:T(8,128)(2,1)S(1)} %all-to-all-done.2), channel_id=1, source_target_pairs={{0,16},{16,0},{1,17},{17,1},{2,18},{18,2},{3,19},{19,3},{4,20},{20... | collective-permute-start | bytes 1671176 | tf_op jit(solution)/shard_map/ppermute | solution.py:374
  93.2 1.6 %collective-permute-done.7 = bf16[16,136,128]{2,1,0:T(8,128)(2,1)S(1)} collective-permute-done((bf16[16,136,128]{2,1,0:T(8,128)(2,1)S(1)}, bf16[16,136,128]{2,1,0:T(8,128)(2,1)S(1)}, u32[]{:S(2)}, u32[]{:S(2)}) %collective-permute-start.7) | collective-permute-done | bytes 557088 | tf_op jit(solution)/shard_map/ppermute | solution.py:374
  94.8 4.2 %attend.1 = bf16[4,136,128]{2,1,0:T(8,128)(2,1)S(1)} custom-call(s32[14]{0:T(128)S(1)} %concatenate.3.place, bf16[4,136,4352]{2,1,0:T(8,128)(2,1)} %get-tuple-element.51.weights_in, f32[4,136,128]{2,1,0:T(8,128)S(1)} %get-tuple-element.54.denom, bf16[2176,128]{1,0:T(8,128)(2,1)S(1)} %bitcast.29, bf16[2176,128]{1,0:T(8,128)(2,1)S(1)} %bitcast.30), custom_call_target="tpu_custom_call" | custom-call | flops 606076928 | bytes 7000000 | tf_op jit(solution)/shard_map/attend/pallas_call | solution.py:355
  99.0 8.1 %all_to_all.21 = bf16[4,136,128]{2,1,0:T(8,128)(2,1)S(1)} all-to-all(bf16[4,136,128]{2,1,0:T(8,128)(2,1)S(1)} %attend.1), channel_id=1, replica_groups=mesh['zh'=2,'s'=2,'h'=4,'c'=2,'x'=4,'zl'=4] {'h'}, dimensions={0} | all-to-all | bytes 278528 | tf_op jit(solution)/shard_map/all_to_all | solution.py:370
  107.1 0.7 copy_bitcast_fusion
  (11 shorter events, 0.1 us)
Async XLA Ops:
  2.6 35.6 %all-to-all-start = ((bf16[8,136,128]{2,1,0:T(8,128)(2,1)}), bf16[8,136,128]{2,1,0:T(8,128)(2,1)S(1)}, u32[]{:S(2)}, u32[]{:S(2)}) async-start(bf16[8,136,128]{2,1,0:T(8,128)(2,1)} %bitcast.14), calls=%async_computation | async-start | bytes 557056 | tf_op jit(solution)/shard_map/all_to_all | solution.py:370
  10.2 9.0 %copy-start = (bf16[136,512]{1,0:T(8,128)(2,1)S(1)}, bf16[136,512]{1,0:T(8,128)(2,1)}, u32[]{:S(2)}) copy-start(bf16[136,512]{1,0:T(8,128)(2,1)} %param.16) | copy-start | bytes 417796
  10.2 10.8 %collective-permute-start = (bf16[280,512]{1,0:T(8,128)(2,1)S(1)}, bf16[280,512]{1,0:T(8,128)(2,1)S(1)}, u32[]{:S(2)}, u32[]{:S(2)}) collective-permute-start(bf16[280,512]{1,0:T(8,128)(2,1)S(1)} %get-tuple-element.29.packed), channel_id=1, source_target_pairs={{0,16},{16,32},{32,48},{48,64},{64,80},{80,96},{96,112},{112,128},... | collective-permute-start | bytes 860168 | tf_op jit(solution)/shard_map/ppermute | solution.py:394
  24.4 9.3 %collective-permute-start.1 = (bf16[136,128]{1,0:T(8,128)(2,1)S(1)}, bf16[136,128]{1,0:T(8,128)(2,1)S(1)}, u32[]{:S(2)}, u32[]{:S(2)}) collective-permute-start(bf16[136,128]{1,0:T(8,128)(2,1)S(1)} %get-tuple-element.40), channel_id=1, source_target_pairs={{0,32},{32,0},{64,96},{96,64},{1,33},{33,1},{65,97},{97,65},{2,34}... | collective-permute-start | bytes 104456 | tf_op jit(solution)/shard_map/ppermute | solution.py:401
  26.9 6.8 %collective-permute-start.2 = (bf16[136,128]{1,0:T(8,128)(2,1)S(1)}, bf16[136,128]{1,0:T(8,128)(2,1)S(1)}, u32[]{:S(2)}, u32[]{:S(2)}) collective-permute-start(bf16[136,128]{1,0:T(8,128)(2,1)S(1)} %get-tuple-element.41), channel_id=1, source_target_pairs={{0,64},{32,96},{64,0},{96,32},{1,65},{33,97},{65,1},{97,33},{2,66}... | collective-permute-start | bytes 104456 | tf_op jit(solution)/shard_map/ppermute | solution.py:401
  31.6 6.6 %collective-permute-start.3 = (bf16[136,128]{1,0:T(8,128)(2,1)S(1)}, bf16[136,128]{1,0:T(8,128)(2,1)S(1)}, u32[]{:S(2)}, u32[]{:S(2)}) collective-permute-start(bf16[136,128]{1,0:T(8,128)(2,1)S(1)} %get-tuple-element.42), channel_id=1, source_target_pairs={{0,96},{32,64},{64,32},{96,0},{1,97},{33,65},{65,33},{97,1},{2,98}... | collective-permute-start | bytes 104456 | tf_op jit(solution)/shard_map/ppermute | solution.py:401
  38.2 25.5 %collective-permute-start.5 = (bf16[8,136,128]{2,1,0:T(8,128)(2,1)S(1)}, bf16[8,136,128]{2,1,0:T(8,128)(2,1)S(1)}, u32[]{:S(2)}, u32[]{:S(2)}) collective-permute-start(bf16[8,136,128]{2,1,0:T(8,128)(2,1)S(1)} %all-to-all-done), channel_id=1, source_target_pairs={{0,256},{1,257},{2,258},{3,259},{4,260},{5,261},{6,262},{7,263},{8... | collective-permute-start | bytes 835592 | tf_op jit(solution)/shard_map/ppermute | solution.py:403
  63.6 23.4 %all-to-all-start.2 = ((bf16[16,136,128]{2,1,0:T(8,128)(2,1)}), bf16[16,136,128]{2,1,0:T(8,128)(2,1)S(1)}, u32[]{:S(2)}, u32[]{:S(2)}) async-start(bf16[16,136,128]{2,1,0:T(8,128)(2,1)} %bitcast.35), calls=%async_computation.2 | async-start | bytes 1114112 | tf_op jit(solution)/shard_map/all_to_all | solution.py:370
  68.5 11.2 %collective-permute-start.4 = (bf16[8,136,128]{2,1,0:T(8,128)(2,1)S(1)}, bf16[8,136,128]{2,1,0:T(8,128)(2,1)S(1)}, u32[]{:S(2)}, u32[]{:S(2)}) collective-permute-start(bf16[8,136,128]{2,1,0:T(8,128)(2,1)S(1)} %all-to-all-done), channel_id=1, source_target_pairs={{0,16},{16,0},{1,17},{17,1},{2,18},{18,2},{3,19},{19,3},{4,20},{20... | collective-permute-start | bytes 835592 | tf_op jit(solution)/shard_map/ppermute | solution.py:374
  77.5 3.5 %collective-permute-start.6 = (bf16[8,136,128]{2,1,0:T(8,128)(2,1)S(1)}, bf16[8,136,128]{2,1,0:T(8,128)(2,1)S(1)}, u32[]{:S(2)}, u32[]{:S(2)}) collective-permute-start(bf16[8,136,128]{2,1,0:T(8,128)(2,1)S(1)} %collective-permute-done.5), channel_id=1, source_target_pairs={{0,16},{16,0},{1,17},{17,1},{2,18},{18,2},{3,19},{19,3},{4,20},{20... | collective-permute-start | bytes 835592 | tf_op jit(solution)/shard_map/ppermute | solution.py:374
  87.1 7.7 %collective-permute-start.7 = (bf16[16,136,128]{2,1,0:T(8,128)(2,1)S(1)}, bf16[16,136,128]{2,1,0:T(8,128)(2,1)S(1)}, u32[]{:S(2)}, u32[]{:S(2)}) collective-permute-start(bf16[16,136,128]{2,1,0:T(8,128)(2,1)S(1)} %all-to-all-done.2), channel_id=1, source_target_pairs={{0,16},{16,0},{1,17},{17,1},{2,18},{18,2},{3,19},{19,3},{4,20},{20... | collective-permute-start | bytes 1671176 | tf_op jit(solution)/shard_map/ppermute | solution.py:374

commit v5 on v4

--- a/solution.py
+++ b/solution.py
@@ -183,12 +183,13 @@
     )(halo, partial, feat, res, edge, taps, long_taps)
 
 
-def pack_kernel(gf, hv, gs, keys, halo, keys_out, sems):
+def pack_kernel(gf, hv, gs, keys, queries, halo, blocks, sems):
     rows = gf.shape[0]
     pairs = []
-    for copy in range(keys_out.shape[0]):
-        for head in range(keys_out.shape[1]):
-            pairs.append((keys.at[:, head * HD : (head + 1) * HD], keys_out.at[copy, head]))
+    for copy in range(blocks.shape[0]):
+        for head in range(blocks.shape[1]):
+            for kind, source in enumerate((keys, queries)):
+                pairs.append((source.at[:, head * HD : (head + 1) * HD], blocks.at[copy, head, kind]))
     pairs += [
         (gf, halo.at[0:rows]),
         (hv, halo.at[rows : 2 * rows]),
@@ -201,24 +202,24 @@
         move.wait()
 
 
-def pack(gf, hv, gs, keys):
+def pack(gf, hv, gs, keys, queries):
     rows, chans = gf.shape
     heads = chans // HD
     vmem = pl.BlockSpec(memory_space=pltpu.VMEM)
     hbm = pl.BlockSpec(memory_space=pltpu.HBM)
     return pl.pallas_call(
         pack_kernel,
-        in_specs=[hbm] * 4,
+        in_specs=[hbm] * 5,
         out_specs=[vmem, vmem],
         out_shape=[
             jax.ShapeDtypeStruct((2 * rows + 8, chans), jnp.bfloat16),
-            jax.ShapeDtypeStruct((2, heads, rows, HD), jnp.bfloat16),
-        ],
-        scratch_shapes=[pltpu.SemaphoreType.DMA((2 * heads + 3,))],
+            jax.ShapeDtypeStruct((2, heads, 2, rows, HD), jnp.bfloat16),
+        ],
+        scratch_shapes=[pltpu.SemaphoreType.DMA((4 * heads + 3,))],
         compiler_params=pltpu.CompilerParams(vmem_limit_bytes=16 << 20),
         cost_estimate=pl.CostEstimate(flops=0, bytes_accessed=600_000, transcendentals=0),
         name="pack",
-    )(*in_hbm(gf, hv, gs, keys))
+    )(*in_hbm(gf, hv, gs, keys, queries))
 
 
 def normalize_kernel(width, gathered, stream, gain, packed):
@@ -255,115 +256,118 @@
     )(gathered, stream, gain)
 
 
-def score_kernel(place, q0, q1, q2, q3, k0, k1, k2, k3, out, denom, scores, weights, sems):
-    rows = q0.shape[0]
-    keys = k0.shape[0]
+def score_kernel(place, q, k0, k1, k2, k3, out, denom, keys, scores, weights, sems):
+    rows = keys.shape[1] // 16
+    count = keys.shape[1]
+    block = scores.shape[0]
     unit = math.log2(math.e) / math.sqrt(HD)
-    chunks = [(begin, min(256, keys - begin)) for begin in range(0, keys, 256)]
-    for index, query_ref in enumerate((q0, q1, q2, q3)):
-        query = query_ref[...]
-        query_pos = place[4 + index] + lax.broadcasted_iota(jnp.int32, (rows, 1), 0)
+    for part, ref in enumerate((k0, k1, k2, k3)):
+        begin = pl.multiple_of(place[6 + part // 2], 64)
+        keys[part % 2, pl.ds(begin, count // 2), :] = ref[...]
+    chunks = [(begin, min(256, count - begin)) for begin in range(0, count, 256)]
+    line = lax.broadcasted_iota(jnp.int32, (block, 1), 0)
+    for index in range(q.shape[0] // block):
+        query = q[index * block : (index + 1) * block, :]
+        query_pos = line + place[2 + index * (block // rows)]
+        for step in range(1, block // rows):
+            moved = place[2 + index * (block // rows) + step] - step * rows
+            query_pos = jnp.where(line >= step * rows, line + moved, query_pos)
         top = None
-        for part, ref in enumerate((k0, k1, k2, k3)):
+        for part in range(2):
             for begin, width in chunks:
                 score = lax.dot_general(
                     query,
-                    ref[begin : begin + width, :],
+                    keys[part, begin : begin + width, :],
                     (((1,), (1,)), ((), ())),
                     preferred_element_type=jnp.float32,
                 )
                 lane = begin + lax.broadcasted_iota(jnp.int32, (1, width), 1)
                 key_pos = place[part] + lane
-                for edge in range(rows, keys, rows):
+                for edge in range(rows, count, rows):
                     if edge < begin + width:
                         key_pos = key_pos + jnp.where(lane >= edge, rows, 0)
                 score = jnp.where(key_pos <= query_pos, score * unit, -1e30)
-                scores[:, part * keys + begin : part * keys + begin + width] = score
+                scores[:, part * count + begin : part * count + begin + width] = score
                 for piece in range(0, width, 128):
-                    piece = score[:, piece : min(piece + 128, width)]
-                    if piece.shape[1] < 128:
-                        piece = jnp.concatenate(
-                            [piece, jnp.full((rows, 128 - piece.shape[1]), -1e30, jnp.float32)], axis=1
-                        )
+                    piece = score[:, piece : piece + 128]
                     top = piece if top is None else jnp.maximum(top, piece)
         top = jnp.max(top, axis=1, keepdims=True)
-        total = jnp.zeros((rows, 128), jnp.float32)
-        for begin in range(0, 4 * keys, 128):
+        total = jnp.zeros((block, 128), jnp.float32)
+        for begin in range(0, 2 * count, 128):
             expo = jnp.exp2(scores[:, begin : begin + 128] - top)
             total = total + expo
-            weights[index, :, begin : begin + 128] = expo.astype(jnp.bfloat16)
+            weights[index * block : (index + 1) * block, begin : begin + 128] = expo.astype(jnp.bfloat16)
         total = jnp.sum(total, axis=1, keepdims=True)
-        denom[index] = jnp.broadcast_to(total, (rows, 128))
-        pltpu.make_async_copy(weights.at[index], out.at[index], sems.at[index]).start()
-    for index in range(4):
-        pltpu.make_async_copy(weights.at[index], out.at[index], sems.at[index]).wait()
-
-
-def score(place, queries, keys):
-    rows = queries[0].shape[0]
-    blocks = len(queries)
+        denom[index * block : (index + 1) * block, :] = jnp.broadcast_to(total, (block, 128))
+        lines = pl.ds(index * block, block)
+        pltpu.make_async_copy(weights.at[lines], out.at[lines], sems.at[index]).start()
+    for index in range(q.shape[0] // block):
+        lines = pl.ds(index * block, block)
+        pltpu.make_async_copy(weights.at[lines], out.at[lines], sems.at[index]).wait()
+
+
+def score(place, q, keys):
+    lines = q.shape[0]
     count = sum(part.shape[0] for part in keys)
+    block = lines // 2
     vmem = pl.BlockSpec(memory_space=pltpu.VMEM)
     return pl.pallas_call(
         score_kernel,
-        in_specs=[pl.BlockSpec(memory_space=pltpu.SMEM)] + [vmem] * 8,
+        in_specs=[pl.BlockSpec(memory_space=pltpu.SMEM)] + [vmem] * 5,
         out_specs=[pl.BlockSpec(memory_space=pltpu.HBM), vmem],
         out_shape=[
-            pltpu.HBM((blocks, rows, count), jnp.bfloat16),
-            jax.ShapeDtypeStruct((blocks, rows, 128), jnp.float32),
+            pltpu.HBM((lines, count), jnp.bfloat16),
+            jax.ShapeDtypeStruct((lines, 128), jnp.float32),
         ],
         scratch_shapes=[
-            pltpu.VMEM((rows, count), jnp.float32),
-            pltpu.VMEM((blocks, rows, count), jnp.bfloat16),
-            pltpu.SemaphoreType.DMA((blocks,)),
+            pltpu.VMEM((2, count // 2, HD), jnp.bfloat16),
+            pltpu.VMEM((block, count), jnp.float32),
+            pltpu.VMEM((lines, count), jnp.bfloat16),
+            pltpu.SemaphoreType.DMA((2,)),
         ],
         compiler_params=pltpu.CompilerParams(vmem_limit_bytes=32 << 20),
         cost_estimate=pl.CostEstimate(
-            flops=2 * blocks * rows * count * HD,
-            bytes_accessed=8_000_000,
-            transcendentals=blocks * rows * count,
+            flops=2 * lines * count * HD, bytes_accessed=8_000_000, transcendentals=lines * count
         ),
         name="score",
-    )(place, *queries, *keys)
-
-
-def attend_kernel(place, weights_in, denom, v_own, v_other, out, weights, sems):
-    blocks, rows, _ = out.shape
-    half = v_own.shape[0] // 2
-    moves = [
-        pltpu.make_async_copy(weights_in.at[index], weights.at[index], sems.at[index]) for index in range(blocks)
-    ]
+    )(place, q, *keys)
+
+
+def attend_kernel(weights_in, denom, v_own, v_other, out, weights, sems):
+    keys = v_own.shape[0]
+    cuts = [0, 1152, keys, keys + 1152, 2 * keys]
+    moves = []
+    for index, (begin, end) in enumerate(zip(cuts, cuts[1:])):
+        moves.append(
+            pltpu.make_async_copy(weights_in.at[:, begin:end], weights.at[:, begin:end], sems.at[index])
+        )
     for move in moves:
         move.start()
-    for index, move in enumerate(moves):
+    total = jnp.zeros(out.shape, jnp.float32)
+    for move, begin, end in zip(moves, cuts, cuts[1:]):
         move.wait()
-        total = jnp.zeros((rows, HD), jnp.float32)
-        for part in range(4):
-            begin = pl.multiple_of(place[12 + part // 2] * half, 16)
-            ref = v_other if part % 2 else v_own
-            total = total + jnp.dot(
-                weights[index, :, part * half : (part + 1) * half],
-                ref[pl.ds(begin, half), :],
-                preferred_element_type=jnp.float32,
-            )
-        out[place[8 + index]] = (total / denom[index]).astype(jnp.bfloat16)
-
-
-def attend(place, weights, denom, v_own, v_other):
-    blocks, rows, keys = weights.shape
+        ref, first = (v_own, begin) if begin < keys else (v_other, begin - keys)
+        total = total + jnp.dot(
+            weights[:, begin:end], ref[first : first + end - begin, :], preferred_element_type=jnp.float32
+        )
+    out[...] = (total / denom[...]).astype(jnp.bfloat16)
+
+
+def attend(weights, denom, v_own, v_other):
+    lines, count = weights.shape
     vmem = pl.BlockSpec(memory_space=pltpu.VMEM)
     return pl.pallas_call(
         attend_kernel,
-        in_specs=[pl.BlockSpec(memory_space=pltpu.SMEM), pl.BlockSpec(memory_space=pltpu.HBM), vmem, vmem, vmem],
+        in_specs=[pl.BlockSpec(memory_space=pltpu.HBM), vmem, vmem, vmem],
         out_specs=vmem,
-        out_shape=jax.ShapeDtypeStruct((blocks, rows, HD), jnp.bfloat16),
-        scratch_shapes=[pltpu.VMEM((blocks, rows, keys), jnp.bfloat16), pltpu.SemaphoreType.DMA((blocks,))],
+        out_shape=jax.ShapeDtypeStruct((lines, HD), jnp.bfloat16),
+        scratch_shapes=[pltpu.VMEM((lines, count), jnp.bfloat16), pltpu.SemaphoreType.DMA((4,))],
         compiler_params=pltpu.CompilerParams(vmem_limit_bytes=16 << 20),
         cost_estimate=pl.CostEstimate(
-            flops=2 * blocks * rows * keys * HD, bytes_accessed=7_000_000, transcendentals=0
+            flops=2 * lines * count * HD, bytes_accessed=7_000_000, transcendentals=0
         ),
         name="attend",
-    )(place, *in_hbm(weights), denom, v_own, v_other)
+    )(*in_hbm(weights), denom, v_own, v_other)
 
 
 def exchange(value, axes):
@@ -381,25 +385,20 @@
     width = chans * 16
 
     core = lax.axis_index("c")
-    head = lax.axis_index("h")
     side = lax.axis_index("zh")
     group = side * 16 + lax.axis_index("s") * 8 + core
-    owners = [head ^ flip for flip in range(heads)]
-    place = [side * 16 + core, side * 16 + 1 - core, (1 - side) * 16 + core, (1 - side) * 16 + 1 - core]
-    place = place + [group + owner * 2 for owner in owners]
-    place = jnp.concatenate([jnp.stack(place) * rows, jnp.stack(owners + [side, 1 - side])]).astype(jnp.int32)
-
-    last, keys_by_head = pack(gate_first, hyena_value, gate_second, attn_keys)
-    keys_near = exchange(keys_by_head.reshape(8, rows, HD), ("s", "h"))
+    place = [core, 1 - core] + [group + owner * 2 for owner in range(heads)]
+    place = (jnp.stack(place + [side * 8, (1 - side) * 8]) * rows).astype(jnp.int32)
+
+    last, blocks = pack(gate_first, hyena_value, gate_second, attn_keys, queries)
+    blocks = exchange(blocks.reshape(8, 2, rows, HD), ("s", "h"))
     halo = lax.ppermute(last, ROWS_AXES, [(source, source + 1) for source in range(count - 1)])
     early_parts = early(last, gate_second, residual, short_taps, long_taps)
     stream, squares = late(halo, *early_parts)
 
-    blocks = [lax.dynamic_slice_in_dim(queries, owner * HD, HD, 1) for owner in owners]
     blocks, squares = lax.optimization_barrier((blocks, squares))
-    for flip in range(1, heads):
-        blocks[flip] = lax.ppermute(blocks[flip], "h", [(source, source ^ flip) for source in range(heads)])
-    keys_near, blocks, squares = lax.optimization_barrier((keys_near, blocks, squares))
+    keys_near = blocks[:, 0]
+    my_queries = lax.dynamic_slice_in_dim(blocks, lax.axis_index("s") * heads, heads, 0)[:, 1]
     keys_far = lax.ppermute(keys_near, "zh", [(0, 1)])
     gathered = exchange(squares, CHAN_AXES)
     packed = normalize(width, gathered, stream, norm_gain.reshape(1, chans))
@@ -407,13 +406,15 @@
     values_own = exchange(packed.reshape(16, rows, HD), PEERS)
 
     parts = [keys_near, swap_cores(keys_near), keys_far, swap_cores(keys_far)]
-    weights, denom = score(place, blocks, [part.reshape(8 * rows, HD) for part in parts])
+    weights, denom = score(
+        place, my_queries.reshape(heads * rows, HD), [part.reshape(8 * rows, HD) for part in parts]
+    )
     values_own, denom = lax.optimization_barrier((values_own, denom))
     values_other = swap_cores(values_own)
     result = attend(
-        place, weights, denom, values_own.reshape(16 * rows, HD), values_other.reshape(16 * rows, HD)
+        weights, denom, values_own.reshape(16 * rows, HD), values_other.reshape(16 * rows, HD)
     )
-    attended = exchange(result, "h").transpose(1, 0, 2).reshape(rows, chans)
+    attended = exchange(result.reshape(heads, rows, HD), "h").transpose(1, 0, 2).reshape(rows, chans)
     return stream, attended
 
 

time: 108 us -> 103 us (0.954)
  starting transfers between devices: 54.6 us -> 44.8 us
  waiting for transfers between devices: 9.19 us -> 12.4 us
  blocking collectives: 21.9 us -> 23.4 us
    ppermute x3 -> x0, starting transfers between devices: 9.26 us -> none  [shards(): lax.ppermute(blocks[flip], 'h', [(source, source ^ flip) for source in ra...]
    ppermute x3, starting transfers between devices: 17.1 us -> 12.5 us  [swap_cores(): return lax.ppermute(value, 'c', [(0, 1), (1, 0)])]
    ppermute x3 -> x0, waiting for transfers between devices: 4.53 us -> none  [shards(): lax.ppermute(blocks[flip], 'h', [(source, source ^ flip) for source in ra...]
    ppermute x1, waiting for transfers between devices: 1.78 us -> 6.05 us  [shards(): lax.ppermute(last, ROWS_AXES, [(source, source + 1) for source in range(c...]
    all_to_all x2, waiting for transfers between devices: 0.01 us -> 3.26 us  [exchange(): return lax.all_to_all(value, axes, 0, 0, tiled=True)]
    all_to_all x2, starting transfers between devices: 12.5 us -> 14.9 us  [exchange(): return lax.all_to_all(value, axes, 0, 0, tiled=True)]
    ppermute x1, starting transfers between devices: 9.6 us -> 11.2 us  [shards(): keys_far = lax.ppermute(keys_near, 'zh', [(0, 1)])]
    all_to_all x2, blocking collectives: 21.9 us -> 23.4 us  [exchange(): return lax.all_to_all(value, axes, 0, 0, tiled=True)]
  transfers between devices with their start and end apart: 10 -> 7, of which waited for: 4 -> 4; matrix products, arithmetic and copies ran while one was open for 0% -> 0% of each run, Pallas kernels for 13% -> 13%
where the time goes in v5:
time: 103 us; the launch traced here: 102 us
  starting transfers between devices  44.8 us (43%)
  blocking collectives  23.4 us (23%)
  Pallas kernels  20.2 us (20%)
  waiting for transfers between devices  12.4 us (12%)
    all_to_all x2, blocking collectives, exchange(): return lax.all_to_all(value, axes, 0, 0, tiled=True)  23.4 us
    all_to_all x2, starting transfers between devices, exchange(): return lax.all_to_all(value, axes, 0, 0, tiled=True)  14.9 us
    ppermute x3, starting transfers between devices, swap_cores(): return lax.ppermute(value, 'c', [(0, 1), (1, 0)])  12.5 us
    ppermute x1, starting transfers between devices, shards(): keys_far = lax.ppermute(keys_near, 'zh', [(0, 1)])  11.2 us
    ppermute x1, starting transfers between devices, shards(): lax.ppermute(last, ROWS_AXES, [(source, source + 1) for source in range(c...  6.19 us
    ppermute x1, waiting for transfers between devices, shards(): lax.ppermute(last, ROWS_AXES, [(source, source + 1) for source in range(c...  6.05 us
    pallas_call x1, Pallas kernels, score(): pl.pallas_call(score_kernel, in_specs=[pl.BlockSpec(memory_space=pltpu.SM...  5.38 us
    pallas_call x1, Pallas kernels, attend(): pl.pallas_call(attend_kernel, in_specs=[pl.BlockSpec(memory_space=pltpu.H...  4.42 us
  transfers between devices with their start and end apart: 7, of which 4 were waited for; matrix products, arithmetic and copies ran while one was open for 0% of the time, Pallas kernels for 13%

profile of v5, /device:TPU:1, one launch (start us, length us, event | category | flops | bytes accessed | tf_op | source)
XLA Modules:
  0.0 102.3 jit_solution(11492036067763769094)
XLA Ops:
  0.6 2.2 %pack.1 = (bf16[280,512]{1,0:T(8,128)(2,1)S(1)}, bf16[2,4,2,136,128]{4,3,2,1,0:T(8,128)(2,1)}) custom-call(bf16[136,512]{1,0:T(8,128)(2,1)} %gf.1, bf16[136,512]{1,0:T(8,128)(2,1)} %hv.1, bf16[136,512]{1,0:T(8,128)(2,1)} %gs.3, bf16[136,512]{1,0:T(8,128)(2,1)} %keys.1, bf16[136,512]{1,0:T(8,128)(2,1)} %queries.1), custom_call_target="tpu_custom_call" | custom-call | bytes 600000 | tf_op jit(solution)/shard_map/pack/pallas_call | solution.py:210
  2.9 7.7 %all-to-all-start = ((bf16[8,2,136,128]{3,2,1,0:T(8,128)(2,1)}), bf16[8,2,136,128]{3,2,1,0:T(8,128)(2,1)S(1)}, u32[]{:S(2)}, u32[]{:S(2)}) async-start(bf16[8,2,136,128]{3,2,1,0:T(8,128)(2,1)} %bitcast.8), calls=%async_computation | async-start | bytes 1114112 | tf_op jit(solution)/shard_map/all_to_all | solution.py:374
  10.5 6.2 %collective-permute-start = (bf16[280,512]{1,0:T(8,128)(2,1)S(1)}, bf16[280,512]{1,0:T(8,128)(2,1)S(1)}, u32[]{:S(2)}, u32[]{:S(2)}) collective-permute-start(bf16[280,512]{1,0:T(8,128)(2,1)S(1)} %get-tuple-element.20.packed), channel_id=1, source_target_pairs={{0,16},{16,32},{32,48},{48,64},{64,80},{80,96},{96,112},{112,128},... | collective-permute-start | bytes 860168 | tf_op jit(solution)/shard_map/ppermute | solution.py:395
  16.7 2.8 %early.1 = (f32[136,512]{1,0:T(8,128)S(1)}, f32[136,512]{1,0:T(8,128)S(1)}, bf16[136,512]{1,0:T(8,128)(2,1)S(1)}, f32[3,8,512]{2,1,0:T(8,128)S(1)}, f32[3,3,512]...) custom-call(bf16[280,512]{1,0:T(8,128)(2,1)S(1)} %get-tuple-element.20.packed, bf16[136,512]{1,0:T(8,128)(2,1)} %gs.3, ...), custom_call_target="tpu_custom_call" | custom-call | flops 6000000000 | bytes 2000000 | tf_op jit(solution)/shard_map/early/pallas_call | solution.py:95
  19.5 6.1 %collective-permute-done.halo = bf16[280,512]{1,0:T(8,128)(2,1)S(1)} collective-permute-done((bf16[280,512]{1,0:T(8,128)(2,1)S(1)}, bf16[280,512]{1,0:T(8,128)(2,1)S(1)}, u32[]{:S(2)}, u32[]{:S(2)}) %collective-permute-start) | collective-permute-done | bytes 286752 | tf_op jit(solution)/shard_map/ppermute | solution.py:395
  25.6 3.3 %late.1 = (bf16[136,512]{1,0:T(8,128)(2,1)}, f32[16,1,136]{2,1,0:T(1,128)S(1)}) custom-call(bf16[280,512]{1,0:T(8,128)(2,1)S(1)} %collective-permute-done.halo, f32[136,512]{1,0:T(8,128)S(1)} %get-tuple-element.21.partial, f32[136,512]{1,0:T(8,128)S(1)} %get-tuple-element.22.feat, bf16[136,512]{1,0:T(8,128)(2,1)S(1)} %get-tuple-element.23.res, ...), custom_call_target="tpu_custom_call" | custom-call | flops 30000001024 | bytes 2000000 | tf_op jit(solution)/shard_map/late/pallas_call | solution.py:167
  28.8 0.0 all-to-all-done
  28.8 0.1 slice_bitcast_fusion
  28.9 11.2 %collective-permute-start.2 = (bf16[8,136,128]{2,1,0:T(8,128)(2,1)S(1)}, bf16[8,136,128]{2,1,0:T(8,128)(2,1)S(1)}, u32[]{:S(2)}, u32[]{:S(2)}) collective-permute-start(bf16[8,136,128]{2,1,0:T(8,128)(2,1)S(1)} %get-tuple-element.38), channel_id=1, source_target_pairs={{0,256},{1,257},{2,258},{3,259},{4,260},{5,261},{6,262},{7,263},{8... | collective-permute-start | bytes 835592 | tf_op jit(solution)/shard_map/ppermute | solution.py:402
  40.1 14.7 %all_to_all.20.gathered = f32[16,1,136]{2,1,0:T(1,128)} all-to-all(f32[16,1,136]{2,1,0:T(1,128)S(1)} %get-tuple-element.31), channel_id=1, replica_groups=mesh['zh'=2,'s'=2,'h'=4,'c'=2,'x'=4,'zl'=4] {'x','zl'}, dimensions={0} | all-to-all | bytes 17408 | tf_op jit(solution)/shard_map/all_to_all | solution.py:374
  54.9 2.1 %normalize.1 = bf16[4,4,136,128]{3,2,1,0:T(8,128)(2,1)} custom-call(f32[16,1,136]{2,1,0:T(1,128)} %all_to_all.20.gathered, bf16[136,512]{1,0:T(8,128)(2,1)} %get-tuple-element.18.stream, f32[1,512]{1,0:T(1,128)} %bitcast.36), custom_call_target="tpu_custom_call" | custom-call | flops 1000000 | bytes 800000 | tf_op jit(solution)/shard_map/normalize/pallas_call | solution.py:249
  57.0 0.0 collective-permute-done.2
  57.0 7.2 %all-to-all-start.2 = ((bf16[16,136,128]{2,1,0:T(8,128)(2,1)}), bf16[16,136,128]{2,1,0:T(8,128)(2,1)S(1)}, u32[]{:S(2)}, u32[]{:S(2)}) async-start(bf16[16,136,128]{2,1,0:T(8,128)(2,1)} %bitcast.35), calls=%async_computation.2 | async-start | bytes 1114112 | tf_op jit(solution)/shard_map/all_to_all | solution.py:374
  64.2 0.1 stack.35
  64.3 4.6 %collective-permute-start.1 = (bf16[8,136,128]{2,1,0:T(8,128)(2,1)S(1)}, bf16[8,136,128]{2,1,0:T(8,128)(2,1)S(1)}, u32[]{:S(2)}, u32[]{:S(2)}) collective-permute-start(bf16[8,136,128]{2,1,0:T(8,128)(2,1)S(1)} %get-tuple-element.38), channel_id=1, source_target_pairs={{0,16},{16,0},{1,17},{17,1},{2,18},{18,2},{3,19},{19,3},{4,20},{20... | collective-permute-start | bytes 835592 | tf_op jit(solution)/shard_map/ppermute | solution.py:378
  69.0 1.9 %collective-permute-start.3 = (bf16[8,136,128]{2,1,0:T(8,128)(2,1)S(1)}, bf16[8,136,128]{2,1,0:T(8,128)(2,1)S(1)}, u32[]{:S(2)}, u32[]{:S(2)}) collective-permute-start(bf16[8,136,128]{2,1,0:T(8,128)(2,1)S(1)} %collective-permute-done.2), channel_id=1, source_target_pairs={{0,16},{16,0},{1,17},{17,1},{2,18},{18,2},{3,19},{19,3},{4,20},{20... | collective-permute-start | bytes 835592 | tf_op jit(solution)/shard_map/ppermute | solution.py:378
  70.9 1.5 %collective-permute-done.3 = bf16[8,136,128]{2,1,0:T(8,128)(2,1)S(1)} collective-permute-done((bf16[8,136,128]{2,1,0:T(8,128)(2,1)S(1)}, bf16[8,136,128]{2,1,0:T(8,128)(2,1)S(1)}, u32[]{:S(2)}, u32[]{:S(2)}) %collective-permute-start.3) | collective-permute-done | bytes 278560 | tf_op jit(solution)/shard_map/ppermute | solution.py:378
  72.4 5.4 %score.1 = (bf16[544,4352]{1,0:T(8,128)(2,1)}, f32[544,128]{1,0:T(8,128)S(1)}) custom-call(s32[8]{0:T(128)S(1)} %broadcast_multiply_fusion.place, bf16[544,128]{1,0:T(8,128)(2,1)S(1)} %bitcast.31, bf16[1088,128]{1,0:T(8,128)(2,1)S(1)} %bitcast.30, bf16[1088,128]{1,0:T(8,128)(2,1)S(1)} %bitcast.33, bf16[1088,128]{1,0:T(8,128)(2,1)S(1)} %bitcast.32, ...), custom_call_target="tpu_custom_call" | custom-call | flops 606076928 | bytes 8000000 | tf_op jit(solution)/shard_map/score/pallas_call | solution.py:314
  77.8 3.3 %all-to-all-done.2 = bf16[16,136,128]{2,1,0:T(8,128)(2,1)S(1)} async-done(((bf16[16,136,128]{2,1,0:T(8,128)(2,1)}), bf16[16,136,128]{2,1,0:T(8,128)(2,1)S(1)}, u32[]{:S(2)}, u32[]{:S(2)}) %all-to-all-start.2) | async-done | bytes 557088 | tf_op jit(solution)/shard_map/all_to_all | solution.py:374
  81.1 6.0 %collective-permute-start.4 = (bf16[16,136,128]{2,1,0:T(8,128)(2,1)S(1)}, bf16[16,136,128]{2,1,0:T(8,128)(2,1)S(1)}, u32[]{:S(2)}, u32[]{:S(2)}) collective-permute-start(bf16[16,136,128]{2,1,0:T(8,128)(2,1)S(1)} %all-to-all-done.2), channel_id=1, source_target_pairs={{0,16},{16,0},{1,17},{17,1},{2,18},{18,2},{3,19},{19,3},{4,20},{20... | collective-permute-start | bytes 1671176 | tf_op jit(solution)/shard_map/ppermute | solution.py:378
  87.0 1.6 %collective-permute-done.4 = bf16[16,136,128]{2,1,0:T(8,128)(2,1)S(1)} collective-permute-done((bf16[16,136,128]{2,1,0:T(8,128)(2,1)S(1)}, bf16[16,136,128]{2,1,0:T(8,128)(2,1)S(1)}, u32[]{:S(2)}, u32[]{:S(2)}) %collective-permute-start.4) | collective-permute-done | bytes 557088 | tf_op jit(solution)/shard_map/ppermute | solution.py:378
  88.6 4.4 %attend.1 = bf16[544,128]{1,0:T(8,128)(2,1)S(1)} custom-call(bf16[544,4352]{1,0:T(8,128)(2,1)} %get-tuple-element.33.weights_in, f32[544,128]{1,0:T(8,128)S(1)} %get-tuple-element.36.denom, bf16[2176,128]{1,0:T(8,128)(2,1)S(1)} %bitcast.27, bf16[2176,128]{1,0:T(8,128)(2,1)S(1)} %bitcast.28), custom_call_target="tpu_custom_call" | custom-call | flops 606076928 | bytes 7000000 | tf_op jit(solution)/shard_map/attend/pallas_call | solution.py:359
  93.0 8.6 %all_to_all.21 = bf16[4,136,128]{2,1,0:T(8,128)(2,1)S(1)} all-to-all(bf16[4,136,128]{2,1,0:T(8,128)(2,1)S(1)} %bitcast.29), channel_id=1, replica_groups=mesh['zh'=2,'s'=2,'h'=4,'c'=2,'x'=4,'zl'=4] {'h'}, dimensions={0} | all-to-all | bytes 278528 | tf_op jit(solution)/shard_map/all_to_all | solution.py:374
  101.6 0.7 copy_bitcast_fusion
  (3 shorter events, 0.0 us)
Async XLA Ops:
  2.9 26.0 %all-to-all-start = ((bf16[8,2,136,128]{3,2,1,0:T(8,128)(2,1)}), bf16[8,2,136,128]{3,2,1,0:T(8,128)(2,1)S(1)}, u32[]{:S(2)}, u32[]{:S(2)}) async-start(bf16[8,2,136,128]{3,2,1,0:T(8,128)(2,1)} %bitcast.8), calls=%async_computation | async-start | bytes 1114112 | tf_op jit(solution)/shard_map/all_to_all | solution.py:374
  10.5 15.0 %collective-permute-start = (bf16[280,512]{1,0:T(8,128)(2,1)S(1)}, bf16[280,512]{1,0:T(8,128)(2,1)S(1)}, u32[]{:S(2)}, u32[]{:S(2)}) collective-permute-start(bf16[280,512]{1,0:T(8,128)(2,1)S(1)} %get-tuple-element.20.packed), channel_id=1, source_target_pairs={{0,16},{16,32},{32,48},{48,64},{64,80},{80,96},{96,112},{112,128},... | collective-permute-start | bytes 860168 | tf_op jit(solution)/shard_map/ppermute | solution.py:395
  28.9 28.1 %collective-permute-start.2 = (bf16[8,136,128]{2,1,0:T(8,128)(2,1)S(1)}, bf16[8,136,128]{2,1,0:T(8,128)(2,1)S(1)}, u32[]{:S(2)}, u32[]{:S(2)}) collective-permute-start(bf16[8,136,128]{2,1,0:T(8,128)(2,1)S(1)} %get-tuple-element.38), channel_id=1, source_target_pairs={{0,256},{1,257},{2,258},{3,259},{4,260},{5,261},{6,262},{7,263},{8... | collective-permute-start | bytes 835592 | tf_op jit(solution)/shard_map/ppermute | solution.py:402
  57.0 24.1 %all-to-all-start.2 = ((bf16[16,136,128]{2,1,0:T(8,128)(2,1)}), bf16[16,136,128]{2,1,0:T(8,128)(2,1)S(1)}, u32[]{:S(2)}, u32[]{:S(2)}) async-start(bf16[16,136,128]{2,1,0:T(8,128)(2,1)} %bitcast.35), calls=%async_computation.2 | async-start | bytes 1114112 | tf_op jit(solution)/shard_map/all_to_all | solution.py:374
  64.3 6.6 %collective-permute-start.1 = (bf16[8,136,128]{2,1,0:T(8,128)(2,1)S(1)}, bf16[8,136,128]{2,1,0:T(8,128)(2,1)S(1)}, u32[]{:S(2)}, u32[]{:S(2)}) collective-permute-start(bf16[8,136,128]{2,1,0:T(8,128)(2,1)S(1)} %get-tuple-element.38), channel_id=1, source_target_pairs={{0,16},{16,0},{1,17},{17,1},{2,18},{18,2},{3,19},{19,3},{4,20},{20... | collective-permute-start | bytes 835592 | tf_op jit(solution)/shard_map/ppermute | solution.py:378
  69.0 3.5 %collective-permute-start.3 = (bf16[8,136,128]{2,1,0:T(8,128)(2,1)S(1)}, bf16[8,136,128]{2,1,0:T(8,128)(2,1)S(1)}, u32[]{:S(2)}, u32[]{:S(2)}) collective-permute-start(bf16[8,136,128]{2,1,0:T(8,128)(2,1)S(1)} %collective-permute-done.2), channel_id=1, source_target_pairs={{0,16},{16,0},{1,17},{17,1},{2,18},{18,2},{3,19},{19,3},{4,20},{20... | collective-permute-start | bytes 835592 | tf_op jit(solution)/shard_map/ppermute | solution.py:378
  81.1 7.5 %collective-permute-start.4 = (bf16[16,136,128]{2,1,0:T(8,128)(2,1)S(1)}, bf16[16,136,128]{2,1,0:T(8,128)(2,1)S(1)}, u32[]{:S(2)}, u32[]{:S(2)}) collective-permute-start(bf16[16,136,128]{2,1,0:T(8,128)(2,1)S(1)} %all-to-all-done.2), channel_id=1, source_target_pairs={{0,16},{16,0},{1,17},{17,1},{2,18},{18,2},{3,19},{19,3},{4,20},{20... | collective-permute-start | bytes 1671176 | tf_op jit(solution)/shard_map/ppermute | solution.py:378

commit v6 on v5

--- a/solution.py
+++ b/solution.py
@@ -183,13 +183,12 @@
     )(halo, partial, feat, res, edge, taps, long_taps)
 
 
-def pack_kernel(gf, hv, gs, keys, queries, halo, blocks, sems):
+def pack_kernel(gf, hv, gs, keys, halo, blocks, sems):
     rows = gf.shape[0]
     pairs = []
     for copy in range(blocks.shape[0]):
         for head in range(blocks.shape[1]):
-            for kind, source in enumerate((keys, queries)):
-                pairs.append((source.at[:, head * HD : (head + 1) * HD], blocks.at[copy, head, kind]))
+            pairs.append((keys.at[:, head * HD : (head + 1) * HD], blocks.at[copy, head]))
     pairs += [
         (gf, halo.at[0:rows]),
         (hv, halo.at[rows : 2 * rows]),
@@ -202,24 +201,24 @@
         move.wait()
 
 
-def pack(gf, hv, gs, keys, queries):
+def pack(gf, hv, gs, keys):
     rows, chans = gf.shape
     heads = chans // HD
     vmem = pl.BlockSpec(memory_space=pltpu.VMEM)
     hbm = pl.BlockSpec(memory_space=pltpu.HBM)
     return pl.pallas_call(
         pack_kernel,
-        in_specs=[hbm] * 5,
+        in_specs=[hbm] * 4,
         out_specs=[vmem, vmem],
         out_shape=[
             jax.ShapeDtypeStruct((2 * rows + 8, chans), jnp.bfloat16),
-            jax.ShapeDtypeStruct((2, heads, 2, rows, HD), jnp.bfloat16),
-        ],
-        scratch_shapes=[pltpu.SemaphoreType.DMA((4 * heads + 3,))],
+            jax.ShapeDtypeStruct((2, heads, rows, HD), jnp.bfloat16),
+        ],
+        scratch_shapes=[pltpu.SemaphoreType.DMA((2 * heads + 3,))],
         compiler_params=pltpu.CompilerParams(vmem_limit_bytes=16 << 20),
         cost_estimate=pl.CostEstimate(flops=0, bytes_accessed=600_000, transcendentals=0),
         name="pack",
-    )(*in_hbm(gf, hv, gs, keys, queries))
+    )(*in_hbm(gf, hv, gs, keys))
 
 
 def normalize_kernel(width, gathered, stream, gain, packed):
@@ -251,12 +250,13 @@
         in_specs=[vmem] * 3,
         out_specs=vmem,
         out_shape=jax.ShapeDtypeStruct((4, chans // HD, rows, HD), jnp.bfloat16),
+        compiler_params=pltpu.CompilerParams(vmem_limit_bytes=8 << 20),
         cost_estimate=pl.CostEstimate(flops=1_000_000, bytes_accessed=800_000, transcendentals=20_000),
         name="normalize",
-    )(gathered, stream, gain)
-
-
-def score_kernel(place, q, k0, k1, k2, k3, out, denom, keys, scores, weights, sems):
+    )(gathered, *in_hbm(stream), gain)
+
+
+def score_kernel(place, q0, q1, q2, q3, k0, k1, k2, k3, out, denom, q, keys, scores, weights, sems):
     rows = keys.shape[1] // 16
     count = keys.shape[1]
     block = scores.shape[0]
@@ -264,10 +264,13 @@
     for part, ref in enumerate((k0, k1, k2, k3)):
         begin = pl.multiple_of(place[6 + part // 2], 64)
         keys[part % 2, pl.ds(begin, count // 2), :] = ref[...]
+    for flip, ref in enumerate((q0, q1, q2, q3)):
+        begin = pl.multiple_of(place[8 + flip], 8)
+        q[pl.ds(begin, rows), :] = ref[...].astype(jnp.float32)
     chunks = [(begin, min(256, count - begin)) for begin in range(0, count, 256)]
     line = lax.broadcasted_iota(jnp.int32, (block, 1), 0)
     for index in range(q.shape[0] // block):
-        query = q[index * block : (index + 1) * block, :]
+        query = q[index * block : (index + 1) * block, :].astype(jnp.bfloat16)
         query_pos = line + place[2 + index * (block // rows)]
         for step in range(1, block // rows):
             moved = place[2 + index * (block // rows) + step] - step * rows
@@ -306,20 +309,21 @@
         pltpu.make_async_copy(weights.at[lines], out.at[lines], sems.at[index]).wait()
 
 
-def score(place, q, keys):
-    lines = q.shape[0]
+def score(place, queries, keys):
+    lines = sum(part.shape[0] for part in queries)
     count = sum(part.shape[0] for part in keys)
     block = lines // 2
     vmem = pl.BlockSpec(memory_space=pltpu.VMEM)
     return pl.pallas_call(
         score_kernel,
-        in_specs=[pl.BlockSpec(memory_space=pltpu.SMEM)] + [vmem] * 5,
+        in_specs=[pl.BlockSpec(memory_space=pltpu.SMEM)] + [vmem] * 8,
         out_specs=[pl.BlockSpec(memory_space=pltpu.HBM), vmem],
         out_shape=[
             pltpu.HBM((lines, count), jnp.bfloat16),
             jax.ShapeDtypeStruct((lines, 128), jnp.float32),
         ],
         scratch_shapes=[
+            pltpu.VMEM((lines, HD), jnp.float32),
             pltpu.VMEM((2, count // 2, HD), jnp.bfloat16),
             pltpu.VMEM((block, count), jnp.float32),
             pltpu.VMEM((lines, count), jnp.bfloat16),
@@ -330,44 +334,49 @@
             flops=2 * lines * count * HD, bytes_accessed=8_000_000, transcendentals=lines * count
         ),
         name="score",
-    )(place, q, *keys)
-
-
-def attend_kernel(weights_in, denom, v_own, v_other, out, weights, sems):
-    keys = v_own.shape[0]
-    cuts = [0, 1152, keys, keys + 1152, 2 * keys]
+    )(place, *queries, *keys)
+
+
+def attend_kernel(half, weights_in, *refs):
+    if half:
+        denom, before, values, out, weights, sems = refs
+    else:
+        values, out, weights, sems = refs
+    keys = values.shape[0]
+    cuts = [0] + list(range(keys % 512 + 512, keys + 1, 512))
     moves = []
     for index, (begin, end) in enumerate(zip(cuts, cuts[1:])):
-        moves.append(
-            pltpu.make_async_copy(weights_in.at[:, begin:end], weights.at[:, begin:end], sems.at[index])
+        src = weights_in.at[:, half * keys + begin : half * keys + end]
+        moves.append(pltpu.make_async_copy(src, weights.at[:, begin:end], sems.at[index]))
+    moves[0].start()
+    moves[1].start()
+    total = before[...] if half else jnp.zeros(out.shape, jnp.float32)
+    for index, (begin, end) in enumerate(zip(cuts, cuts[1:])):
+        moves[index].wait()
+        if index + 2 < len(moves):
+            moves[index + 2].start()
+        total = total + jnp.dot(
+            weights[:, begin:end], values[begin:end, :], preferred_element_type=jnp.float32
         )
-    for move in moves:
-        move.start()
-    total = jnp.zeros(out.shape, jnp.float32)
-    for move, begin, end in zip(moves, cuts, cuts[1:]):
-        move.wait()
-        ref, first = (v_own, begin) if begin < keys else (v_other, begin - keys)
-        total = total + jnp.dot(
-            weights[:, begin:end], ref[first : first + end - begin, :], preferred_element_type=jnp.float32
-        )
-    out[...] = (total / denom[...]).astype(jnp.bfloat16)
-
-
-def attend(weights, denom, v_own, v_other):
+    out[...] = (total / denom[...]).astype(jnp.bfloat16) if half else total
+
+
+def attend(half, weights, *args):
     lines, count = weights.shape
-    vmem = pl.BlockSpec(memory_space=pltpu.VMEM)
-    return pl.pallas_call(
-        attend_kernel,
-        in_specs=[pl.BlockSpec(memory_space=pltpu.HBM), vmem, vmem, vmem],
+    keys = count // 2
+    vmem = pl.BlockSpec(memory_space=pltpu.VMEM)
+    return pl.pallas_call(
+        functools.partial(attend_kernel, half),
+        in_specs=[pl.BlockSpec(memory_space=pltpu.HBM)] + [vmem] * len(args),
         out_specs=vmem,
-        out_shape=jax.ShapeDtypeStruct((lines, HD), jnp.bfloat16),
-        scratch_shapes=[pltpu.VMEM((lines, count), jnp.bfloat16), pltpu.SemaphoreType.DMA((4,))],
+        out_shape=jax.ShapeDtypeStruct((lines, HD), jnp.bfloat16 if half else jnp.float32),
+        scratch_shapes=[pltpu.VMEM((lines, keys), jnp.bfloat16), pltpu.SemaphoreType.DMA((4,))],
         compiler_params=pltpu.CompilerParams(vmem_limit_bytes=16 << 20),
         cost_estimate=pl.CostEstimate(
-            flops=2 * lines * count * HD, bytes_accessed=7_000_000, transcendentals=0
+            flops=2 * lines * keys * HD, bytes_accessed=3_500_000, transcendentals=0
         ),
-        name="attend",
-    )(*in_hbm(weights), denom, v_own, v_other)
+        name="attend_other" if half else "attend_own",
+    )(*in_hbm(weights), *args)
 
 
 def exchange(value, axes):
@@ -387,33 +396,34 @@
     core = lax.axis_index("c")
     side = lax.axis_index("zh")
     group = side * 16 + lax.axis_index("s") * 8 + core
+    head = lax.axis_index("h")
+    owners = [head ^ flip for flip in range(heads)]
     place = [core, 1 - core] + [group + owner * 2 for owner in range(heads)]
-    place = (jnp.stack(place + [side * 8, (1 - side) * 8]) * rows).astype(jnp.int32)
-
-    last, blocks = pack(gate_first, hyena_value, gate_second, attn_keys, queries)
-    blocks = exchange(blocks.reshape(8, 2, rows, HD), ("s", "h"))
+    place = (jnp.stack(place + [side * 8, (1 - side) * 8] + owners) * rows).astype(jnp.int32)
+
+    last, blocks = pack(gate_first, hyena_value, gate_second, attn_keys)
+    keys_near = exchange(blocks.reshape(8, rows, HD), ("s", "h"))
     halo = lax.ppermute(last, ROWS_AXES, [(source, source + 1) for source in range(count - 1)])
     early_parts = early(last, gate_second, residual, short_taps, long_taps)
     stream, squares = late(halo, *early_parts)
 
-    blocks, squares = lax.optimization_barrier((blocks, squares))
-    keys_near = blocks[:, 0]
-    my_queries = lax.dynamic_slice_in_dim(blocks, lax.axis_index("s") * heads, heads, 0)[:, 1]
+    keys_near, squares = lax.optimization_barrier((keys_near, squares))
+    gathered = exchange(squares, CHAN_AXES)
     keys_far = lax.ppermute(keys_near, "zh", [(0, 1)])
-    gathered = exchange(squares, CHAN_AXES)
     packed = normalize(width, gathered, stream, norm_gain.reshape(1, chans))
-    packed, keys_far = lax.optimization_barrier((packed, keys_far))
+    heads_of_q = [lax.dynamic_slice_in_dim(queries, owner * HD, HD, 1) for owner in owners]
+    packed, keys_far, heads_of_q = lax.optimization_barrier((packed, keys_far, heads_of_q))
+    for flip in range(1, heads):
+        pairs = [(source, source ^ flip) for source in range(heads)]
+        heads_of_q[flip] = lax.ppermute(heads_of_q[flip], "h", pairs)
     values_own = exchange(packed.reshape(16, rows, HD), PEERS)
 
     parts = [keys_near, swap_cores(keys_near), keys_far, swap_cores(keys_far)]
-    weights, denom = score(
-        place, my_queries.reshape(heads * rows, HD), [part.reshape(8 * rows, HD) for part in parts]
-    )
+    weights, denom = score(place, heads_of_q, [part.reshape(8 * rows, HD) for part in parts])
     values_own, denom = lax.optimization_barrier((values_own, denom))
     values_other = swap_cores(values_own)
-    result = attend(
-        weights, denom, values_own.reshape(16 * rows, HD), values_other.reshape(16 * rows, HD)
-    )
+    result = attend(0, weights, values_own.reshape(16 * rows, HD))
+    result = attend(1, weights, denom, result, values_other.reshape(16 * rows, HD))
     attended = exchange(result.reshape(heads, rows, HD), "h").transpose(1, 0, 2).reshape(rows, chans)
     return stream, attended
 

time: 103 us -> 106 us (1.029)
  starting transfers between devices: 44.8 us -> 59.7 us
  blocking collectives: 23.4 us -> 8.56 us
  Pallas kernels: 20.2 us -> 21.8 us
  waiting for transfers between devices: 12.4 us -> 13.5 us
    all_to_all x2 -> x1, blocking collectives: 23.4 us -> 8.56 us  [exchange(): return lax.all_to_all(value, axes, 0, 0, tiled=True)]
    ppermute x0 -> x3, starting transfers between devices: none -> 9.35 us  [shards(): heads_of_q[flip] = lax.ppermute(heads_of_q[flip], 'h', pairs)]
    all_to_all x2 -> x3, starting transfers between devices: 14.9 us -> 22.4 us  [exchange(): return lax.all_to_all(value, axes, 0, 0, tiled=True)]
    ppermute x0 -> x3, waiting for transfers between devices: none -> 4.61 us  [shards(): heads_of_q[flip] = lax.ppermute(heads_of_q[flip], 'h', pairs)]
    ppermute x1, waiting for transfers between devices: 6.05 us -> 1.99 us  [shards(): lax.ppermute(last, ROWS_AXES, [(source, source + 1) for source in range(c...]
    all_to_all x2 -> x3, waiting for transfers between devices: 3.26 us -> 6.86 us  [exchange(): return lax.all_to_all(value, axes, 0, 0, tiled=True)]
    ppermute x3, waiting for transfers between devices: 3.04 us -> 0.01 us  [swap_cores(): return lax.ppermute(value, 'c', [(0, 1), (1, 0)])]
    ppermute x1, starting transfers between devices: 11.2 us -> 9.31 us  [shards(): keys_far = lax.ppermute(keys_near, 'zh', [(0, 1)])]
  transfers between devices with their start and end apart: 7 -> 11, of which waited for: 4 -> 4; matrix products, arithmetic and copies ran while one was open for 0% -> 0% of each run, Pallas kernels for 13% -> 16%
where the time goes in v6:
time: 106 us; the launch traced here: 105 us
  starting transfers between devices  59.7 us (56%)
  Pallas kernels  21.8 us (21%)
  waiting for transfers between devices  13.5 us (13%)
  blocking collectives  8.56 us (8%)
    all_to_all x3, starting transfers between devices, exchange(): return lax.all_to_all(value, axes, 0, 0, tiled=True)  22.4 us
    ppermute x3, starting transfers between devices, swap_cores(): return lax.ppermute(value, 'c', [(0, 1), (1, 0)])  12.5 us
    ppermute x3, starting transfers between devices, shards(): heads_of_q[flip] = lax.ppermute(heads_of_q[flip], 'h', pairs)  9.35 us
    ppermute x1, starting transfers between devices, shards(): keys_far = lax.ppermute(keys_near, 'zh', [(0, 1)])  9.31 us
    all_to_all x1, blocking collectives, exchange(): return lax.all_to_all(value, axes, 0, 0, tiled=True)  8.56 us
    all_to_all x3, waiting for transfers between devices, exchange(): return lax.all_to_all(value, axes, 0, 0, tiled=True)  6.86 us
    pallas_call x2, Pallas kernels, attend(): pl.pallas_call(functools.partial(attend_kernel, half), in_specs=[pl.Block...  6.22 us
    ppermute x1, starting transfers between devices, shards(): lax.ppermute(last, ROWS_AXES, [(source, source + 1) for source in range(c...  6.07 us
  transfers between devices with their start and end apart: 11, of which 4 were waited for; matrix products, arithmetic and copies ran while one was open for 0% of the time, Pallas kernels for 16%

profile of v6, /device:TPU:1, one launch (start us, length us, event | category | flops | bytes accessed | tf_op | source)
XLA Modules:
  0.0 105.2 jit_solution(2259274580026056573)
XLA Ops:
  0.6 1.9 %pack.1 = (bf16[280,512]{1,0:T(8,128)(2,1)S(1)}, bf16[2,4,136,128]{3,2,1,0:T(8,128)(2,1)}) custom-call(bf16[136,512]{1,0:T(8,128)(2,1)} %gf.1, bf16[136,512]{1,0:T(8,128)(2,1)} %hv.1, bf16[136,512]{1,0:T(8,128)(2,1)} %gs.3, bf16[136,512]{1,0:T(8,128)(2,1)} %keys.1), custom_call_target="tpu_custom_call" | custom-call | bytes 600000 | tf_op jit(solution)/shard_map/pack/pallas_call | solution.py:209
  2.6 7.7 %all-to-all-start = ((bf16[8,136,128]{2,1,0:T(8,128)(2,1)}), bf16[8,136,128]{2,1,0:T(8,128)(2,1)S(1)}, u32[]{:S(2)}, u32[]{:S(2)}) async-start(bf16[8,136,128]{2,1,0:T(8,128)(2,1)} %bitcast.12), calls=%async_computation | async-start | bytes 557056 | tf_op jit(solution)/shard_map/all_to_all | solution.py:383
  10.2 6.1 %collective-permute-start = (bf16[280,512]{1,0:T(8,128)(2,1)S(1)}, bf16[280,512]{1,0:T(8,128)(2,1)S(1)}, u32[]{:S(2)}, u32[]{:S(2)}) collective-permute-start(bf16[280,512]{1,0:T(8,128)(2,1)S(1)} %get-tuple-element.24.packed), channel_id=1, source_target_pairs={{0,16},{16,32},{32,48},{48,64},{64,80},{80,96},{96,112},{112,128},... | collective-permute-start | bytes 860168 | tf_op jit(solution)/shard_map/ppermute | solution.py:406
  16.3 2.8 %early.1 = (f32[136,512]{1,0:T(8,128)S(1)}, f32[136,512]{1,0:T(8,128)S(1)}, bf16[136,512]{1,0:T(8,128)(2,1)S(1)}, f32[3,8,512]{2,1,0:T(8,128)S(1)}, f32[3,3,512]...) custom-call(bf16[280,512]{1,0:T(8,128)(2,1)S(1)} %get-tuple-element.24.packed, bf16[136,512]{1,0:T(8,128)(2,1)} %gs.3, ...), custom_call_target="tpu_custom_call" | custom-call | flops 6000000000 | bytes 2000000 | tf_op jit(solution)/shard_map/early/pallas_call | solution.py:95
  19.1 2.0 %collective-permute-done.halo = bf16[280,512]{1,0:T(8,128)(2,1)S(1)} collective-permute-done((bf16[280,512]{1,0:T(8,128)(2,1)S(1)}, bf16[280,512]{1,0:T(8,128)(2,1)S(1)}, u32[]{:S(2)}, u32[]{:S(2)}) %collective-permute-start) | collective-permute-done | bytes 286752 | tf_op jit(solution)/shard_map/ppermute | solution.py:406
  21.1 3.4 %late.1 = (bf16[136,512]{1,0:T(8,128)(2,1)}, f32[16,1,136]{2,1,0:T(1,128)}) custom-call(bf16[280,512]{1,0:T(8,128)(2,1)S(1)} %collective-permute-done.halo, f32[136,512]{1,0:T(8,128)S(1)} %get-tuple-element.25.partial, f32[136,512]{1,0:T(8,128)S(1)} %get-tuple-element.26.feat, bf16[136,512]{1,0:T(8,128)(2,1)S(1)} %get-tuple-element.27.res, ...), custom_call_target="tpu_custom_call" | custom-call | flops 30000001024 | bytes 2000000 | tf_op jit(solution)/shard_map/late/pallas_call | solution.py:167
  24.5 9.3 %collective-permute-start.1 = (bf16[8,136,128]{2,1,0:T(8,128)(2,1)S(1)}, bf16[8,136,128]{2,1,0:T(8,128)(2,1)S(1)}, u32[]{:S(2)}, u32[]{:S(2)}) collective-permute-start(bf16[8,136,128]{2,1,0:T(8,128)(2,1)S(1)} %all-to-all-done), channel_id=1, source_target_pairs={{0,256},{1,257},{2,258},{3,259},{4,260},{5,261},{6,262},{7,263},{8... | collective-permute-start | bytes 835592 | tf_op jit(solution)/shard_map/ppermute | solution.py:412
  33.9 6.9 %all-to-all-start.1 = ((f32[16,1,136]{2,1,0:T(1,128)}), f32[16,1,136]{2,1,0:T(1,128)S(1)}, u32[]{:S(2)}, u32[]{:S(2)}) async-start(f32[16,1,136]{2,1,0:T(1,128)} %get-tuple-element.34), calls=%async_computation.1 | async-start | bytes 32768 | tf_op jit(solution)/shard_map/all_to_all | solution.py:383
  40.8 6.9 %all-to-all-done.1.gathered = f32[16,1,136]{2,1,0:T(1,128)S(1)} async-done(((f32[16,1,136]{2,1,0:T(1,128)}), f32[16,1,136]{2,1,0:T(1,128)S(1)}, u32[]{:S(2)}, u32[]{:S(2)}) %all-to-all-start.1) | async-done | bytes 8736 | tf_op jit(solution)/shard_map/all_to_all | solution.py:383
  47.6 2.1 %normalize.1 = bf16[4,4,136,128]{3,2,1,0:T(8,128)(2,1)} custom-call(f32[16,1,136]{2,1,0:T(1,128)S(1)} %all-to-all-done.1.gathered, bf16[136,512]{1,0:T(8,128)(2,1)} %get-tuple-element.22.stream, f32[1,512]{1,0:T(1,128)S(1)} %bitcast.32), custom_call_target="tpu_custom_call" | custom-call | flops 1000000 | bytes 800000 | tf_op jit(solution)/shard_map/normalize/pallas_call | solution.py:248
  49.7 7.9 %all-to-all-start.2 = ((bf16[16,136,128]{2,1,0:T(8,128)(2,1)}), bf16[16,136,128]{2,1,0:T(8,128)(2,1)S(1)}, u32[]{:S(2)}, u32[]{:S(2)}) async-start(bf16[16,136,128]{2,1,0:T(8,128)(2,1)} %bitcast.18), calls=%async_computation.2 | async-start | bytes 1114112 | tf_op jit(solution)/shard_map/all_to_all | solution.py:383
  57.6 6.6 %collective-permute-start.5 = (bf16[8,136,128]{2,1,0:T(8,128)(2,1)S(1)}, bf16[8,136,128]{2,1,0:T(8,128)(2,1)S(1)}, u32[]{:S(2)}, u32[]{:S(2)}) collective-permute-start(bf16[8,136,128]{2,1,0:T(8,128)(2,1)S(1)} %all-to-all-done), channel_id=1, source_target_pairs={{0,16},{16,0},{1,17},{17,1},{2,18},{18,2},{3,19},{19,3},{4,20},{20... | collective-permute-start | bytes 835592 | tf_op jit(solution)/shard_map/ppermute | solution.py:387
  64.2 1.9 %collective-permute-start.6 = (bf16[8,136,128]{2,1,0:T(8,128)(2,1)S(1)}, bf16[8,136,128]{2,1,0:T(8,128)(2,1)S(1)}, u32[]{:S(2)}, u32[]{:S(2)}) collective-permute-start(bf16[8,136,128]{2,1,0:T(8,128)(2,1)S(1)} %collective-permute-done.1), channel_id=1, source_target_pairs={{0,16},{16,0},{1,17},{17,1},{2,18},{18,2},{3,19},{19,3},{4,20},{20... | collective-permute-start | bytes 835592 | tf_op jit(solution)/shard_map/ppermute | solution.py:387
  66.3 3.4 %collective-permute-start.2 = (bf16[136,128]{1,0:T(8,128)(2,1)S(1)}, bf16[136,128]{1,0:T(8,128)(2,1)S(1)}, u32[]{:S(2)}, u32[]{:S(2)}) collective-permute-start(bf16[136,128]{1,0:T(8,128)(2,1)S(1)} %get-tuple-element.37), channel_id=1, source_target_pairs={{0,32},{32,0},{64,96},{96,64},{1,33},{33,1},{65,97},{97,65},{2,34}... | collective-permute-start | bytes 104456 | tf_op jit(solution)/shard_map/ppermute | solution.py:418
  69.7 4.0 %collective-permute-start.3 = (bf16[136,128]{1,0:T(8,128)(2,1)S(1)}, bf16[136,128]{1,0:T(8,128)(2,1)S(1)}, u32[]{:S(2)}, u32[]{:S(2)}) collective-permute-start(bf16[136,128]{1,0:T(8,128)(2,1)S(1)} %get-tuple-element.38), channel_id=1, source_target_pairs={{0,64},{32,96},{64,0},{96,32},{1,65},{33,97},{65,1},{97,33},{2,66}... | collective-permute-start | bytes 104456 | tf_op jit(solution)/shard_map/ppermute | solution.py:418
  73.7 1.9 %collective-permute-start.4 = (bf16[136,128]{1,0:T(8,128)(2,1)S(1)}, bf16[136,128]{1,0:T(8,128)(2,1)S(1)}, u32[]{:S(2)}, u32[]{:S(2)}) collective-permute-start(bf16[136,128]{1,0:T(8,128)(2,1)S(1)} %get-tuple-element.39), channel_id=1, source_target_pairs={{0,96},{32,64},{64,32},{96,0},{1,97},{33,65},{65,33},{97,1},{2,98}... | collective-permute-start | bytes 104456 | tf_op jit(solution)/shard_map/ppermute | solution.py:418
  75.7 0.4 collective-permute-done.3.q2
  76.1 4.2 %collective-permute-done.4.q3 = bf16[136,128]{1,0:T(8,128)(2,1)S(1)} collective-permute-done((bf16[136,128]{1,0:T(8,128)(2,1)S(1)}, bf16[136,128]{1,0:T(8,128)(2,1)S(1)}, u32[]{:S(2)}, u32[]{:S(2)}) %collective-permute-start.4) | collective-permute-done | bytes 34848 | tf_op jit(solution)/shard_map/ppermute | solution.py:418
  80.3 5.4 %score.1 = (bf16[544,4352]{1,0:T(8,128)(2,1)}, f32[544,128]{1,0:T(8,128)S(1)}) custom-call(s32[12]{0:T(128)S(1)} %broadcast_multiply_fusion.place, bf16[136,128]{1,0:T(8,128)(2,1)S(1)} %get-tuple-element.36.q0, bf16[136,128]{1,0:T(8,128)(2,1)S(1)} %collective-permute-done.2.q1, bf16[136,128]{1,0:T(8,128)(2,1)S(1)} %collective-permute-done.3.q2, ...), custom_call_target="tpu_custom_call" | custom-call | flops 606076928 | bytes 8000000 | tf_op jit(solution)/shard_map/score/pallas_call | solution.py:317
  85.7 4.0 %collective-permute-start.7 = (bf16[16,136,128]{2,1,0:T(8,128)(2,1)S(1)}, bf16[16,136,128]{2,1,0:T(8,128)(2,1)S(1)}, u32[]{:S(2)}, u32[]{:S(2)}) collective-permute-start(bf16[16,136,128]{2,1,0:T(8,128)(2,1)S(1)} %all-to-all-done.2), channel_id=1, source_target_pairs={{0,16},{16,0},{1,17},{17,1},{2,18},{18,2},{3,19},{19,3},{4,20},{20... | collective-permute-start | bytes 1671176 | tf_op jit(solution)/shard_map/ppermute | solution.py:387
  89.7 3.1 %attend_own.1.refs_1_ = f32[544,128]{1,0:T(8,128)S(1)} custom-call(bf16[544,4352]{1,0:T(8,128)(2,1)} %get-tuple-element.41.weights_in, bf16[2176,128]{1,0:T(8,128)(2,1)S(1)} %bitcast.28), custom_call_target="tpu_custom_call" | custom-call | flops 303038464 | bytes 3500000 | tf_op jit(solution)/shard_map/attend_own/pallas_call | solution.py:368
  92.9 3.1 %attend_other.1 = bf16[544,128]{1,0:T(8,128)(2,1)S(1)} custom-call(bf16[544,4352]{1,0:T(8,128)(2,1)} %get-tuple-element.41.weights_in, f32[544,128]{1,0:T(8,128)S(1)} %get-tuple-element.44.refs_0_, f32[544,128]{1,0:T(8,128)S(1)} %attend_own.1.refs_1_, bf16[2176,128]{1,0:T(8,128)(2,1)S(1)} %bitcast.29), custom_call_target="tpu_custom_call" | custom-call | flops 303038464 | bytes 3500000 | tf_op jit(solution)/shard_map/attend_other/pallas_call | solution.py:368
  96.0 8.6 %all_to_all.20 = bf16[4,136,128]{2,1,0:T(8,128)(2,1)S(1)} all-to-all(bf16[4,136,128]{2,1,0:T(8,128)(2,1)S(1)} %bitcast.30), channel_id=1, replica_groups=mesh['zh'=2,'s'=2,'h'=4,'c'=2,'x'=4,'zl'=4] {'h'}, dimensions={0} | all-to-all | bytes 278528 | tf_op jit(solution)/shard_map/all_to_all | solution.py:383
  104.5 0.7 copy_bitcast_fusion
  (14 shorter events, 0.2 us)
Async XLA Ops:
  2.6 22.0 %all-to-all-start = ((bf16[8,136,128]{2,1,0:T(8,128)(2,1)}), bf16[8,136,128]{2,1,0:T(8,128)(2,1)S(1)}, u32[]{:S(2)}, u32[]{:S(2)}) async-start(bf16[8,136,128]{2,1,0:T(8,128)(2,1)} %bitcast.12), calls=%async_computation | async-start | bytes 557056 | tf_op jit(solution)/shard_map/all_to_all | solution.py:383
  10.2 10.8 %collective-permute-start = (bf16[280,512]{1,0:T(8,128)(2,1)S(1)}, bf16[280,512]{1,0:T(8,128)(2,1)S(1)}, u32[]{:S(2)}, u32[]{:S(2)}) collective-permute-start(bf16[280,512]{1,0:T(8,128)(2,1)S(1)} %get-tuple-element.24.packed), channel_id=1, source_target_pairs={{0,16},{16,32},{32,48},{48,64},{64,80},{80,96},{96,112},{112,128},... | collective-permute-start | bytes 860168 | tf_op jit(solution)/shard_map/ppermute | solution.py:406
  21.1 19.7 %copy-start.1 = (bf16[136,512]{1,0:T(8,128)(2,1)S(1)}, bf16[136,512]{1,0:T(8,128)(2,1)}, u32[]{:S(2)}) copy-start(bf16[136,512]{1,0:T(8,128)(2,1)} %param.16) | copy-start | bytes 417796
  21.1 26.6 %copy-start = (f32[512]{0:T(512)S(1)}, f32[512]{0:T(512)}, u32[]{:S(2)}) copy-start(f32[512]{0:T(512)} %param.15) | copy-start | bytes 6148
  24.5 25.2 %collective-permute-start.1 = (bf16[8,136,128]{2,1,0:T(8,128)(2,1)S(1)}, bf16[8,136,128]{2,1,0:T(8,128)(2,1)S(1)}, u32[]{:S(2)}, u32[]{:S(2)}) collective-permute-start(bf16[8,136,128]{2,1,0:T(8,128)(2,1)S(1)} %all-to-all-done), channel_id=1, source_target_pairs={{0,256},{1,257},{2,258},{3,259},{4,260},{5,261},{6,262},{7,263},{8... | collective-permute-start | bytes 835592 | tf_op jit(solution)/shard_map/ppermute | solution.py:412
  33.9 13.8 %all-to-all-start.1 = ((f32[16,1,136]{2,1,0:T(1,128)}), f32[16,1,136]{2,1,0:T(1,128)S(1)}, u32[]{:S(2)}, u32[]{:S(2)}) async-start(f32[16,1,136]{2,1,0:T(1,128)} %get-tuple-element.34), calls=%async_computation.1 | async-start | bytes 32768 | tf_op jit(solution)/shard_map/all_to_all | solution.py:383
  49.7 36.0 %all-to-all-start.2 = ((bf16[16,136,128]{2,1,0:T(8,128)(2,1)}), bf16[16,136,128]{2,1,0:T(8,128)(2,1)S(1)}, u32[]{:S(2)}, u32[]{:S(2)}) async-start(bf16[16,136,128]{2,1,0:T(8,128)(2,1)} %bitcast.18), calls=%async_computation.2 | async-start | bytes 1114112 | tf_op jit(solution)/shard_map/all_to_all | solution.py:383
  57.6 18.0 %collective-permute-start.5 = (bf16[8,136,128]{2,1,0:T(8,128)(2,1)S(1)}, bf16[8,136,128]{2,1,0:T(8,128)(2,1)S(1)}, u32[]{:S(2)}, u32[]{:S(2)}) collective-permute-start(bf16[8,136,128]{2,1,0:T(8,128)(2,1)S(1)} %all-to-all-done), channel_id=1, source_target_pairs={{0,16},{16,0},{1,17},{17,1},{2,18},{18,2},{3,19},{19,3},{4,20},{20... | collective-permute-start | bytes 835592 | tf_op jit(solution)/shard_map/ppermute | solution.py:387
  64.2 16.0 %collective-permute-start.6 = (bf16[8,136,128]{2,1,0:T(8,128)(2,1)S(1)}, bf16[8,136,128]{2,1,0:T(8,128)(2,1)S(1)}, u32[]{:S(2)}, u32[]{:S(2)}) collective-permute-start(bf16[8,136,128]{2,1,0:T(8,128)(2,1)S(1)} %collective-permute-done.1), channel_id=1, source_target_pairs={{0,16},{16,0},{1,17},{17,1},{2,18},{18,2},{3,19},{19,3},{4,20},{20... | collective-permute-start | bytes 835592 | tf_op jit(solution)/shard_map/ppermute | solution.py:387
  66.3 9.4 %collective-permute-start.2 = (bf16[136,128]{1,0:T(8,128)(2,1)S(1)}, bf16[136,128]{1,0:T(8,128)(2,1)S(1)}, u32[]{:S(2)}, u32[]{:S(2)}) collective-permute-start(bf16[136,128]{1,0:T(8,128)(2,1)S(1)} %get-tuple-element.37), channel_id=1, source_target_pairs={{0,32},{32,0},{64,96},{96,64},{1,33},{33,1},{65,97},{97,65},{2,34}... | collective-permute-start | bytes 104456 | tf_op jit(solution)/shard_map/ppermute | solution.py:418
  69.7 6.4 %collective-permute-start.3 = (bf16[136,128]{1,0:T(8,128)(2,1)S(1)}, bf16[136,128]{1,0:T(8,128)(2,1)S(1)}, u32[]{:S(2)}, u32[]{:S(2)}) collective-permute-start(bf16[136,128]{1,0:T(8,128)(2,1)S(1)} %get-tuple-element.38), channel_id=1, source_target_pairs={{0,64},{32,96},{64,0},{96,32},{1,65},{33,97},{65,1},{97,33},{2,66}... | collective-permute-start | bytes 104456 | tf_op jit(solution)/shard_map/ppermute | solution.py:418
  73.7 6.6 %collective-permute-start.4 = (bf16[136,128]{1,0:T(8,128)(2,1)S(1)}, bf16[136,128]{1,0:T(8,128)(2,1)S(1)}, u32[]{:S(2)}, u32[]{:S(2)}) collective-permute-start(bf16[136,128]{1,0:T(8,128)(2,1)S(1)} %get-tuple-element.39), channel_id=1, source_target_pairs={{0,96},{32,64},{64,32},{96,0},{1,97},{33,65},{65,33},{97,1},{2,98}... | collective-permute-start | bytes 104456 | tf_op jit(solution)/shard_map/ppermute | solution.py:418
  85.7 7.2 %collective-permute-start.7 = (bf16[16,136,128]{2,1,0:T(8,128)(2,1)S(1)}, bf16[16,136,128]{2,1,0:T(8,128)(2,1)S(1)}, u32[]{:S(2)}, u32[]{:S(2)}) collective-permute-start(bf16[16,136,128]{2,1,0:T(8,128)(2,1)S(1)} %all-to-all-done.2), channel_id=1, source_target_pairs={{0,16},{16,0},{1,17},{17,1},{2,18},{18,2},{3,19},{19,3},{4,20},{20... | collective-permute-start | bytes 1671176 | tf_op jit(solution)/shard_map/ppermute | solution.py:387

commit v7 on v5

--- a/solution.py
+++ b/solution.py
@@ -46,15 +46,22 @@
 
 
 def early_kernel(
-    packed, gs, res, taps_in, long_in, partial, feat, res_out, edge, taps_out, long_out,
+    packed, gs, res, taps_in, long_in, keys, queries, partial, feat, res_out, edge, taps_out, long_out, blocks,
     gs_v, ext, prod, copies, sems,
 ):
     rows, chans = gs.shape
     loads = [(taps_in, taps_out), (long_in, long_out), (gs, gs_v), (res, res_out)]
     moves = [pltpu.make_async_copy(src, dst, sems.at[i]) for i, (src, dst) in enumerate(loads)]
+    first = len(moves)
+    for copy in range(blocks.shape[0]):
+        for head in range(blocks.shape[1]):
+            for kind, source in enumerate((keys, queries)):
+                src = source.at[:, head * HD : (head + 1) * HD]
+                dst = blocks.at[copy, head, kind]
+                moves.append(pltpu.make_async_copy(src, dst, sems.at[len(moves)]))
     for move in moves:
         move.start()
-    for move in moves:
+    for move in moves[:first]:
         move.wait()
     tiles = rows // 8
     pairs = [(tile, group) for group in range(long_in.shape[0] // 8) for tile in range(group, tiles)]
@@ -82,20 +89,23 @@
         return carry
 
     lax.fori_loop(0, chans // HD, one_head, 0)
+    for move in moves[first:]:
+        move.wait()
 
 
 def in_hbm(*arrays):
     return [pltpu.with_memory_space_constraint(array, pltpu.HBM) for array in arrays]
 
 
-def early(packed, gs, res, taps, long_taps):
+def early(packed, gs, res, taps, long_taps, keys, queries):
     rows, chans = gs.shape
+    heads = chans // HD
     hbm = pl.BlockSpec(memory_space=pltpu.HBM)
     vmem = pl.BlockSpec(memory_space=pltpu.VMEM)
     return pl.pallas_call(
         early_kernel,
-        in_specs=[vmem] + [hbm] * 4,
-        out_specs=[vmem] * 6,
+        in_specs=[vmem] + [hbm] * 6,
+        out_specs=[vmem] * 7,
         out_shape=[
             jax.ShapeDtypeStruct((rows, chans), jnp.float32),
             jax.ShapeDtypeStruct((rows, chans), jnp.float32),
@@ -103,18 +113,19 @@
             jax.ShapeDtypeStruct((3, 8, chans), jnp.float32),
             jax.ShapeDtypeStruct(taps.shape, jnp.float32),
             jax.ShapeDtypeStruct(long_taps.shape, jnp.bfloat16),
+            jax.ShapeDtypeStruct((2, heads, 2, rows, HD), jnp.bfloat16),
         ],
         scratch_shapes=[
             pltpu.VMEM((rows, chans), jnp.bfloat16),
             pltpu.VMEM((rows + 8, HD), jnp.float32),
             pltpu.VMEM((rows + 8, HD), jnp.float32),
             pltpu.VMEM((8, rows + 8, HD), jnp.float32),
-            pltpu.SemaphoreType.DMA((4,)),
+            pltpu.SemaphoreType.DMA((4 + 4 * heads,)),
         ],
         compiler_params=pltpu.CompilerParams(vmem_limit_bytes=32 << 20),
         cost_estimate=pl.CostEstimate(flops=6_000_000_000, bytes_accessed=2_000_000, transcendentals=0),
         name="early",
-    )(packed, *in_hbm(gs, res, taps, long_taps))
+    )(packed, *in_hbm(gs, res, taps, long_taps, keys, queries))
 
 
 def late_kernel(halo, partial, feat, res, edge, taps_in, long_in, stream, squares, ext, prod, copies):
@@ -157,8 +168,7 @@
         return total
 
     total = lax.fori_loop(0, chans // HD, one_head, total)
-    for peer in range(squares.shape[0]):
-        squares[peer] = total[0:1, :]
+    squares[...] = total
 
 
 def late(halo, partial, feat, res, edge, taps, long_taps):
@@ -170,7 +180,7 @@
         out_specs=[vmem] * 2,
         out_shape=[
             jax.ShapeDtypeStruct((rows, chans), jnp.bfloat16),
-            jax.ShapeDtypeStruct((16, 1, rows), jnp.float32),
+            jax.ShapeDtypeStruct((8, rows), jnp.float32),
         ],
         scratch_shapes=[
             pltpu.VMEM((rows + 8, HD), jnp.float32),
@@ -183,14 +193,9 @@
     )(halo, partial, feat, res, edge, taps, long_taps)
 
 
-def pack_kernel(gf, hv, gs, keys, queries, halo, blocks, sems):
+def pack_kernel(gf, hv, gs, halo, sems):
     rows = gf.shape[0]
-    pairs = []
-    for copy in range(blocks.shape[0]):
-        for head in range(blocks.shape[1]):
-            for kind, source in enumerate((keys, queries)):
-                pairs.append((source.at[:, head * HD : (head + 1) * HD], blocks.at[copy, head, kind]))
-    pairs += [
+    pairs = [
         (gf, halo.at[0:rows]),
         (hv, halo.at[rows : 2 * rows]),
         (gs.at[rows - 8 : rows], halo.at[2 * rows : 2 * rows + 8]),
@@ -202,31 +207,22 @@
         move.wait()
 
 
-def pack(gf, hv, gs, keys, queries):
+def pack(gf, hv, gs):
     rows, chans = gf.shape
-    heads = chans // HD
-    vmem = pl.BlockSpec(memory_space=pltpu.VMEM)
-    hbm = pl.BlockSpec(memory_space=pltpu.HBM)
     return pl.pallas_call(
         pack_kernel,
-        in_specs=[hbm] * 5,
-        out_specs=[vmem, vmem],
-        out_shape=[
-            jax.ShapeDtypeStruct((2 * rows + 8, chans), jnp.bfloat16),
-            jax.ShapeDtypeStruct((2, heads, 2, rows, HD), jnp.bfloat16),
-        ],
-        scratch_shapes=[pltpu.SemaphoreType.DMA((4 * heads + 3,))],
+        in_specs=[pl.BlockSpec(memory_space=pltpu.HBM)] * 3,
+        out_specs=pl.BlockSpec(memory_space=pltpu.VMEM),
+        out_shape=jax.ShapeDtypeStruct((2 * rows + 8, chans), jnp.bfloat16),
+        scratch_shapes=[pltpu.SemaphoreType.DMA((3,))],
         compiler_params=pltpu.CompilerParams(vmem_limit_bytes=16 << 20),
         cost_estimate=pl.CostEstimate(flops=0, bytes_accessed=600_000, transcendentals=0),
         name="pack",
-    )(*in_hbm(gf, hv, gs, keys, queries))
-
-
-def normalize_kernel(width, gathered, stream, gain, packed):
-    total = gathered[0]
-    for peer in range(1, gathered.shape[0]):
-        total = total + gathered[peer]
-    total = jnp.broadcast_to(total, (8, total.shape[1]))
+    )(*in_hbm(gf, hv, gs))
+
+
+def normalize_kernel(width, part0, part1, part2, part3, stream, gain, packed):
+    total = part0[...] + part1[...] + part2[...] + part3[...]
     total = lax.dot_general(
         jnp.where(lax.broadcasted_iota(jnp.int32, total.shape, 0) == 0, total, 0.0),
         jnp.ones((8, HD), jnp.float32),
@@ -243,17 +239,18 @@
             packed[copy, head] = value
 
 
-def normalize(width, gathered, stream, gain):
+def normalize(width, parts, stream, gain):
     rows, chans = stream.shape
     vmem = pl.BlockSpec(memory_space=pltpu.VMEM)
     return pl.pallas_call(
         functools.partial(normalize_kernel, width),
-        in_specs=[vmem] * 3,
+        in_specs=[vmem] * 6,
         out_specs=vmem,
         out_shape=jax.ShapeDtypeStruct((4, chans // HD, rows, HD), jnp.bfloat16),
+        compiler_params=pltpu.CompilerParams(vmem_limit_bytes=8 << 20),
         cost_estimate=pl.CostEstimate(flops=1_000_000, bytes_accessed=800_000, transcendentals=20_000),
         name="normalize",
-    )(gathered, stream, gain)
+    )(*parts, *in_hbm(stream), gain)
 
 
 def score_kernel(place, q, k0, k1, k2, k3, out, denom, keys, scores, weights, sems):
@@ -333,45 +330,79 @@
     )(place, q, *keys)
 
 
-def attend_kernel(weights_in, denom, v_own, v_other, out, weights, sems):
-    keys = v_own.shape[0]
-    cuts = [0, 1152, keys, keys + 1152, 2 * keys]
+def attend_own_kernel(weights_in, values, out, later, weights, sems):
+    keys = values.shape[0]
+    cuts = [0, 640, 1152, 1664, keys]
     moves = []
-    for index, (begin, end) in enumerate(zip(cuts, cuts[1:])):
-        moves.append(
-            pltpu.make_async_copy(weights_in.at[:, begin:end], weights.at[:, begin:end], sems.at[index])
-        )
-    for move in moves:
+    for half, target in enumerate((weights, later)):
+        for begin, end in zip(cuts, cuts[1:]):
+            src = weights_in.at[:, half * keys + begin : half * keys + end]
+            moves.append(pltpu.make_async_copy(src, target.at[:, begin:end], sems.at[len(moves)]))
+    for move in moves[:3]:
         move.start()
     total = jnp.zeros(out.shape, jnp.float32)
-    for move, begin, end in zip(moves, cuts, cuts[1:]):
+    for index, (begin, end) in enumerate(zip(cuts, cuts[1:])):
+        moves[index].wait()
+        for move in moves[3 + 2 * index : min(5 + 2 * index, len(moves))]:
+            move.start()
+        total = total + jnp.dot(
+            weights[:, begin:end], values[begin:end, :], preferred_element_type=jnp.float32
+        )
+    out[...] = total
+    for move in moves[4:]:
         move.wait()
-        ref, first = (v_own, begin) if begin < keys else (v_other, begin - keys)
-        total = total + jnp.dot(
-            weights[:, begin:end], ref[first : first + end - begin, :], preferred_element_type=jnp.float32
-        )
+
+
+def attend_other_kernel(weights, denom, before, values, out):
+    total = before[...] + jnp.dot(weights[...], values[...], preferred_element_type=jnp.float32)
     out[...] = (total / denom[...]).astype(jnp.bfloat16)
 
 
-def attend(weights, denom, v_own, v_other):
+def attend_own(weights, values):
     lines, count = weights.shape
-    vmem = pl.BlockSpec(memory_space=pltpu.VMEM)
-    return pl.pallas_call(
-        attend_kernel,
-        in_specs=[pl.BlockSpec(memory_space=pltpu.HBM), vmem, vmem, vmem],
+    keys = count // 2
+    vmem = pl.BlockSpec(memory_space=pltpu.VMEM)
+    return pl.pallas_call(
+        attend_own_kernel,
+        in_specs=[pl.BlockSpec(memory_space=pltpu.HBM), vmem],
+        out_specs=[vmem, vmem],
+        out_shape=[
+            jax.ShapeDtypeStruct((lines, HD), jnp.float32),
+            jax.ShapeDtypeStruct((lines, keys), jnp.bfloat16),
+        ],
+        scratch_shapes=[pltpu.VMEM((lines, keys), jnp.bfloat16), pltpu.SemaphoreType.DMA((8,))],
+        compiler_params=pltpu.CompilerParams(vmem_limit_bytes=16 << 20),
+        cost_estimate=pl.CostEstimate(
+            flops=2 * lines * keys * HD, bytes_accessed=5_500_000, transcendentals=0
+        ),
+        name="attend_own",
+    )(*in_hbm(weights), values)
+
+
+def attend_other(weights, denom, before, values):
+    lines, keys = weights.shape
+    vmem = pl.BlockSpec(memory_space=pltpu.VMEM)
+    return pl.pallas_call(
+        attend_other_kernel,
+        in_specs=[vmem] * 4,
         out_specs=vmem,
         out_shape=jax.ShapeDtypeStruct((lines, HD), jnp.bfloat16),
-        scratch_shapes=[pltpu.VMEM((lines, count), jnp.bfloat16), pltpu.SemaphoreType.DMA((4,))],
         compiler_params=pltpu.CompilerParams(vmem_limit_bytes=16 << 20),
         cost_estimate=pl.CostEstimate(
-            flops=2 * lines * count * HD, bytes_accessed=7_000_000, transcendentals=0
+            flops=2 * lines * keys * HD, bytes_accessed=3_500_000, transcendentals=0
         ),
-        name="attend",
-    )(*in_hbm(weights), denom, v_own, v_other)
+        name="attend_other",
+    )(weights, denom, before, values)
 
 
 def exchange(value, axes):
     return lax.all_to_all(value, axes, 0, 0, tiled=True)
+
+
+def three_others(value, axis):
+    return [
+        lax.ppermute(value, axis, [(source, source ^ flip) for source in range(4)]) for flip in range(1, 4)
+    ]
 
 
 def swap_cores(value):
@@ -390,30 +421,29 @@
     place = [core, 1 - core] + [group + owner * 2 for owner in range(heads)]
     place = (jnp.stack(place + [side * 8, (1 - side) * 8]) * rows).astype(jnp.int32)
 
-    last, blocks = pack(gate_first, hyena_value, gate_second, attn_keys, queries)
+    last = pack(gate_first, hyena_value, gate_second)
+    halo = lax.ppermute(last, ROWS_AXES, [(source, source + 1) for source in range(count - 1)])
+    *early_parts, blocks = early(
+        last, gate_second, residual, short_taps, long_taps, attn_keys, queries
+    )
     blocks = exchange(blocks.reshape(8, 2, rows, HD), ("s", "h"))
-    halo = lax.ppermute(last, ROWS_AXES, [(source, source + 1) for source in range(count - 1)])
-    early_parts = early(last, gate_second, residual, short_taps, long_taps)
     stream, squares = late(halo, *early_parts)
-
-    blocks, squares = lax.optimization_barrier((blocks, squares))
+    squares = sum(three_others(squares, "x"), squares)
+    parts = [squares] + three_others(squares, "zl")
+    packed = normalize(width, parts, stream, norm_gain.reshape(1, chans))
+    values_own = exchange(packed.reshape(16, rows, HD), PEERS)
+
     keys_near = blocks[:, 0]
     my_queries = lax.dynamic_slice_in_dim(blocks, lax.axis_index("s") * heads, heads, 0)[:, 1]
     keys_far = lax.ppermute(keys_near, "zh", [(0, 1)])
-    gathered = exchange(squares, CHAN_AXES)
-    packed = normalize(width, gathered, stream, norm_gain.reshape(1, chans))
-    packed, keys_far = lax.optimization_barrier((packed, keys_far))
-    values_own = exchange(packed.reshape(16, rows, HD), PEERS)
-
     parts = [keys_near, swap_cores(keys_near), keys_far, swap_cores(keys_far)]
     weights, denom = score(
         place, my_queries.reshape(heads * rows, HD), [part.reshape(8 * rows, HD) for part in parts]
     )
     values_own, denom = lax.optimization_barrier((values_own, denom))
     values_other = swap_cores(values_own)
-    result = attend(
-        weights, denom, values_own.reshape(16 * rows, HD), values_other.reshape(16 * rows, HD)
-    )
+    result, weights_other = attend_own(weights, values_own.reshape(16 * rows, HD))
+    result = attend_other(weights_other, denom, result, values_other.reshape(16 * rows, HD))
     attended = exchange(result.reshape(heads, rows, HD), "h").transpose(1, 0, 2).reshape(rows, chans)
     return stream, attended
 

time: 103 us -> 110 us (1.068)
  the two profiles are of different devices: /device:TPU:1 before, /device:TPU:64 now
where the time goes in v7:
time: 110 us
  starting transfers between devices  57.4 us (52%)
  waiting for transfers between devices  20.4 us (19%)
  Pallas kernels  19.6 us (18%)
  blocking collectives  10.7 us (10%)
    ppermute x6, starting transfers between devices, three_others(): lax.ppermute(value, axis, [(source, source ^ flip) for source in range(4)])  21.2 us
    all_to_all x2, starting transfers between devices, exchange(): return lax.all_to_all(value, axes, 0, 0, tiled=True)  20.8 us
    ppermute x1, waiting for transfers between devices, shards(): keys_far = lax.ppermute(keys_near, 'zh', [(0, 1)])  13.6 us
    all_to_all x1, blocking collectives, exchange(): return lax.all_to_all(value, axes, 0, 0, tiled=True)  10.7 us
    ppermute x1, starting transfers between devices, shards(): keys_far = lax.ppermute(keys_near, 'zh', [(0, 1)])  7.75 us
    ppermute x3, starting transfers between devices, swap_cores(): return lax.ppermute(value, 'c', [(0, 1), (1, 0)])  5.87 us
    pallas_call x1, Pallas kernels, score(): pl.pallas_call(score_kernel, in_specs=[pl.BlockSpec(memory_space=pltpu.SM...  5.39 us
    ppermute x6, waiting for transfers between devices, three_others(): lax.ppermute(value, axis, [(source, source ^ flip) for source in range(4)])  5.24 us
  transfers between devices with their start and end apart: 13, of which 5 were waited for; matrix products, arithmetic and copies ran while one was open for 0% of the time, Pallas kernels for 16%

profile of v7, /device:TPU:64, one launch (start us, length us, event | category | flops | bytes accessed | tf_op | source)
XLA Modules:
  0.0 109.8 jit_solution(13570007317271570657)
XLA Ops:
  1.6 1.8 %collective-permute-start = (bf16[280,512]{1,0:T(8,128)(2,1)S(1)}, bf16[280,512]{1,0:T(8,128)(2,1)S(1)}, u32[]{:S(2)}, u32[]{:S(2)}) collective-permute-start(bf16[280,512]{1,0:T(8,128)(2,1)S(1)} %pack.1.packed), channel_id=1, source_target_pairs={{0,16},{16,32},{32,48},{48,64},{64,80},{80,96},{96,112},{112,128},... | collective-permute-start | bytes 860168 | tf_op jit(solution)/shard_map/ppermute | solution.py:425
  3.4 3.7 %early.1 = (f32[136,512]{1,0:T(8,128)S(1)}, f32[136,512]{1,0:T(8,128)S(1)}, bf16[136,512]{1,0:T(8,128)(2,1)S(1)}, f32[3,8,512]{2,1,0:T(8,128)S(1)}, f32[3,3,512]...) custom-call(bf16[280,512]{1,0:T(8,128)(2,1)S(1)} %pack.1.packed, ...), custom_call_target="tpu_custom_call" | custom-call | flops 6000000000 | bytes 2000000 | tf_op jit(solution)/shard_map/early/pallas_call | solution.py:105
  7.2 7.3 %all-to-all-start = ((bf16[8,2,136,128]{3,2,1,0:T(8,128)(2,1)}), bf16[8,2,136,128]{3,2,1,0:T(8,128)(2,1)S(1)}, u32[]{:S(2)}, u32[]{:S(2)}) async-start(bf16[8,2,136,128]{3,2,1,0:T(8,128)(2,1)} %bitcast.8), calls=%async_computation | async-start | bytes 1114112 | tf_op jit(solution)/shard_map/all_to_all | solution.py:399
  14.5 3.3 %late.1 = (bf16[136,512]{1,0:T(8,128)(2,1)}, f32[8,136]{1,0:T(8,128)S(1)}) custom-call(bf16[280,512]{1,0:T(8,128)(2,1)S(1)} %collective-permute-done.halo, f32[136,512]{1,0:T(8,128)S(1)} %get-tuple-element.17.partial, f32[136,512]{1,0:T(8,128)S(1)} %get-tuple-element.18.feat, bf16[136,512]{1,0:T(8,128)(2,1)S(1)} %get-tuple-element.19.res, ...), custom_call_target="tpu_custom_call" | custom-call | flops 30000001024 | bytes 2000000 | tf_op jit(solution)/shard_map/late/pallas_call | solution.py:177
  17.7 4.7 %collective-permute-start.6 = (f32[8,136]{1,0:T(8,128)S(1)}, f32[8,136]{1,0:T(8,128)S(1)}, u32[]{:S(2)}, u32[]{:S(2)}) collective-permute-start(f32[8,136]{1,0:T(8,128)S(1)} %get-tuple-element.26), channel_id=1, source_target_pairs={{0,12},{4,8},{8,4},{12,0},{1,13},{5,9},{9,5},{13,1},{2,14},{6,10},... | collective-permute-start | bytes 13064 | tf_op jit(solution)/shard_map/ppermute | solution.py:404
  22.4 2.7 %collective-permute-start.5 = (f32[8,136]{1,0:T(8,128)S(1)}, f32[8,136]{1,0:T(8,128)S(1)}, u32[]{:S(2)}, u32[]{:S(2)}) collective-permute-start(f32[8,136]{1,0:T(8,128)S(1)} %get-tuple-element.26), channel_id=1, source_target_pairs={{0,8},{4,12},{8,0},{12,4},{1,9},{5,13},{9,1},{13,5},{2,10},{6,14},... | collective-permute-start | bytes 13064 | tf_op jit(solution)/shard_map/ppermute | solution.py:404
  25.1 2.4 %collective-permute-start.4 = (f32[8,136]{1,0:T(8,128)S(1)}, f32[8,136]{1,0:T(8,128)S(1)}, u32[]{:S(2)}, u32[]{:S(2)}) collective-permute-start(f32[8,136]{1,0:T(8,128)S(1)} %get-tuple-element.26), channel_id=1, source_target_pairs={{0,4},{4,0},{8,12},{12,8},{1,5},{5,1},{9,13},{13,9},{2,6},{6,2},{1... | collective-permute-start | bytes 13064 | tf_op jit(solution)/shard_map/ppermute | solution.py:404
  27.6 1.9 %collective-permute-done.5 = f32[8,136]{1,0:T(8,128)S(1)} collective-permute-done((f32[8,136]{1,0:T(8,128)S(1)}, f32[8,136]{1,0:T(8,128)S(1)}, u32[]{:S(2)}, u32[]{:S(2)}) %collective-permute-start.5) | collective-permute-done | bytes 4384 | tf_op jit(solution)/shard_map/ppermute | solution.py:404
  29.4 1.2 %collective-permute-done.4 = f32[8,136]{1,0:T(8,128)S(1)} collective-permute-done((f32[8,136]{1,0:T(8,128)S(1)}, f32[8,136]{1,0:T(8,128)S(1)}, u32[]{:S(2)}, u32[]{:S(2)}) %collective-permute-start.4) | collective-permute-done | bytes 4384 | tf_op jit(solution)/shard_map/ppermute | solution.py:404
  30.7 4.3 %collective-permute-start.9 = (f32[8,136]{1,0:T(8,128)S(1)}, f32[8,136]{1,0:T(8,128)S(1)}, u32[]{:S(2)}, u32[]{:S(2)}) collective-permute-start(f32[8,136]{1,0:T(8,128)S(1)} %add_add_fusion.part0), channel_id=1, source_target_pairs={{0,3},{1,2},{2,1},{3,0},{4,7},{5,6},{6,5},{7,4},{8,11},{9,10},{10,... | collective-permute-start | bytes 13064 | tf_op jit(solution)/shard_map/ppermute | solution.py:404
  34.9 3.7 %collective-permute-start.8 = (f32[8,136]{1,0:T(8,128)S(1)}, f32[8,136]{1,0:T(8,128)S(1)}, u32[]{:S(2)}, u32[]{:S(2)}) collective-permute-start(f32[8,136]{1,0:T(8,128)S(1)} %add_add_fusion.part0), channel_id=1, source_target_pairs={{0,2},{1,3},{2,0},{3,1},{4,6},{5,7},{6,4},{7,5},{8,10},{9,11},{10,... | collective-permute-start | bytes 13064 | tf_op jit(solution)/shard_map/ppermute | solution.py:404
  38.7 3.4 %collective-permute-start.7 = (f32[8,136]{1,0:T(8,128)S(1)}, f32[8,136]{1,0:T(8,128)S(1)}, u32[]{:S(2)}, u32[]{:S(2)}) collective-permute-start(f32[8,136]{1,0:T(8,128)S(1)} %add_add_fusion.part0), channel_id=1, source_target_pairs={{0,1},{1,0},{2,3},{3,2},{4,5},{5,4},{6,7},{7,6},{8,9},{9,8},{10,11... | collective-permute-start | bytes 13064 | tf_op jit(solution)/shard_map/ppermute | solution.py:404
  42.1 2.1 %collective-permute-done.7.part1 = f32[8,136]{1,0:T(8,128)S(1)} collective-permute-done((f32[8,136]{1,0:T(8,128)S(1)}, f32[8,136]{1,0:T(8,128)S(1)}, u32[]{:S(2)}, u32[]{:S(2)}) %collective-permute-start.7) | collective-permute-done | bytes 4384 | tf_op jit(solution)/shard_map/ppermute | solution.py:404
  44.2 2.1 %normalize.1 = bf16[4,4,136,128]{3,2,1,0:T(8,128)(2,1)} custom-call(f32[8,136]{1,0:T(8,128)S(1)} %add_add_fusion.part0, f32[8,136]{1,0:T(8,128)S(1)} %collective-permute-done.7.part1, f32[8,136]{1,0:T(8,128)S(1)} %collective-permute-done.8.part2, f32[8,136]{1,0:T(8,128)S(1)} %collective-permute-done.9.part3, bf16[136,512]{1,0:T(8,128)(2,1)} %get-tuple-element.15.stream, ...), custom_call_target="tpu_custom_call" | custom-call | flops 1000000 | bytes 800000 | tf_op jit(solution)/shard_map/normalize/pallas_call | solution.py:245
  46.3 13.6 %all-to-all-start.1 = ((bf16[16,136,128]{2,1,0:T(8,128)(2,1)}), bf16[16,136,128]{2,1,0:T(8,128)(2,1)S(1)}, u32[]{:S(2)}, u32[]{:S(2)}) async-start(bf16[16,136,128]{2,1,0:T(8,128)(2,1)} %bitcast.16), calls=%async_computation.1 | async-start | bytes 1114112 | tf_op jit(solution)/shard_map/all_to_all | solution.py:399
  59.9 7.8 %collective-permute-start.2 = (bf16[8,136,128]{2,1,0:T(8,128)(2,1)S(1)}, bf16[8,136,128]{2,1,0:T(8,128)(2,1)S(1)}, u32[]{:S(2)}, u32[]{:S(2)}) collective-permute-start(bf16[8,136,128]{2,1,0:T(8,128)(2,1)S(1)} %get-tuple-element.32), channel_id=1, source_target_pairs={{0,256},{1,257},{2,258},{3,259},{4,260},{5,261},{6,262},{7,263},{8... | collective-permute-start | bytes 835592 | tf_op jit(solution)/shard_map/ppermute | solution.py:438
  67.8 1.9 %collective-permute-start.1 = (bf16[8,136,128]{2,1,0:T(8,128)(2,1)S(1)}, bf16[8,136,128]{2,1,0:T(8,128)(2,1)S(1)}, u32[]{:S(2)}, u32[]{:S(2)}) collective-permute-start(bf16[8,136,128]{2,1,0:T(8,128)(2,1)S(1)} %get-tuple-element.32), channel_id=1, source_target_pairs={{0,16},{16,0},{1,17},{17,1},{2,18},{18,2},{3,19},{19,3},{4,20},{20... | collective-permute-start | bytes 835592 | tf_op jit(solution)/shard_map/ppermute | solution.py:409
  69.7 13.6 %collective-permute-done.2 = bf16[8,136,128]{2,1,0:T(8,128)(2,1)S(1)} collective-permute-done((bf16[8,136,128]{2,1,0:T(8,128)(2,1)S(1)}, bf16[8,136,128]{2,1,0:T(8,128)(2,1)S(1)}, u32[]{:S(2)}, u32[]{:S(2)}) %collective-permute-start.2) | collective-permute-done | bytes 278560 | tf_op jit(solution)/shard_map/ppermute | solution.py:438
  83.4 1.9 %collective-permute-start.3 = (bf16[8,136,128]{2,1,0:T(8,128)(2,1)S(1)}, bf16[8,136,128]{2,1,0:T(8,128)(2,1)S(1)}, u32[]{:S(2)}, u32[]{:S(2)}) collective-permute-start(bf16[8,136,128]{2,1,0:T(8,128)(2,1)S(1)} %collective-permute-done.2), channel_id=1, source_target_pairs={{0,16},{16,0},{1,17},{17,1},{2,18},{18,2},{3,19},{19,3},{4,20},{20... | collective-permute-start | bytes 835592 | tf_op jit(solution)/shard_map/ppermute | solution.py:409
  85.3 1.5 %collective-permute-done.3 = bf16[8,136,128]{2,1,0:T(8,128)(2,1)S(1)} collective-permute-done((bf16[8,136,128]{2,1,0:T(8,128)(2,1)S(1)}, bf16[8,136,128]{2,1,0:T(8,128)(2,1)S(1)}, u32[]{:S(2)}, u32[]{:S(2)}) %collective-permute-start.3) | collective-permute-done | bytes 278560 | tf_op jit(solution)/shard_map/ppermute | solution.py:409
  86.8 5.4 %score.1 = (bf16[544,4352]{1,0:T(8,128)(2,1)}, f32[544,128]{1,0:T(8,128)S(1)}) custom-call(s32[8]{0:T(128)S(1)} %broadcast_multiply_fusion.place, bf16[544,128]{1,0:T(8,128)(2,1)S(1)} %bitcast.31, bf16[1088,128]{1,0:T(8,128)(2,1)S(1)} %bitcast.30, bf16[1088,128]{1,0:T(8,128)(2,1)S(1)} %bitcast.34, bf16[1088,128]{1,0:T(8,128)(2,1)S(1)} %bitcast.33, ...), custom_call_target="tpu_custom_call" | custom-call | flops 606076928 | bytes 8000000 | tf_op jit(solution)/shard_map/score/pallas_call | solution.py:311
  92.2 2.0 %collective-permute-start.10 = (bf16[16,136,128]{2,1,0:T(8,128)(2,1)S(1)}, bf16[16,136,128]{2,1,0:T(8,128)(2,1)S(1)}, u32[]{:S(2)}, u32[]{:S(2)}) collective-permute-start(bf16[16,136,128]{2,1,0:T(8,128)(2,1)S(1)} %all-to-all-done.1), channel_id=1, source_target_pairs={{0,16},{16,0},{1,17},{17,1},{2,18},{18,2},{3,19},{19,3},{4,20},{20... | collective-permute-start | bytes 1671176 | tf_op jit(solution)/shard_map/ppermute | solution.py:409
  94.3 3.3 %attend_own.1 = (f32[544,128]{1,0:T(8,128)S(1)}, bf16[544,2176]{1,0:T(8,128)(2,1)S(1)}) custom-call(bf16[544,4352]{1,0:T(8,128)(2,1)} %get-tuple-element.25.weights_in, bf16[2176,128]{1,0:T(8,128)(2,1)S(1)} %bitcast.27), custom_call_target="tpu_custom_call" | custom-call | flops 303038464 | bytes 5500000 | tf_op jit(solution)/shard_map/attend_own/pallas_call | solution.py:365
  98.4 10.7 %all_to_all.15 = bf16[4,136,128]{2,1,0:T(8,128)(2,1)S(1)} all-to-all(bf16[4,136,128]{2,1,0:T(8,128)(2,1)S(1)} %bitcast.29), channel_id=1, replica_groups=mesh['zh'=2,'s'=2,'h'=4,'c'=2,'x'=4,'zl'=4] {'h'}, dimensions={0} | all-to-all | bytes 278528 | tf_op jit(solution)/shard_map/all_to_all | solution.py:399
  (18 shorter events, 2.7 us)
Async XLA Ops:
  1.6 12.8 %collective-permute-start = (bf16[280,512]{1,0:T(8,128)(2,1)S(1)}, bf16[280,512]{1,0:T(8,128)(2,1)S(1)}, u32[]{:S(2)}, u32[]{:S(2)}) collective-permute-start(bf16[280,512]{1,0:T(8,128)(2,1)S(1)} %pack.1.packed), channel_id=1, source_target_pairs={{0,16},{16,32},{32,48},{48,64},{64,80},{80,96},{96,112},{112,128},... | collective-permute-start | bytes 860168 | tf_op jit(solution)/shard_map/ppermute | solution.py:425
  7.2 39.1 %all-to-all-start = ((bf16[8,2,136,128]{3,2,1,0:T(8,128)(2,1)}), bf16[8,2,136,128]{3,2,1,0:T(8,128)(2,1)S(1)}, u32[]{:S(2)}, u32[]{:S(2)}) async-start(bf16[8,2,136,128]{3,2,1,0:T(8,128)(2,1)} %bitcast.8), calls=%async_computation | async-start | bytes 1114112 | tf_op jit(solution)/shard_map/all_to_all | solution.py:399
  14.4 29.8 %copy-start = (f32[512]{0:T(512)S(1)}, f32[512]{0:T(512)}, u32[]{:S(2)}) copy-start(f32[512]{0:T(512)} %param.15) | copy-start | bytes 6148
  17.7 9.8 %collective-permute-start.6 = (f32[8,136]{1,0:T(8,128)S(1)}, f32[8,136]{1,0:T(8,128)S(1)}, u32[]{:S(2)}, u32[]{:S(2)}) collective-permute-start(f32[8,136]{1,0:T(8,128)S(1)} %get-tuple-element.26), channel_id=1, source_target_pairs={{0,12},{4,8},{8,4},{12,0},{1,13},{5,9},{9,5},{13,1},{2,14},{6,10},... | collective-permute-start | bytes 13064 | tf_op jit(solution)/shard_map/ppermute | solution.py:404
  22.4 7.0 %collective-permute-start.5 = (f32[8,136]{1,0:T(8,128)S(1)}, f32[8,136]{1,0:T(8,128)S(1)}, u32[]{:S(2)}, u32[]{:S(2)}) collective-permute-start(f32[8,136]{1,0:T(8,128)S(1)} %get-tuple-element.26), channel_id=1, source_target_pairs={{0,8},{4,12},{8,0},{12,4},{1,9},{5,13},{9,1},{13,5},{2,10},{6,14},... | collective-permute-start | bytes 13064 | tf_op jit(solution)/shard_map/ppermute | solution.py:404
  25.1 5.5 %collective-permute-start.4 = (f32[8,136]{1,0:T(8,128)S(1)}, f32[8,136]{1,0:T(8,128)S(1)}, u32[]{:S(2)}, u32[]{:S(2)}) collective-permute-start(f32[8,136]{1,0:T(8,128)S(1)} %get-tuple-element.26), channel_id=1, source_target_pairs={{0,4},{4,0},{8,12},{12,8},{1,5},{5,1},{9,13},{13,9},{2,6},{6,2},{1... | collective-permute-start | bytes 13064 | tf_op jit(solution)/shard_map/ppermute | solution.py:404
  30.7 11.4 %collective-permute-start.9 = (f32[8,136]{1,0:T(8,128)S(1)}, f32[8,136]{1,0:T(8,128)S(1)}, u32[]{:S(2)}, u32[]{:S(2)}) collective-permute-start(f32[8,136]{1,0:T(8,128)S(1)} %add_add_fusion.part0), channel_id=1, source_target_pairs={{0,3},{1,2},{2,1},{3,0},{4,7},{5,6},{6,5},{7,4},{8,11},{9,10},{10,... | collective-permute-start | bytes 13064 | tf_op jit(solution)/shard_map/ppermute | solution.py:404
  34.9 7.1 %collective-permute-start.8 = (f32[8,136]{1,0:T(8,128)S(1)}, f32[8,136]{1,0:T(8,128)S(1)}, u32[]{:S(2)}, u32[]{:S(2)}) collective-permute-start(f32[8,136]{1,0:T(8,128)S(1)} %add_add_fusion.part0), channel_id=1, source_target_pairs={{0,2},{1,3},{2,0},{3,1},{4,6},{5,7},{6,4},{7,5},{8,10},{9,11},{10,... | collective-permute-start | bytes 13064 | tf_op jit(solution)/shard_map/ppermute | solution.py:404
  38.7 5.5 %collective-permute-start.7 = (f32[8,136]{1,0:T(8,128)S(1)}, f32[8,136]{1,0:T(8,128)S(1)}, u32[]{:S(2)}, u32[]{:S(2)}) collective-permute-start(f32[8,136]{1,0:T(8,128)S(1)} %add_add_fusion.part0), channel_id=1, source_target_pairs={{0,1},{1,0},{2,3},{3,2},{4,5},{5,4},{6,7},{7,6},{8,9},{9,8},{10,11... | collective-permute-start | bytes 13064 | tf_op jit(solution)/shard_map/ppermute | solution.py:404
  46.3 45.9 %all-to-all-start.1 = ((bf16[16,136,128]{2,1,0:T(8,128)(2,1)}), bf16[16,136,128]{2,1,0:T(8,128)(2,1)S(1)}, u32[]{:S(2)}, u32[]{:S(2)}) async-start(bf16[16,136,128]{2,1,0:T(8,128)(2,1)} %bitcast.16), calls=%async_computation.1 | async-start | bytes 1114112 | tf_op jit(solution)/shard_map/all_to_all | solution.py:399
  59.9 23.4 %collective-permute-start.2 = (bf16[8,136,128]{2,1,0:T(8,128)(2,1)S(1)}, bf16[8,136,128]{2,1,0:T(8,128)(2,1)S(1)}, u32[]{:S(2)}, u32[]{:S(2)}) collective-permute-start(bf16[8,136,128]{2,1,0:T(8,128)(2,1)S(1)} %get-tuple-element.32), channel_id=1, source_target_pairs={{0,256},{1,257},{2,258},{3,259},{4,260},{5,261},{6,262},{7,263},{8... | collective-permute-start | bytes 835592 | tf_op jit(solution)/shard_map/ppermute | solution.py:438
  67.8 17.5 %collective-permute-start.1 = (bf16[8,136,128]{2,1,0:T(8,128)(2,1)S(1)}, bf16[8,136,128]{2,1,0:T(8,128)(2,1)S(1)}, u32[]{:S(2)}, u32[]{:S(2)}) collective-permute-start(bf16[8,136,128]{2,1,0:T(8,128)(2,1)S(1)} %get-tuple-element.32), channel_id=1, source_target_pairs={{0,16},{16,0},{1,17},{17,1},{2,18},{18,2},{3,19},{19,3},{4,20},{20... | collective-permute-start | bytes 835592 | tf_op jit(solution)/shard_map/ppermute | solution.py:409
  83.4 3.4 %collective-permute-start.3 = (bf16[8,136,128]{2,1,0:T(8,128)(2,1)S(1)}, bf16[8,136,128]{2,1,0:T(8,128)(2,1)S(1)}, u32[]{:S(2)}, u32[]{:S(2)}) collective-permute-start(bf16[8,136,128]{2,1,0:T(8,128)(2,1)S(1)} %collective-permute-done.2), channel_id=1, source_target_pairs={{0,16},{16,0},{1,17},{17,1},{2,18},{18,2},{3,19},{19,3},{4,20},{20... | collective-permute-start | bytes 835592 | tf_op jit(solution)/shard_map/ppermute | solution.py:409
  92.2 5.4 %collective-permute-start.10 = (bf16[16,136,128]{2,1,0:T(8,128)(2,1)S(1)}, bf16[16,136,128]{2,1,0:T(8,128)(2,1)S(1)}, u32[]{:S(2)}, u32[]{:S(2)}) collective-permute-start(bf16[16,136,128]{2,1,0:T(8,128)(2,1)S(1)} %all-to-all-done.1), channel_id=1, source_target_pairs={{0,16},{16,0},{1,17},{17,1},{2,18},{18,2},{3,19},{19,3},{4,20},{20... | collective-permute-start | bytes 1671176 | tf_op jit(solution)/shard_map/ppermute | solution.py:409

commit v8 on v7

--- a/solution.py
+++ b/solution.py
@@ -46,22 +46,15 @@
 
 
 def early_kernel(
-    packed, gs, res, taps_in, long_in, keys, queries, partial, feat, res_out, edge, taps_out, long_out, blocks,
+    packed, gs, res, taps_in, long_in, partial, feat, res_out, edge, taps_out, long_out,
     gs_v, ext, prod, copies, sems,
 ):
     rows, chans = gs.shape
     loads = [(taps_in, taps_out), (long_in, long_out), (gs, gs_v), (res, res_out)]
     moves = [pltpu.make_async_copy(src, dst, sems.at[i]) for i, (src, dst) in enumerate(loads)]
-    first = len(moves)
-    for copy in range(blocks.shape[0]):
-        for head in range(blocks.shape[1]):
-            for kind, source in enumerate((keys, queries)):
-                src = source.at[:, head * HD : (head + 1) * HD]
-                dst = blocks.at[copy, head, kind]
-                moves.append(pltpu.make_async_copy(src, dst, sems.at[len(moves)]))
     for move in moves:
         move.start()
-    for move in moves[:first]:
+    for move in moves:
         move.wait()
     tiles = rows // 8
     pairs = [(tile, group) for group in range(long_in.shape[0] // 8) for tile in range(group, tiles)]
@@ -89,23 +82,20 @@
         return carry
 
     lax.fori_loop(0, chans // HD, one_head, 0)
-    for move in moves[first:]:
-        move.wait()
 
 
 def in_hbm(*arrays):
     return [pltpu.with_memory_space_constraint(array, pltpu.HBM) for array in arrays]
 
 
-def early(packed, gs, res, taps, long_taps, keys, queries):
+def early(packed, gs, res, taps, long_taps):
     rows, chans = gs.shape
-    heads = chans // HD
     hbm = pl.BlockSpec(memory_space=pltpu.HBM)
     vmem = pl.BlockSpec(memory_space=pltpu.VMEM)
     return pl.pallas_call(
         early_kernel,
-        in_specs=[vmem] + [hbm] * 6,
-        out_specs=[vmem] * 7,
+        in_specs=[vmem] + [hbm] * 4,
+        out_specs=[vmem] * 6,
         out_shape=[
             jax.ShapeDtypeStruct((rows, chans), jnp.float32),
             jax.ShapeDtypeStruct((rows, chans), jnp.float32),
@@ -113,19 +103,18 @@
             jax.ShapeDtypeStruct((3, 8, chans), jnp.float32),
             jax.ShapeDtypeStruct(taps.shape, jnp.float32),
             jax.ShapeDtypeStruct(long_taps.shape, jnp.bfloat16),
-            jax.ShapeDtypeStruct((2, heads, 2, rows, HD), jnp.bfloat16),
         ],
         scratch_shapes=[
             pltpu.VMEM((rows, chans), jnp.bfloat16),
             pltpu.VMEM((rows + 8, HD), jnp.float32),
             pltpu.VMEM((rows + 8, HD), jnp.float32),
             pltpu.VMEM((8, rows + 8, HD), jnp.float32),
-            pltpu.SemaphoreType.DMA((4 + 4 * heads,)),
+            pltpu.SemaphoreType.DMA((4,)),
         ],
         compiler_params=pltpu.CompilerParams(vmem_limit_bytes=32 << 20),
-        cost_estimate=pl.CostEstimate(flops=6_000_000_000, bytes_accessed=2_000_000, transcendentals=0),
+        cost_estimate=pl.CostEstimate(flops=20_000_000, bytes_accessed=2_000_000, transcendentals=0),
         name="early",
-    )(packed, *in_hbm(gs, res, taps, long_taps, keys, queries))
+    )(packed, *in_hbm(gs, res, taps, long_taps))
 
 
 def late_kernel(halo, partial, feat, res, edge, taps_in, long_in, stream, squares, ext, prod, copies):
@@ -168,7 +157,8 @@
         return total
 
     total = lax.fori_loop(0, chans // HD, one_head, total)
-    squares[...] = total
+    for peer in range(squares.shape[0]):
+        squares[peer] = total[0:1, :]
 
 
 def late(halo, partial, feat, res, edge, taps, long_taps):
@@ -180,7 +170,7 @@
         out_specs=[vmem] * 2,
         out_shape=[
             jax.ShapeDtypeStruct((rows, chans), jnp.bfloat16),
-            jax.ShapeDtypeStruct((8, rows), jnp.float32),
+            jax.ShapeDtypeStruct((16, 1, rows), jnp.float32),
         ],
         scratch_shapes=[
             pltpu.VMEM((rows + 8, HD), jnp.float32),
@@ -193,36 +183,59 @@
     )(halo, partial, feat, res, edge, taps, long_taps)
 
 
-def pack_kernel(gf, hv, gs, halo, sems):
+def pack_kernel(gf, hv, gs, keys, queries, halo, blocks, whole, sems):
     rows = gf.shape[0]
     pairs = [
+        (keys, whole.at[0]),
+        (queries, whole.at[1]),
         (gf, halo.at[0:rows]),
         (hv, halo.at[rows : 2 * rows]),
         (gs.at[rows - 8 : rows], halo.at[2 * rows : 2 * rows + 8]),
     ]
+    for kind in range(2):
+        for copy in range(blocks.shape[0]):
+            for head in range(blocks.shape[1]):
+                src = whole.at[kind, :, head * HD : (head + 1) * HD]
+                pairs.append((src, blocks.at[copy, head, kind]))
     moves = [pltpu.make_async_copy(src, dst, sems.at[i]) for i, (src, dst) in enumerate(pairs)]
-    for move in moves:
+    half = (len(moves) - 5) // 2
+    for move in moves[:5]:
         move.start()
-    for move in moves:
+    moves[0].wait()
+    for move in moves[5 : 5 + half]:
+        move.start()
+    moves[1].wait()
+    for move in moves[5 + half :]:
+        move.start()
+    for move in moves[2:]:
         move.wait()
 
 
-def pack(gf, hv, gs):
+def pack(gf, hv, gs, keys, queries):
     rows, chans = gf.shape
+    heads = chans // HD
+    vmem = pl.BlockSpec(memory_space=pltpu.VMEM)
+    hbm = pl.BlockSpec(memory_space=pltpu.HBM)
     return pl.pallas_call(
         pack_kernel,
-        in_specs=[pl.BlockSpec(memory_space=pltpu.HBM)] * 3,
-        out_specs=pl.BlockSpec(memory_space=pltpu.VMEM),
-        out_shape=jax.ShapeDtypeStruct((2 * rows + 8, chans), jnp.bfloat16),
-        scratch_shapes=[pltpu.SemaphoreType.DMA((3,))],
+        in_specs=[hbm] * 5,
+        out_specs=[vmem, hbm],
+        out_shape=[
+            jax.ShapeDtypeStruct((2 * rows + 8, chans), jnp.bfloat16),
+            pltpu.HBM((2, heads, 2, rows, HD), jnp.bfloat16),
+        ],
+        scratch_shapes=[pltpu.VMEM((2, rows, chans), jnp.bfloat16), pltpu.SemaphoreType.DMA((4 * heads + 5,))],
         compiler_params=pltpu.CompilerParams(vmem_limit_bytes=16 << 20),
         cost_estimate=pl.CostEstimate(flops=0, bytes_accessed=600_000, transcendentals=0),
         name="pack",
-    )(*in_hbm(gf, hv, gs))
-
-
-def normalize_kernel(width, part0, part1, part2, part3, stream, gain, packed):
-    total = part0[...] + part1[...] + part2[...] + part3[...]
+    )(*in_hbm(gf, hv, gs, keys, queries))
+
+
+def normalize_kernel(width, gathered, stream, gain, packed):
+    total = gathered[0]
+    for peer in range(1, gathered.shape[0]):
+        total = total + gathered[peer]
+    total = jnp.broadcast_to(total, (8, total.shape[1]))
     total = lax.dot_general(
         jnp.where(lax.broadcasted_iota(jnp.int32, total.shape, 0) == 0, total, 0.0),
         jnp.ones((8, HD), jnp.float32),
@@ -239,18 +252,18 @@
             packed[copy, head] = value
 
 
-def normalize(width, parts, stream, gain):
+def normalize(width, gathered, stream, gain):
     rows, chans = stream.shape
     vmem = pl.BlockSpec(memory_space=pltpu.VMEM)
     return pl.pallas_call(
         functools.partial(normalize_kernel, width),
-        in_specs=[vmem] * 6,
+        in_specs=[vmem] * 3,
         out_specs=vmem,
         out_shape=jax.ShapeDtypeStruct((4, chans // HD, rows, HD), jnp.bfloat16),
         compiler_params=pltpu.CompilerParams(vmem_limit_bytes=8 << 20),
         cost_estimate=pl.CostEstimate(flops=1_000_000, bytes_accessed=800_000, transcendentals=20_000),
         name="normalize",
-    )(*parts, *in_hbm(stream), gain)
+    )(gathered, *in_hbm(stream), gain)
 
 
 def score_kernel(place, q, k0, k1, k2, k3, out, denom, keys, scores, weights, sems):
@@ -399,12 +412,6 @@
     return lax.all_to_all(value, axes, 0, 0, tiled=True)
 
 
-def three_others(value, axis):
-    return [
-        lax.ppermute(value, axis, [(source, source ^ flip) for source in range(4)]) for flip in range(1, 4)
-    ]
-
-
 def swap_cores(value):
     return lax.ppermute(value, "c", [(0, 1), (1, 0)])
 
@@ -421,21 +428,21 @@
     place = [core, 1 - core] + [group + owner * 2 for owner in range(heads)]
     place = (jnp.stack(place + [side * 8, (1 - side) * 8]) * rows).astype(jnp.int32)
 
-    last = pack(gate_first, hyena_value, gate_second)
+    last, blocks = pack(gate_first, hyena_value, gate_second, attn_keys, queries)
+    blocks = exchange(blocks.reshape(8, 2, rows, HD), ("s", "h"))
     halo = lax.ppermute(last, ROWS_AXES, [(source, source + 1) for source in range(count - 1)])
-    *early_parts, blocks = early(
-        last, gate_second, residual, short_taps, long_taps, attn_keys, queries
-    )
-    blocks = exchange(blocks.reshape(8, 2, rows, HD), ("s", "h"))
+    early_parts = early(last, gate_second, residual, short_taps, long_taps)
     stream, squares = late(halo, *early_parts)
-    squares = sum(three_others(squares, "x"), squares)
-    parts = [squares] + three_others(squares, "zl")
-    packed = normalize(width, parts, stream, norm_gain.reshape(1, chans))
-    values_own = exchange(packed.reshape(16, rows, HD), PEERS)
-
+
+    blocks, squares = lax.optimization_barrier((blocks, squares))
     keys_near = blocks[:, 0]
     my_queries = lax.dynamic_slice_in_dim(blocks, lax.axis_index("s") * heads, heads, 0)[:, 1]
     keys_far = lax.ppermute(keys_near, "zh", [(0, 1)])
+    gathered = exchange(squares, CHAN_AXES)
+    packed = normalize(width, gathered, stream, norm_gain.reshape(1, chans))
+    packed, keys_far = lax.optimization_barrier((packed, keys_far))
+    values_own = exchange(packed.reshape(16, rows, HD), PEERS)
+
     parts = [keys_near, swap_cores(keys_near), keys_far, swap_cores(keys_far)]
     weights, denom = score(
         place, my_queries.reshape(heads * rows, HD), [part.reshape(8 * rows, HD) for part in parts]

time: 110 us -> 101 us (0.918)
  the two profiles are of different devices: /device:TPU:64 before, /device:TPU:1 now
where the time goes in v8:
time: 101 us
  starting transfers between devices  39.3 us (39%)
  blocking collectives  25 us (25%)
  Pallas kernels  19.5 us (19%)
  waiting for transfers between devices  15.2 us (15%)
    all_to_all x2, blocking collectives, exchange(): return lax.all_to_all(value, axes, 0, 0, tiled=True)  25 us
    all_to_all x2, starting transfers between devices, exchange(): return lax.all_to_all(value, axes, 0, 0, tiled=True)  14.7 us
    all_to_all x2, waiting for transfers between devices, exchange(): return lax.all_to_all(value, axes, 0, 0, tiled=True)  13.7 us
    ppermute x3, starting transfers between devices, swap_cores(): return lax.ppermute(value, 'c', [(0, 1), (1, 0)])  10.6 us
    ppermute x1, starting transfers between devices, shards(): keys_far = lax.ppermute(keys_near, 'zh', [(0, 1)])  9.36 us
    pallas_call x1, Pallas kernels, score(): pl.pallas_call(score_kernel, in_specs=[pl.BlockSpec(memory_space=pltpu.SM...  5.38 us
    ppermute x1, starting transfers between devices, shards(): lax.ppermute(last, ROWS_AXES, [(source, source + 1) for source in range(c...  4.59 us
    pallas_call x1, Pallas kernels, attend_own(): pl.pallas_call(attend_own_kernel, in_specs=[pl.BlockSpec(memory_space=plt...  3.32 us
  transfers between devices with their start and end apart: 7, of which 3 were waited for; matrix products, arithmetic and copies ran while one was open for 0% of the time, Pallas kernels for 17%

profile of v8, /device:TPU:1, one launch (start us, length us, event | category | flops | bytes accessed | tf_op | source)
XLA Modules:
  0.0 100.6 jit_solution(16393215035653645371)
XLA Ops:
  0.6 1.9 %pack.1 = (bf16[280,512]{1,0:T(8,128)(2,1)S(1)}, bf16[2,4,2,136,128]{4,3,2,1,0:T(8,128)(2,1)}) custom-call(bf16[136,512]{1,0:T(8,128)(2,1)} %gf.1, bf16[136,512]{1,0:T(8,128)(2,1)} %hv.1, bf16[136,512]{1,0:T(8,128)(2,1)} %gs.3, bf16[136,512]{1,0:T(8,128)(2,1)} %keys.1, bf16[136,512]{1,0:T(8,128)(2,1)} %queries.1), custom_call_target="tpu_custom_call" | custom-call | bytes 600000 | tf_op jit(solution)/shard_map/pack/pallas_call | solution.py:219
  2.5 4.6 %collective-permute-start = (bf16[280,512]{1,0:T(8,128)(2,1)S(1)}, bf16[280,512]{1,0:T(8,128)(2,1)S(1)}, u32[]{:S(2)}, u32[]{:S(2)}) collective-permute-start(bf16[280,512]{1,0:T(8,128)(2,1)S(1)} %get-tuple-element.22.packed), channel_id=1, source_target_pairs={{0,16},{16,32},{32,48},{48,64},{64,80},{80,96},{96,112},{112,128},... | collective-permute-start | bytes 860168 | tf_op jit(solution)/shard_map/ppermute | solution.py:433
  7.1 11.1 %all-to-all-start = ((bf16[8,2,136,128]{3,2,1,0:T(8,128)(2,1)}), bf16[8,2,136,128]{3,2,1,0:T(8,128)(2,1)S(1)}, u32[]{:S(2)}, u32[]{:S(2)}) async-start(bf16[8,2,136,128]{3,2,1,0:T(8,128)(2,1)} %bitcast.36), calls=%async_computation | async-start | bytes 1114112 | tf_op jit(solution)/shard_map/all_to_all | solution.py:412
  18.3 2.8 %early.1 = (f32[136,512]{1,0:T(8,128)S(1)}, f32[136,512]{1,0:T(8,128)S(1)}, bf16[136,512]{1,0:T(8,128)(2,1)S(1)}, f32[3,8,512]{2,1,0:T(8,128)S(1)}, f32[3,3,512]...) custom-call(bf16[280,512]{1,0:T(8,128)(2,1)S(1)} %get-tuple-element.22.packed, bf16[136,512]{1,0:T(8,128)(2,1)} %gs.3, ...), custom_call_target="tpu_custom_call" | custom-call | flops 20000000 | bytes 2000000 | tf_op jit(solution)/shard_map/early/pallas_call | solution.py:95
  21.0 0.0 copy-start
  21.0 3.3 %late.1 = (bf16[136,512]{1,0:T(8,128)(2,1)}, f32[16,1,136]{2,1,0:T(1,128)S(1)}) custom-call(bf16[280,512]{1,0:T(8,128)(2,1)S(1)} %collective-permute-done.halo, f32[136,512]{1,0:T(8,128)S(1)} %get-tuple-element.23.partial, f32[136,512]{1,0:T(8,128)S(1)} %get-tuple-element.24.feat, bf16[136,512]{1,0:T(8,128)(2,1)S(1)} %get-tuple-element.25.res, ...), custom_call_target="tpu_custom_call" | custom-call | flops 30000001024 | bytes 2000000 | tf_op jit(solution)/shard_map/late/pallas_call | solution.py:167
  24.3 8.8 %all-to-all-done = bf16[8,2,136,128]{3,2,1,0:T(8,128)(2,1)S(1)} async-done(((bf16[8,2,136,128]{3,2,1,0:T(8,128)(2,1)}), bf16[8,2,136,128]{3,2,1,0:T(8,128)(2,1)S(1)}, u32[]{:S(2)}, u32[]{:S(2)}) %all-to-all-start) | async-done | bytes 557088 | tf_op jit(solution)/shard_map/all_to_all | solution.py:412
  33.1 0.1 slice_bitcast_fusion
  33.2 9.4 %collective-permute-start.2 = (bf16[8,136,128]{2,1,0:T(8,128)(2,1)S(1)}, bf16[8,136,128]{2,1,0:T(8,128)(2,1)S(1)}, u32[]{:S(2)}, u32[]{:S(2)}) collective-permute-start(bf16[8,136,128]{2,1,0:T(8,128)(2,1)S(1)} %get-tuple-element.42), channel_id=1, source_target_pairs={{0,256},{1,257},{2,258},{3,259},{4,260},{5,261},{6,262},{7,263},{8... | collective-permute-start | bytes 835592 | tf_op jit(solution)/shard_map/ppermute | solution.py:440
  42.6 15.8 %all_to_all.20.gathered = f32[16,1,136]{2,1,0:T(1,128)S(1)} all-to-all(f32[16,1,136]{2,1,0:T(1,128)S(1)} %get-tuple-element.33), channel_id=1, replica_groups=mesh['zh'=2,'s'=2,'h'=4,'c'=2,'x'=4,'zl'=4] {'x','zl'}, dimensions={0} | all-to-all | bytes 17408 | tf_op jit(solution)/shard_map/all_to_all | solution.py:412
  58.4 2.1 %normalize.1 = bf16[4,4,136,128]{3,2,1,0:T(8,128)(2,1)} custom-call(f32[16,1,136]{2,1,0:T(1,128)S(1)} %all_to_all.20.gathered, bf16[136,512]{1,0:T(8,128)(2,1)} %get-tuple-element.20.stream, f32[1,512]{1,0:T(1,128)S(1)} %bitcast.32), custom_call_target="tpu_custom_call" | custom-call | flops 1000000 | bytes 800000 | tf_op jit(solution)/shard_map/normalize/pallas_call | solution.py:258
  60.5 3.6 %all-to-all-start.2 = ((bf16[16,136,128]{2,1,0:T(8,128)(2,1)}), bf16[16,136,128]{2,1,0:T(8,128)(2,1)S(1)}, u32[]{:S(2)}, u32[]{:S(2)}) async-start(bf16[16,136,128]{2,1,0:T(8,128)(2,1)} %bitcast.16), calls=%async_computation.2 | async-start | bytes 1114112 | tf_op jit(solution)/shard_map/all_to_all | solution.py:412
  64.1 0.1 stack.35
  64.2 3.5 %collective-permute-start.1 = (bf16[8,136,128]{2,1,0:T(8,128)(2,1)S(1)}, bf16[8,136,128]{2,1,0:T(8,128)(2,1)S(1)}, u32[]{:S(2)}, u32[]{:S(2)}) collective-permute-start(bf16[8,136,128]{2,1,0:T(8,128)(2,1)S(1)} %get-tuple-element.42), channel_id=1, source_target_pairs={{0,16},{16,0},{1,17},{17,1},{2,18},{18,2},{3,19},{19,3},{4,20},{20... | collective-permute-start | bytes 835592 | tf_op jit(solution)/shard_map/ppermute | solution.py:416
  67.7 1.9 %collective-permute-start.3 = (bf16[8,136,128]{2,1,0:T(8,128)(2,1)S(1)}, bf16[8,136,128]{2,1,0:T(8,128)(2,1)S(1)}, u32[]{:S(2)}, u32[]{:S(2)}) collective-permute-start(bf16[8,136,128]{2,1,0:T(8,128)(2,1)S(1)} %collective-permute-done.2), channel_id=1, source_target_pairs={{0,16},{16,0},{1,17},{17,1},{2,18},{18,2},{3,19},{19,3},{4,20},{20... | collective-permute-start | bytes 835592 | tf_op jit(solution)/shard_map/ppermute | solution.py:416
  69.7 0.0 collective-permute-done.1
  69.7 1.5 %collective-permute-done.3 = bf16[8,136,128]{2,1,0:T(8,128)(2,1)S(1)} collective-permute-done((bf16[8,136,128]{2,1,0:T(8,128)(2,1)S(1)}, bf16[8,136,128]{2,1,0:T(8,128)(2,1)S(1)}, u32[]{:S(2)}, u32[]{:S(2)}) %collective-permute-start.3) | collective-permute-done | bytes 278560 | tf_op jit(solution)/shard_map/ppermute | solution.py:416
  71.2 5.4 %score.1 = (bf16[544,4352]{1,0:T(8,128)(2,1)}, f32[544,128]{1,0:T(8,128)S(1)}) custom-call(s32[8]{0:T(128)S(1)} %broadcast_multiply_fusion.place, bf16[544,128]{1,0:T(8,128)(2,1)S(1)} %bitcast.31, bf16[1088,128]{1,0:T(8,128)(2,1)S(1)} %bitcast.30, bf16[1088,128]{1,0:T(8,128)(2,1)S(1)} %bitcast.34, bf16[1088,128]{1,0:T(8,128)(2,1)S(1)} %bitcast.33, ...), custom_call_target="tpu_custom_call" | custom-call | flops 606076928 | bytes 8000000 | tf_op jit(solution)/shard_map/score/pallas_call | solution.py:324
  76.5 4.9 %all-to-all-done.2 = bf16[16,136,128]{2,1,0:T(8,128)(2,1)S(1)} async-done(((bf16[16,136,128]{2,1,0:T(8,128)(2,1)}), bf16[16,136,128]{2,1,0:T(8,128)(2,1)S(1)}, u32[]{:S(2)}, u32[]{:S(2)}) %all-to-all-start.2) | async-done | bytes 557088 | tf_op jit(solution)/shard_map/all_to_all | solution.py:412
  81.5 5.2 %collective-permute-start.4 = (bf16[16,136,128]{2,1,0:T(8,128)(2,1)S(1)}, bf16[16,136,128]{2,1,0:T(8,128)(2,1)S(1)}, u32[]{:S(2)}, u32[]{:S(2)}) collective-permute-start(bf16[16,136,128]{2,1,0:T(8,128)(2,1)S(1)} %all-to-all-done.2), channel_id=1, source_target_pairs={{0,16},{16,0},{1,17},{17,1},{2,18},{18,2},{3,19},{19,3},{4,20},{20... | collective-permute-start | bytes 1671176 | tf_op jit(solution)/shard_map/ppermute | solution.py:416
  86.7 3.3 %attend_own.1 = (f32[544,128]{1,0:T(8,128)S(1)}, bf16[544,2176]{1,0:T(8,128)(2,1)S(1)}) custom-call(bf16[544,4352]{1,0:T(8,128)(2,1)} %get-tuple-element.35.weights_in, bf16[2176,128]{1,0:T(8,128)(2,1)S(1)} %bitcast.27), custom_call_target="tpu_custom_call" | custom-call | flops 303038464 | bytes 5500000 | tf_op jit(solution)/shard_map/attend_own/pallas_call | solution.py:378
  90.0 0.8 attend_other.1
  90.8 9.1 %all_to_all.21 = bf16[4,136,128]{2,1,0:T(8,128)(2,1)S(1)} all-to-all(bf16[4,136,128]{2,1,0:T(8,128)(2,1)S(1)} %bitcast.29), channel_id=1, replica_groups=mesh['zh'=2,'s'=2,'h'=4,'c'=2,'x'=4,'zl'=4] {'h'}, dimensions={0} | all-to-all | bytes 278528 | tf_op jit(solution)/shard_map/all_to_all | solution.py:412
  99.9 0.7 copy_bitcast_fusion
  (6 shorter events, 0.0 us)
Async XLA Ops:
  2.5 18.5 %collective-permute-start = (bf16[280,512]{1,0:T(8,128)(2,1)S(1)}, bf16[280,512]{1,0:T(8,128)(2,1)S(1)}, u32[]{:S(2)}, u32[]{:S(2)}) collective-permute-start(bf16[280,512]{1,0:T(8,128)(2,1)S(1)} %get-tuple-element.22.packed), channel_id=1, source_target_pairs={{0,16},{16,32},{32,48},{48,64},{64,80},{80,96},{96,112},{112,128},... | collective-permute-start | bytes 860168 | tf_op jit(solution)/shard_map/ppermute | solution.py:433
  7.1 26.0 %all-to-all-start = ((bf16[8,2,136,128]{3,2,1,0:T(8,128)(2,1)}), bf16[8,2,136,128]{3,2,1,0:T(8,128)(2,1)S(1)}, u32[]{:S(2)}, u32[]{:S(2)}) async-start(bf16[8,2,136,128]{3,2,1,0:T(8,128)(2,1)} %bitcast.36), calls=%async_computation | async-start | bytes 1114112 | tf_op jit(solution)/shard_map/all_to_all | solution.py:412
  21.0 37.4 %copy-start = (f32[512]{0:T(512)S(1)}, f32[512]{0:T(512)}, u32[]{:S(2)}) copy-start(f32[512]{0:T(512)} %param.15) | copy-start | bytes 6148
  33.2 27.3 %collective-permute-start.2 = (bf16[8,136,128]{2,1,0:T(8,128)(2,1)S(1)}, bf16[8,136,128]{2,1,0:T(8,128)(2,1)S(1)}, u32[]{:S(2)}, u32[]{:S(2)}) collective-permute-start(bf16[8,136,128]{2,1,0:T(8,128)(2,1)S(1)} %get-tuple-element.42), channel_id=1, source_target_pairs={{0,256},{1,257},{2,258},{3,259},{4,260},{5,261},{6,262},{7,263},{8... | collective-permute-start | bytes 835592 | tf_op jit(solution)/shard_map/ppermute | solution.py:440
  60.5 21.0 %all-to-all-start.2 = ((bf16[16,136,128]{2,1,0:T(8,128)(2,1)}), bf16[16,136,128]{2,1,0:T(8,128)(2,1)S(1)}, u32[]{:S(2)}, u32[]{:S(2)}) async-start(bf16[16,136,128]{2,1,0:T(8,128)(2,1)} %bitcast.16), calls=%async_computation.2 | async-start | bytes 1114112 | tf_op jit(solution)/shard_map/all_to_all | solution.py:412
  64.2 5.5 %collective-permute-start.1 = (bf16[8,136,128]{2,1,0:T(8,128)(2,1)S(1)}, bf16[8,136,128]{2,1,0:T(8,128)(2,1)S(1)}, u32[]{:S(2)}, u32[]{:S(2)}) collective-permute-start(bf16[8,136,128]{2,1,0:T(8,128)(2,1)S(1)} %get-tuple-element.42), channel_id=1, source_target_pairs={{0,16},{16,0},{1,17},{17,1},{2,18},{18,2},{3,19},{19,3},{4,20},{20... | collective-permute-start | bytes 835592 | tf_op jit(solution)/shard_map/ppermute | solution.py:416
  67.7 3.5 %collective-permute-start.3 = (bf16[8,136,128]{2,1,0:T(8,128)(2,1)S(1)}, bf16[8,136,128]{2,1,0:T(8,128)(2,1)S(1)}, u32[]{:S(2)}, u32[]{:S(2)}) collective-permute-start(bf16[8,136,128]{2,1,0:T(8,128)(2,1)S(1)} %collective-permute-done.2), channel_id=1, source_target_pairs={{0,16},{16,0},{1,17},{17,1},{2,18},{18,2},{3,19},{19,3},{4,20},{20... | collective-permute-start | bytes 835592 | tf_op jit(solution)/shard_map/ppermute | solution.py:416
  81.5 8.5 %collective-permute-start.4 = (bf16[16,136,128]{2,1,0:T(8,128)(2,1)S(1)}, bf16[16,136,128]{2,1,0:T(8,128)(2,1)S(1)}, u32[]{:S(2)}, u32[]{:S(2)}) collective-permute-start(bf16[16,136,128]{2,1,0:T(8,128)(2,1)S(1)} %all-to-all-done.2), channel_id=1, source_target_pairs={{0,16},{16,0},{1,17},{17,1},{2,18},{18,2},{3,19},{19,3},{4,20},{20... | collective-permute-start | bytes 1671176 | tf_op jit(solution)/shard_map/ppermute | solution.py:416

commit v9 on v8

--- a/solution.py
+++ b/solution.py
@@ -11,7 +11,6 @@
 HD = 128
 ROWS_AXES = ("zh", "s", "h", "c")
 CHAN_AXES = ("x", "zl")
-PEERS = ("zh", "s", "h")
 HIGHEST = lax.Precision.HIGHEST
 
 
@@ -157,8 +156,7 @@
         return total
 
     total = lax.fori_loop(0, chans // HD, one_head, total)
-    for peer in range(squares.shape[0]):
-        squares[peer] = total[0:1, :]
+    squares[...] = total
 
 
 def late(halo, partial, feat, res, edge, taps, long_taps):
@@ -170,7 +168,7 @@
         out_specs=[vmem] * 2,
         out_shape=[
             jax.ShapeDtypeStruct((rows, chans), jnp.bfloat16),
-            jax.ShapeDtypeStruct((16, 1, rows), jnp.float32),
+            jax.ShapeDtypeStruct((8, rows), jnp.float32),
         ],
         scratch_shapes=[
             pltpu.VMEM((rows + 8, HD), jnp.float32),
@@ -231,7 +229,7 @@
     )(*in_hbm(gf, hv, gs, keys, queries))
 
 
-def normalize_kernel(width, gathered, stream, gain, packed):
+def normalize_kernel(width, gathered, near, far, gain, packed):
     total = gathered[0]
     for peer in range(1, gathered.shape[0]):
         total = total + gathered[peer]
@@ -244,26 +242,28 @@
         preferred_element_type=jnp.float32,
     )
     inverse = 1.0 / jnp.sqrt(total / width + 1e-06)
+    rows = near.shape[0]
     for head in range(packed.shape[1]):
         lanes = slice(head * HD, (head + 1) * HD)
-        value = stream[:, lanes].astype(jnp.float32) * inverse * gain[:, lanes]
-        value = value.astype(jnp.bfloat16)
-        for copy in range(packed.shape[0]):
-            packed[copy, head] = value
-
-
-def normalize(width, gathered, stream, gain):
-    rows, chans = stream.shape
+        for kind, ref in enumerate((near, far)):
+            scale = inverse[kind * rows : (kind + 1) * rows, :]
+            value = (ref[:, lanes].astype(jnp.float32) * scale * gain[:, lanes]).astype(jnp.bfloat16)
+            for copy in range(packed.shape[0]):
+                packed[copy, head, kind] = value
+
+
+def normalize(width, gathered, near, far, gain):
+    rows, chans = near.shape
     vmem = pl.BlockSpec(memory_space=pltpu.VMEM)
     return pl.pallas_call(
         functools.partial(normalize_kernel, width),
-        in_specs=[vmem] * 3,
+        in_specs=[vmem] * 4,
         out_specs=vmem,
-        out_shape=jax.ShapeDtypeStruct((4, chans // HD, rows, HD), jnp.bfloat16),
+        out_shape=jax.ShapeDtypeStruct((2, chans // HD, 2, rows, HD), jnp.bfloat16),
         compiler_params=pltpu.CompilerParams(vmem_limit_bytes=8 << 20),
         cost_estimate=pl.CostEstimate(flops=1_000_000, bytes_accessed=800_000, transcendentals=20_000),
         name="normalize",
-    )(gathered, *in_hbm(stream), gain)
+    )(gathered, *in_hbm(near), far, gain)
 
 
 def score_kernel(place, q, k0, k1, k2, k3, out, denom, keys, scores, weights, sems):
@@ -272,8 +272,9 @@
     block = scores.shape[0]
     unit = math.log2(math.e) / math.sqrt(HD)
     for part, ref in enumerate((k0, k1, k2, k3)):
-        begin = pl.multiple_of(place[6 + part // 2], 64)
-        keys[part % 2, pl.ds(begin, count // 2), :] = ref[...]
+        for peer in range(8):
+            begin = (peer * 2 + part // 2) * rows
+            keys[part % 2, begin : begin + rows, :] = ref[peer]
     chunks = [(begin, min(256, count - begin)) for begin in range(0, count, 256)]
     line = lax.broadcasted_iota(jnp.int32, (block, 1), 0)
     for index in range(q.shape[0] // block):
@@ -292,10 +293,11 @@
                     preferred_element_type=jnp.float32,
                 )
                 lane = begin + lax.broadcasted_iota(jnp.int32, (1, width), 1)
-                key_pos = place[part] + lane
-                for edge in range(rows, count, rows):
-                    if edge < begin + width:
-                        key_pos = key_pos + jnp.where(lane >= edge, rows, 0)
+                odd = begin // rows % 2
+                key_pos = lane + place[6 + 2 * part + odd]
+                for edge in range((begin // rows + 1) * rows, begin + width, rows):
+                    odd = 1 - odd
+                    key_pos = jnp.where(lane >= edge, lane + place[6 + 2 * part + odd], key_pos)
                 score = jnp.where(key_pos <= query_pos, score * unit, -1e30)
                 scores[:, part * count + begin : part * count + begin + width] = score
                 for piece in range(0, width, 128):
@@ -318,7 +320,7 @@
 
 def score(place, q, keys):
     lines = q.shape[0]
-    count = sum(part.shape[0] for part in keys)
+    count = sum(part.shape[0] * part.shape[1] for part in keys)
     block = lines // 2
     vmem = pl.BlockSpec(memory_space=pltpu.VMEM)
     return pl.pallas_call(
@@ -426,7 +428,9 @@
     side = lax.axis_index("zh")
     group = side * 16 + lax.axis_index("s") * 8 + core
     place = [core, 1 - core] + [group + owner * 2 for owner in range(heads)]
-    place = (jnp.stack(place + [side * 8, (1 - side) * 8]) * rows).astype(jnp.int32)
+    for sender in (core, 1 - core):
+        place += [sender + side * 16, sender - 1 + (1 - side) * 16]
+    place = (jnp.stack(place) * rows).astype(jnp.int32)
 
     last, blocks = pack(gate_first, hyena_value, gate_second, attn_keys, queries)
     blocks = exchange(blocks.reshape(8, 2, rows, HD), ("s", "h"))
@@ -434,19 +438,20 @@
     early_parts = early(last, gate_second, residual, short_taps, long_taps)
     stream, squares = late(halo, *early_parts)
 
-    blocks, squares = lax.optimization_barrier((blocks, squares))
+    far_stream, far_squares = [lax.ppermute(value, "zh", [(0, 1)]) for value in (stream, squares)]
+    squares = jnp.concatenate([squares[0:1], far_squares[0:1]], axis=1)
+    squares = jnp.broadcast_to(squares, (16, 1, 2 * rows))
+    blocks, squares, far_stream = lax.optimization_barrier((blocks, squares, far_stream))
+    gathered = exchange(squares, CHAN_AXES)
+    packed = normalize(width, gathered, stream, far_stream, norm_gain.reshape(1, chans))
+    blocks, packed = lax.optimization_barrier((blocks, packed))
+    values_own = exchange(packed.reshape(8, 2 * rows, HD), ("s", "h"))
+
     keys_near = blocks[:, 0]
     my_queries = lax.dynamic_slice_in_dim(blocks, lax.axis_index("s") * heads, heads, 0)[:, 1]
     keys_far = lax.ppermute(keys_near, "zh", [(0, 1)])
-    gathered = exchange(squares, CHAN_AXES)
-    packed = normalize(width, gathered, stream, norm_gain.reshape(1, chans))
-    packed, keys_far = lax.optimization_barrier((packed, keys_far))
-    values_own = exchange(packed.reshape(16, rows, HD), PEERS)
-
     parts = [keys_near, swap_cores(keys_near), keys_far, swap_cores(keys_far)]
-    weights, denom = score(
-        place, my_queries.reshape(heads * rows, HD), [part.reshape(8 * rows, HD) for part in parts]
-    )
+    weights, denom = score(place, my_queries.reshape(heads * rows, HD), parts)
     values_own, denom = lax.optimization_barrier((values_own, denom))
     values_other = swap_cores(values_own)
     result, weights_other = attend_own(weights, values_own.reshape(16 * rows, HD))

time: 101 us -> 103 us (1.020)
  the two profiles are of different devices: /device:TPU:1 before, /device:TPU:64 now
where the time goes in v9:
time: 103 us
  starting transfers between devices  48.9 us (47%)
  blocking collectives  23.6 us (23%)
  Pallas kernels  19.4 us (19%)
  waiting for transfers between devices  9 us (9%)
    all_to_all x2, blocking collectives, exchange(): return lax.all_to_all(value, axes, 0, 0, tiled=True)  23.6 us
    ppermute x2, starting transfers between devices, shards(): lax.ppermute(value, 'zh', [(0, 1)])  21.6 us
    all_to_all x2, starting transfers between devices, exchange(): return lax.all_to_all(value, axes, 0, 0, tiled=True)  10.8 us
    ppermute x1, starting transfers between devices, shards(): keys_far = lax.ppermute(keys_near, 'zh', [(0, 1)])  8.85 us
    ppermute x1, waiting for transfers between devices, shards(): keys_far = lax.ppermute(keys_near, 'zh', [(0, 1)])  5.89 us
    ppermute x3, starting transfers between devices, swap_cores(): return lax.ppermute(value, 'c', [(0, 1), (1, 0)])  5.87 us
    pallas_call x1, Pallas kernels, score(): pl.pallas_call(score_kernel, in_specs=[pl.BlockSpec(memory_space=pltpu.SM...  5.19 us
    pallas_call x1, Pallas kernels, attend_own(): pl.pallas_call(attend_own_kernel, in_specs=[pl.BlockSpec(memory_space=plt...  3.32 us
  transfers between devices with their start and end apart: 9, of which 3 were waited for; matrix products, arithmetic and copies ran while one was open for 0% of the time, Pallas kernels for 14%

profile of v9, /device:TPU:64, one launch (start us, length us, event | category | flops | bytes accessed | tf_op | source)
XLA Modules:
  0.0 102.7 jit_solution(12882307717064237024)
XLA Ops:
  0.6 1.9 %pack.1 = (bf16[280,512]{1,0:T(8,128)(2,1)S(1)}, bf16[2,4,2,136,128]{4,3,2,1,0:T(8,128)(2,1)}) custom-call(bf16[136,512]{1,0:T(8,128)(2,1)} %gf.1, bf16[136,512]{1,0:T(8,128)(2,1)} %hv.1, bf16[136,512]{1,0:T(8,128)(2,1)} %gs.3, bf16[136,512]{1,0:T(8,128)(2,1)} %keys.1, bf16[136,512]{1,0:T(8,128)(2,1)} %queries.1), custom_call_target="tpu_custom_call" | custom-call | bytes 600000 | tf_op jit(solution)/shard_map/pack/pallas_call | solution.py:217
  2.5 1.8 %collective-permute-start = (bf16[280,512]{1,0:T(8,128)(2,1)S(1)}, bf16[280,512]{1,0:T(8,128)(2,1)S(1)}, u32[]{:S(2)}, u32[]{:S(2)}) collective-permute-start(bf16[280,512]{1,0:T(8,128)(2,1)S(1)} %get-tuple-element.23.packed), channel_id=1, source_target_pairs={{0,16},{16,32},{32,48},{48,64},{64,80},{80,96},{96,112},{112,128},... | collective-permute-start | bytes 860168 | tf_op jit(solution)/shard_map/ppermute | solution.py:437
  4.3 7.3 %all-to-all-start = ((bf16[8,2,136,128]{3,2,1,0:T(8,128)(2,1)}), bf16[8,2,136,128]{3,2,1,0:T(8,128)(2,1)S(1)}, u32[]{:S(2)}, u32[]{:S(2)}) async-start(bf16[8,2,136,128]{3,2,1,0:T(8,128)(2,1)} %bitcast.30), calls=%async_computation | async-start | bytes 1114112 | tf_op jit(solution)/shard_map/all_to_all | solution.py:414
  11.6 2.8 %early.1 = (f32[136,512]{1,0:T(8,128)S(1)}, f32[136,512]{1,0:T(8,128)S(1)}, bf16[136,512]{1,0:T(8,128)(2,1)S(1)}, f32[3,8,512]{2,1,0:T(8,128)S(1)}, f32[3,3,512]...) custom-call(bf16[280,512]{1,0:T(8,128)(2,1)S(1)} %get-tuple-element.23.packed, bf16[136,512]{1,0:T(8,128)(2,1)} %gs.3, ...), custom_call_target="tpu_custom_call" | custom-call | flops 20000000 | bytes 2000000 | tf_op jit(solution)/shard_map/early/pallas_call | solution.py:94
  14.4 3.3 %late.1 = (bf16[136,512]{1,0:T(8,128)(2,1)}, f32[8,136]{1,0:T(8,128)S(1)}) custom-call(bf16[280,512]{1,0:T(8,128)(2,1)S(1)} %collective-permute-done.halo, f32[136,512]{1,0:T(8,128)S(1)} %get-tuple-element.24.partial, f32[136,512]{1,0:T(8,128)S(1)} %get-tuple-element.25.feat, bf16[136,512]{1,0:T(8,128)(2,1)S(1)} %get-tuple-element.26.res, ...), custom_call_target="tpu_custom_call" | custom-call | flops 30000001024 | bytes 2000000 | tf_op jit(solution)/shard_map/late/pallas_call | solution.py:165
  17.6 20.4 %collective-permute-start.2 = (bf16[136,512]{1,0:T(8,128)(2,1)}, bf16[136,512]{1,0:T(8,128)(2,1)S(1)}, u32[]{:S(2)}, u32[]{:S(2)}) collective-permute-start(bf16[136,512]{1,0:T(8,128)(2,1)} %get-tuple-element.21.near), channel_id=1, source_target_pairs={{0,256},{1,257},{2,258},{3,259},{4,260},{5,261},{6,262},{7,263},{8... | collective-permute-start | bytes 417800 | tf_op jit(solution)/shard_map/ppermute | solution.py:441
  38.0 1.3 %collective-permute-start.1 = (f32[8,136]{1,0:T(8,128)S(1)}, f32[8,136]{1,0:T(8,128)S(1)}, u32[]{:S(2)}, u32[]{:S(2)}) collective-permute-start(f32[8,136]{1,0:T(8,128)S(1)} %get-tuple-element.32), channel_id=1, source_target_pairs={{0,256},{1,257},{2,258},{3,259},{4,260},{5,261},{6,262},{7,263},{8... | collective-permute-start | bytes 13064 | tf_op jit(solution)/shard_map/ppermute | solution.py:441
  39.3 1.6 %collective-permute-done.1 = f32[8,136]{1,0:T(8,128)S(1)} collective-permute-done((f32[8,136]{1,0:T(8,128)S(1)}, f32[8,136]{1,0:T(8,128)S(1)}, u32[]{:S(2)}, u32[]{:S(2)}) %collective-permute-start.1) | collective-permute-done | bytes 4384 | tf_op jit(solution)/shard_map/ppermute | solution.py:441
  40.9 0.1 maximum_reduce_fusion
  41.1 12.1 %all_to_all.20.gathered = f32[16,1,272]{2,1,0:T(1,128)S(1)} all-to-all(f32[16,1,272]{2,1,0:T(1,128)S(1)} %broadcast_in_dim.3), channel_id=1, replica_groups=mesh['zh'=2,'s'=2,'h'=4,'c'=2,'x'=4,'zl'=4] {'x','zl'}, dimensions={0} | all-to-all | bytes 34816 | tf_op jit(solution)/shard_map/all_to_all | solution.py:414
  53.2 2.2 %normalize.1 = bf16[2,4,2,136,128]{4,3,2,1,0:T(8,128)(2,1)} custom-call(f32[16,1,272]{2,1,0:T(1,128)S(1)} %all_to_all.20.gathered, bf16[136,512]{1,0:T(8,128)(2,1)} %get-tuple-element.21.near, bf16[136,512]{1,0:T(8,128)(2,1)S(1)} %collective-permute-done.2.far, f32[1,512]{1,0:T(1,128)S(1)} %bitcast.29), custom_call_target="tpu_custom_call" | custom-call | flops 1000000 | bytes 800000 | tf_op jit(solution)/shard_map/normalize/pallas_call | solution.py:258
  55.3 3.5 %all-to-all-start.2 = ((bf16[8,272,128]{2,1,0:T(8,128)(2,1)}), bf16[8,272,128]{2,1,0:T(8,128)(2,1)S(1)}, u32[]{:S(2)}, u32[]{:S(2)}) async-start(bf16[8,272,128]{2,1,0:T(8,128)(2,1)} %bitcast.14), calls=%async_computation.2 | async-start | bytes 1114112 | tf_op jit(solution)/shard_map/all_to_all | solution.py:414
  58.9 8.8 %collective-permute-start.4 = (bf16[8,136,128]{2,1,0:T(8,128)(2,1)S(1)}, bf16[8,136,128]{2,1,0:T(8,128)(2,1)S(1)}, u32[]{:S(2)}, u32[]{:S(2)}) collective-permute-start(bf16[8,136,128]{2,1,0:T(8,128)(2,1)S(1)} %slice_bitcast_fusion.k0), channel_id=1, source_target_pairs={{0,256},{1,257},{2,258},{3,259},{4,260},{5,261},{6,262},{7,263},{8... | collective-permute-start | bytes 835592 | tf_op jit(solution)/shard_map/ppermute | solution.py:452
  67.8 0.1 stack.43
  67.9 1.9 %collective-permute-start.3 = (bf16[8,136,128]{2,1,0:T(8,128)(2,1)S(1)}, bf16[8,136,128]{2,1,0:T(8,128)(2,1)S(1)}, u32[]{:S(2)}, u32[]{:S(2)}) collective-permute-start(bf16[8,136,128]{2,1,0:T(8,128)(2,1)S(1)} %slice_bitcast_fusion.k0), channel_id=1, source_target_pairs={{0,16},{16,0},{1,17},{17,1},{2,18},{18,2},{3,19},{19,3},{4,20},{20... | collective-permute-start | bytes 835592 | tf_op jit(solution)/shard_map/ppermute | solution.py:418
  69.8 5.9 %collective-permute-done.4.k2 = bf16[8,136,128]{2,1,0:T(8,128)(2,1)S(1)} collective-permute-done((bf16[8,136,128]{2,1,0:T(8,128)(2,1)S(1)}, bf16[8,136,128]{2,1,0:T(8,128)(2,1)S(1)}, u32[]{:S(2)}, u32[]{:S(2)}) %collective-permute-start.4) | collective-permute-done | bytes 278560 | tf_op jit(solution)/shard_map/ppermute | solution.py:452
  75.7 1.9 %collective-permute-start.5 = (bf16[8,136,128]{2,1,0:T(8,128)(2,1)S(1)}, bf16[8,136,128]{2,1,0:T(8,128)(2,1)S(1)}, u32[]{:S(2)}, u32[]{:S(2)}) collective-permute-start(bf16[8,136,128]{2,1,0:T(8,128)(2,1)S(1)} %collective-permute-done.4.k2), channel_id=1, source_target_pairs={{0,16},{16,0},{1,17},{17,1},{2,18},{18,2},{3,19},{19,3},{4,20},{20... | collective-permute-start | bytes 835592 | tf_op jit(solution)/shard_map/ppermute | solution.py:418
  77.6 1.5 %collective-permute-done.5.k3 = bf16[8,136,128]{2,1,0:T(8,128)(2,1)S(1)} collective-permute-done((bf16[8,136,128]{2,1,0:T(8,128)(2,1)S(1)}, bf16[8,136,128]{2,1,0:T(8,128)(2,1)S(1)}, u32[]{:S(2)}, u32[]{:S(2)}) %collective-permute-start.5) | collective-permute-done | bytes 278560 | tf_op jit(solution)/shard_map/ppermute | solution.py:418
  79.1 5.2 %score.1 = (bf16[544,4352]{1,0:T(8,128)(2,1)}, f32[544,128]{1,0:T(8,128)S(1)}) custom-call(s32[10]{0:T(128)S(1)} %broadcast_multiply_fusion.place, bf16[544,128]{1,0:T(8,128)(2,1)S(1)} %bitcast.28, bf16[8,136,128]{2,1,0:T(8,128)(2,1)S(1)} %slice_bitcast_fusion.k0, bf16[8,136,128]{2,1,0:T(8,128)(2,1)S(1)} %collective-permute-done.3.k1, ...), custom_call_target="tpu_custom_call" | custom-call | flops 606076928 | bytes 8000000 | tf_op jit(solution)/shard_map/score/pallas_call | solution.py:326
  84.3 2.0 %collective-permute-start.6 = (bf16[8,272,128]{2,1,0:T(8,128)(2,1)S(1)}, bf16[8,272,128]{2,1,0:T(8,128)(2,1)S(1)}, u32[]{:S(2)}, u32[]{:S(2)}) collective-permute-start(bf16[8,272,128]{2,1,0:T(8,128)(2,1)S(1)} %all-to-all-done.2), channel_id=1, source_target_pairs={{0,16},{16,0},{1,17},{17,1},{2,18},{18,2},{3,19},{19,3},{4,20},{20... | collective-permute-start | bytes 1671176 | tf_op jit(solution)/shard_map/ppermute | solution.py:418
  86.4 3.3 %attend_own.1 = (f32[544,128]{1,0:T(8,128)S(1)}, bf16[544,2176]{1,0:T(8,128)(2,1)S(1)}) custom-call(bf16[544,4352]{1,0:T(8,128)(2,1)} %get-tuple-element.37.weights_in, bf16[2176,128]{1,0:T(8,128)(2,1)S(1)} %bitcast.25), custom_call_target="tpu_custom_call" | custom-call | flops 303038464 | bytes 5500000 | tf_op jit(solution)/shard_map/attend_own/pallas_call | solution.py:380
  89.7 0.8 attend_other.1
  90.5 11.5 %all_to_all.21 = bf16[4,136,128]{2,1,0:T(8,128)(2,1)S(1)} all-to-all(bf16[4,136,128]{2,1,0:T(8,128)(2,1)S(1)} %bitcast.27), channel_id=1, replica_groups=mesh['zh'=2,'s'=2,'h'=4,'c'=2,'x'=4,'zl'=4] {'h'}, dimensions={0} | all-to-all | bytes 278528 | tf_op jit(solution)/shard_map/all_to_all | solution.py:414
  102.0 0.7 copy_bitcast_fusion
  (14 shorter events, 0.1 us)
Async XLA Ops:
  2.5 11.8 %collective-permute-start = (bf16[280,512]{1,0:T(8,128)(2,1)S(1)}, bf16[280,512]{1,0:T(8,128)(2,1)S(1)}, u32[]{:S(2)}, u32[]{:S(2)}) collective-permute-start(bf16[280,512]{1,0:T(8,128)(2,1)S(1)} %get-tuple-element.23.packed), channel_id=1, source_target_pairs={{0,16},{16,32},{32,48},{48,64},{64,80},{80,96},{96,112},{112,128},... | collective-permute-start | bytes 860168 | tf_op jit(solution)/shard_map/ppermute | solution.py:437
  4.3 36.7 %all-to-all-start = ((bf16[8,2,136,128]{3,2,1,0:T(8,128)(2,1)}), bf16[8,2,136,128]{3,2,1,0:T(8,128)(2,1)S(1)}, u32[]{:S(2)}, u32[]{:S(2)}) async-start(bf16[8,2,136,128]{3,2,1,0:T(8,128)(2,1)} %bitcast.30), calls=%async_computation | async-start | bytes 1114112 | tf_op jit(solution)/shard_map/all_to_all | solution.py:414
  14.4 38.8 %copy-start = (f32[512]{0:T(512)S(1)}, f32[512]{0:T(512)}, u32[]{:S(2)}) copy-start(f32[512]{0:T(512)} %param.15) | copy-start | bytes 6148
  17.6 23.4 %collective-permute-start.2 = (bf16[136,512]{1,0:T(8,128)(2,1)}, bf16[136,512]{1,0:T(8,128)(2,1)S(1)}, u32[]{:S(2)}, u32[]{:S(2)}) collective-permute-start(bf16[136,512]{1,0:T(8,128)(2,1)} %get-tuple-element.21.near), channel_id=1, source_target_pairs={{0,256},{1,257},{2,258},{3,259},{4,260},{5,261},{6,262},{7,263},{8... | collective-permute-start | bytes 417800 | tf_op jit(solution)/shard_map/ppermute | solution.py:441
  38.0 2.9 %collective-permute-start.1 = (f32[8,136]{1,0:T(8,128)S(1)}, f32[8,136]{1,0:T(8,128)S(1)}, u32[]{:S(2)}, u32[]{:S(2)}) collective-permute-start(f32[8,136]{1,0:T(8,128)S(1)} %get-tuple-element.32), channel_id=1, source_target_pairs={{0,256},{1,257},{2,258},{3,259},{4,260},{5,261},{6,262},{7,263},{8... | collective-permute-start | bytes 13064 | tf_op jit(solution)/shard_map/ppermute | solution.py:441
  55.3 29.0 %all-to-all-start.2 = ((bf16[8,272,128]{2,1,0:T(8,128)(2,1)}), bf16[8,272,128]{2,1,0:T(8,128)(2,1)S(1)}, u32[]{:S(2)}, u32[]{:S(2)}) async-start(bf16[8,272,128]{2,1,0:T(8,128)(2,1)} %bitcast.14), calls=%async_computation.2 | async-start | bytes 1114112 | tf_op jit(solution)/shard_map/all_to_all | solution.py:414
  58.9 16.8 %collective-permute-start.4 = (bf16[8,136,128]{2,1,0:T(8,128)(2,1)S(1)}, bf16[8,136,128]{2,1,0:T(8,128)(2,1)S(1)}, u32[]{:S(2)}, u32[]{:S(2)}) collective-permute-start(bf16[8,136,128]{2,1,0:T(8,128)(2,1)S(1)} %slice_bitcast_fusion.k0), channel_id=1, source_target_pairs={{0,256},{1,257},{2,258},{3,259},{4,260},{5,261},{6,262},{7,263},{8... | collective-permute-start | bytes 835592 | tf_op jit(solution)/shard_map/ppermute | solution.py:452
  67.9 9.8 %collective-permute-start.3 = (bf16[8,136,128]{2,1,0:T(8,128)(2,1)S(1)}, bf16[8,136,128]{2,1,0:T(8,128)(2,1)S(1)}, u32[]{:S(2)}, u32[]{:S(2)}) collective-permute-start(bf16[8,136,128]{2,1,0:T(8,128)(2,1)S(1)} %slice_bitcast_fusion.k0), channel_id=1, source_target_pairs={{0,16},{16,0},{1,17},{17,1},{2,18},{18,2},{3,19},{19,3},{4,20},{20... | collective-permute-start | bytes 835592 | tf_op jit(solution)/shard_map/ppermute | solution.py:418
  75.7 3.4 %collective-permute-start.5 = (bf16[8,136,128]{2,1,0:T(8,128)(2,1)S(1)}, bf16[8,136,128]{2,1,0:T(8,128)(2,1)S(1)}, u32[]{:S(2)}, u32[]{:S(2)}) collective-permute-start(bf16[8,136,128]{2,1,0:T(8,128)(2,1)S(1)} %collective-permute-done.4.k2), channel_id=1, source_target_pairs={{0,16},{16,0},{1,17},{17,1},{2,18},{18,2},{3,19},{19,3},{4,20},{20... | collective-permute-start | bytes 835592 | tf_op jit(solution)/shard_map/ppermute | solution.py:418
  84.3 5.4 %collective-permute-start.6 = (bf16[8,272,128]{2,1,0:T(8,128)(2,1)S(1)}, bf16[8,272,128]{2,1,0:T(8,128)(2,1)S(1)}, u32[]{:S(2)}, u32[]{:S(2)}) collective-permute-start(bf16[8,272,128]{2,1,0:T(8,128)(2,1)S(1)} %all-to-all-done.2), channel_id=1, source_target_pairs={{0,16},{16,0},{1,17},{17,1},{2,18},{18,2},{3,19},{19,3},{4,20},{20... | collective-permute-start | bytes 1671176 | tf_op jit(solution)/shard_map/ppermute | solution.py:418

commit v10 on v9

--- a/solution.py
+++ b/solution.py
@@ -444,12 +444,12 @@
     blocks, squares, far_stream = lax.optimization_barrier((blocks, squares, far_stream))
     gathered = exchange(squares, CHAN_AXES)
     packed = normalize(width, gathered, stream, far_stream, norm_gain.reshape(1, chans))
-    blocks, packed = lax.optimization_barrier((blocks, packed))
-    values_own = exchange(packed.reshape(8, 2 * rows, HD), ("s", "h"))
-
     keys_near = blocks[:, 0]
     my_queries = lax.dynamic_slice_in_dim(blocks, lax.axis_index("s") * heads, heads, 0)[:, 1]
     keys_far = lax.ppermute(keys_near, "zh", [(0, 1)])
+    packed, keys_far = lax.optimization_barrier((packed, keys_far))
+    values_own = exchange(packed.reshape(8, 2 * rows, HD), ("s", "h"))
+
     parts = [keys_near, swap_cores(keys_near), keys_far, swap_cores(keys_far)]
     weights, denom = score(place, my_queries.reshape(heads * rows, HD), parts)
     values_own, denom = lax.optimization_barrier((values_own, denom))

time: 103 us -> 103 us (level)
  the two profiles are of different devices: /device:TPU:64 before, /device:TPU:1 now
where the time goes in v10:
time: 103 us
  starting transfers between devices  53.5 us (52%)
  blocking collectives  22.2 us (22%)
  Pallas kernels  19.4 us (19%)
  waiting for transfers between devices  6.07 us (6%)
    all_to_all x2, blocking collectives, exchange(): return lax.all_to_all(value, axes, 0, 0, tiled=True)  22.2 us
    all_to_all x2, starting transfers between devices, exchange(): return lax.all_to_all(value, axes, 0, 0, tiled=True)  21.2 us
    ppermute x3, starting transfers between devices, swap_cores(): return lax.ppermute(value, 'c', [(0, 1), (1, 0)])  11.6 us
    ppermute x1, starting transfers between devices, shards(): keys_far = lax.ppermute(keys_near, 'zh', [(0, 1)])  9.36 us
    ppermute x2, starting transfers between devices, shards(): lax.ppermute(value, 'zh', [(0, 1)])  6.74 us
    pallas_call x1, Pallas kernels, score(): pl.pallas_call(score_kernel, in_specs=[pl.BlockSpec(memory_space=pltpu.SM...  5.19 us
    ppermute x1, starting transfers between devices, shards(): lax.ppermute(last, ROWS_AXES, [(source, source + 1) for source in range(c...  4.59 us
    all_to_all x2, waiting for transfers between devices, exchange(): return lax.all_to_all(value, axes, 0, 0, tiled=True)  3.58 us
  transfers between devices with their start and end apart: 9, of which 4 were waited for; matrix products, arithmetic and copies ran while one was open for 0% of the time, Pallas kernels for 16%

profile of v10, /device:TPU:1, one launch (start us, length us, event | category | flops | bytes accessed | tf_op | source)
XLA Modules:
  0.0 102.9 jit_solution(5204437973793974041)
XLA Ops:
  0.6 1.9 %pack.1 = (bf16[280,512]{1,0:T(8,128)(2,1)S(1)}, bf16[2,4,2,136,128]{4,3,2,1,0:T(8,128)(2,1)}) custom-call(bf16[136,512]{1,0:T(8,128)(2,1)} %gf.1, bf16[136,512]{1,0:T(8,128)(2,1)} %hv.1, bf16[136,512]{1,0:T(8,128)(2,1)} %gs.3, bf16[136,512]{1,0:T(8,128)(2,1)} %keys.1, bf16[136,512]{1,0:T(8,128)(2,1)} %queries.1), custom_call_target="tpu_custom_call" | custom-call | bytes 600000 | tf_op jit(solution)/shard_map/pack/pallas_call | solution.py:217
  2.5 4.6 %collective-permute-start = (bf16[280,512]{1,0:T(8,128)(2,1)S(1)}, bf16[280,512]{1,0:T(8,128)(2,1)S(1)}, u32[]{:S(2)}, u32[]{:S(2)}) collective-permute-start(bf16[280,512]{1,0:T(8,128)(2,1)S(1)} %get-tuple-element.23.packed), channel_id=1, source_target_pairs={{0,16},{16,32},{32,48},{48,64},{64,80},{80,96},{96,112},{112,128},... | collective-permute-start | bytes 860168 | tf_op jit(solution)/shard_map/ppermute | solution.py:437
  7.1 11.1 %all-to-all-start = ((bf16[8,2,136,128]{3,2,1,0:T(8,128)(2,1)}), bf16[8,2,136,128]{3,2,1,0:T(8,128)(2,1)S(1)}, u32[]{:S(2)}, u32[]{:S(2)}) async-start(bf16[8,2,136,128]{3,2,1,0:T(8,128)(2,1)} %bitcast.30), calls=%async_computation | async-start | bytes 1114112 | tf_op jit(solution)/shard_map/all_to_all | solution.py:414
  18.3 2.8 %early.1 = (f32[136,512]{1,0:T(8,128)S(1)}, f32[136,512]{1,0:T(8,128)S(1)}, bf16[136,512]{1,0:T(8,128)(2,1)S(1)}, f32[3,8,512]{2,1,0:T(8,128)S(1)}, f32[3,3,512]...) custom-call(bf16[280,512]{1,0:T(8,128)(2,1)S(1)} %get-tuple-element.23.packed, bf16[136,512]{1,0:T(8,128)(2,1)} %gs.3, ...), custom_call_target="tpu_custom_call" | custom-call | flops 20000000 | bytes 2000000 | tf_op jit(solution)/shard_map/early/pallas_call | solution.py:94
  21.0 3.3 %late.1 = (bf16[136,512]{1,0:T(8,128)(2,1)}, f32[8,136]{1,0:T(8,128)S(1)}) custom-call(bf16[280,512]{1,0:T(8,128)(2,1)S(1)} %collective-permute-done.halo, f32[136,512]{1,0:T(8,128)S(1)} %get-tuple-element.24.partial, f32[136,512]{1,0:T(8,128)S(1)} %get-tuple-element.25.feat, bf16[136,512]{1,0:T(8,128)(2,1)S(1)} %get-tuple-element.26.res, ...), custom_call_target="tpu_custom_call" | custom-call | flops 30000001024 | bytes 2000000 | tf_op jit(solution)/shard_map/late/pallas_call | solution.py:165
  24.3 5.4 %collective-permute-start.2 = (bf16[136,512]{1,0:T(8,128)(2,1)}, bf16[136,512]{1,0:T(8,128)(2,1)S(1)}, u32[]{:S(2)}, u32[]{:S(2)}) collective-permute-start(bf16[136,512]{1,0:T(8,128)(2,1)} %get-tuple-element.21.near), channel_id=1, source_target_pairs={{0,256},{1,257},{2,258},{3,259},{4,260},{5,261},{6,262},{7,263},{8... | collective-permute-start | bytes 417800 | tf_op jit(solution)/shard_map/ppermute | solution.py:441
  29.8 1.3 %collective-permute-start.1 = (f32[8,136]{1,0:T(8,128)S(1)}, f32[8,136]{1,0:T(8,128)S(1)}, u32[]{:S(2)}, u32[]{:S(2)}) collective-permute-start(f32[8,136]{1,0:T(8,128)S(1)} %get-tuple-element.32), channel_id=1, source_target_pairs={{0,256},{1,257},{2,258},{3,259},{4,260},{5,261},{6,262},{7,263},{8... | collective-permute-start | bytes 13064 | tf_op jit(solution)/shard_map/ppermute | solution.py:441
  31.1 1.0 collective-permute-done.1
  32.1 0.1 maximum_reduce_fusion
  32.2 0.9 all-to-all-done
  33.2 9.4 %collective-permute-start.4 = (bf16[8,136,128]{2,1,0:T(8,128)(2,1)S(1)}, bf16[8,136,128]{2,1,0:T(8,128)(2,1)S(1)}, u32[]{:S(2)}, u32[]{:S(2)}) collective-permute-start(bf16[8,136,128]{2,1,0:T(8,128)(2,1)S(1)} %slice_bitcast_fusion.k0), channel_id=1, source_target_pairs={{0,256},{1,257},{2,258},{3,259},{4,260},{5,261},{6,262},{7,263},{8... | collective-permute-start | bytes 835592 | tf_op jit(solution)/shard_map/ppermute | solution.py:449
  42.5 13.7 %all_to_all.20.gathered = f32[16,1,272]{2,1,0:T(1,128)S(1)} all-to-all(f32[16,1,272]{2,1,0:T(1,128)S(1)} %broadcast_in_dim.3), channel_id=1, replica_groups=mesh['zh'=2,'s'=2,'h'=4,'c'=2,'x'=4,'zl'=4] {'x','zl'}, dimensions={0} | all-to-all | bytes 34816 | tf_op jit(solution)/shard_map/all_to_all | solution.py:414
  56.2 2.2 %normalize.1 = bf16[2,4,2,136,128]{4,3,2,1,0:T(8,128)(2,1)} custom-call(f32[16,1,272]{2,1,0:T(1,128)S(1)} %all_to_all.20.gathered, bf16[136,512]{1,0:T(8,128)(2,1)} %get-tuple-element.21.near, bf16[136,512]{1,0:T(8,128)(2,1)S(1)} %collective-permute-done.2.far, f32[1,512]{1,0:T(1,128)S(1)} %bitcast.29), custom_call_target="tpu_custom_call" | custom-call | flops 1000000 | bytes 800000 | tf_op jit(solution)/shard_map/normalize/pallas_call | solution.py:258
  58.4 10.1 %all-to-all-start.2 = ((bf16[8,272,128]{2,1,0:T(8,128)(2,1)}), bf16[8,272,128]{2,1,0:T(8,128)(2,1)S(1)}, u32[]{:S(2)}, u32[]{:S(2)}) async-start(bf16[8,272,128]{2,1,0:T(8,128)(2,1)} %bitcast.14), calls=%async_computation.2 | async-start | bytes 1114112 | tf_op jit(solution)/shard_map/all_to_all | solution.py:414
  68.6 4.5 %collective-permute-start.3 = (bf16[8,136,128]{2,1,0:T(8,128)(2,1)S(1)}, bf16[8,136,128]{2,1,0:T(8,128)(2,1)S(1)}, u32[]{:S(2)}, u32[]{:S(2)}) collective-permute-start(bf16[8,136,128]{2,1,0:T(8,128)(2,1)S(1)} %slice_bitcast_fusion.k0), channel_id=1, source_target_pairs={{0,16},{16,0},{1,17},{17,1},{2,18},{18,2},{3,19},{19,3},{4,20},{20... | collective-permute-start | bytes 835592 | tf_op jit(solution)/shard_map/ppermute | solution.py:418
  73.1 1.9 %collective-permute-start.5 = (bf16[8,136,128]{2,1,0:T(8,128)(2,1)S(1)}, bf16[8,136,128]{2,1,0:T(8,128)(2,1)S(1)}, u32[]{:S(2)}, u32[]{:S(2)}) collective-permute-start(bf16[8,136,128]{2,1,0:T(8,128)(2,1)S(1)} %collective-permute-done.4.k2), channel_id=1, source_target_pairs={{0,16},{16,0},{1,17},{17,1},{2,18},{18,2},{3,19},{19,3},{4,20},{20... | collective-permute-start | bytes 835592 | tf_op jit(solution)/shard_map/ppermute | solution.py:418
  75.0 1.5 %collective-permute-done.5.k3 = bf16[8,136,128]{2,1,0:T(8,128)(2,1)S(1)} collective-permute-done((bf16[8,136,128]{2,1,0:T(8,128)(2,1)S(1)}, bf16[8,136,128]{2,1,0:T(8,128)(2,1)S(1)}, u32[]{:S(2)}, u32[]{:S(2)}) %collective-permute-start.5) | collective-permute-done | bytes 278560 | tf_op jit(solution)/shard_map/ppermute | solution.py:418
  76.5 5.2 %score.1 = (bf16[544,4352]{1,0:T(8,128)(2,1)}, f32[544,128]{1,0:T(8,128)S(1)}) custom-call(s32[10]{0:T(128)S(1)} %broadcast_multiply_fusion.place, bf16[544,128]{1,0:T(8,128)(2,1)S(1)} %bitcast.28, bf16[8,136,128]{2,1,0:T(8,128)(2,1)S(1)} %slice_bitcast_fusion.k0, bf16[8,136,128]{2,1,0:T(8,128)(2,1)S(1)} %collective-permute-done.3.k1, ...), custom_call_target="tpu_custom_call" | custom-call | flops 606076928 | bytes 8000000 | tf_op jit(solution)/shard_map/score/pallas_call | solution.py:326
  81.7 2.7 %all-to-all-done.2 = bf16[8,272,128]{2,1,0:T(8,128)(2,1)S(1)} async-done(((bf16[8,272,128]{2,1,0:T(8,128)(2,1)}), bf16[8,272,128]{2,1,0:T(8,128)(2,1)S(1)}, u32[]{:S(2)}, u32[]{:S(2)}) %all-to-all-start.2) | async-done | bytes 557088 | tf_op jit(solution)/shard_map/all_to_all | solution.py:414
  84.4 5.2 %collective-permute-start.6 = (bf16[8,272,128]{2,1,0:T(8,128)(2,1)S(1)}, bf16[8,272,128]{2,1,0:T(8,128)(2,1)S(1)}, u32[]{:S(2)}, u32[]{:S(2)}) collective-permute-start(bf16[8,272,128]{2,1,0:T(8,128)(2,1)S(1)} %all-to-all-done.2), channel_id=1, source_target_pairs={{0,16},{16,0},{1,17},{17,1},{2,18},{18,2},{3,19},{19,3},{4,20},{20... | collective-permute-start | bytes 1671176 | tf_op jit(solution)/shard_map/ppermute | solution.py:418
  89.5 3.3 %attend_own.1 = (f32[544,128]{1,0:T(8,128)S(1)}, bf16[544,2176]{1,0:T(8,128)(2,1)S(1)}) custom-call(bf16[544,4352]{1,0:T(8,128)(2,1)} %get-tuple-element.37.weights_in, bf16[2176,128]{1,0:T(8,128)(2,1)S(1)} %bitcast.25), custom_call_target="tpu_custom_call" | custom-call | flops 303038464 | bytes 5500000 | tf_op jit(solution)/shard_map/attend_own/pallas_call | solution.py:380
  92.9 0.8 attend_other.1
  93.7 8.6 %all_to_all.21 = bf16[4,136,128]{2,1,0:T(8,128)(2,1)S(1)} all-to-all(bf16[4,136,128]{2,1,0:T(8,128)(2,1)S(1)} %bitcast.27), channel_id=1, replica_groups=mesh['zh'=2,'s'=2,'h'=4,'c'=2,'x'=4,'zl'=4] {'h'}, dimensions={0} | all-to-all | bytes 278528 | tf_op jit(solution)/shard_map/all_to_all | solution.py:414
  102.2 0.7 copy_bitcast_fusion
  (14 shorter events, 0.2 us)
Async XLA Ops:
  2.5 18.5 %collective-permute-start = (bf16[280,512]{1,0:T(8,128)(2,1)S(1)}, bf16[280,512]{1,0:T(8,128)(2,1)S(1)}, u32[]{:S(2)}, u32[]{:S(2)}) collective-permute-start(bf16[280,512]{1,0:T(8,128)(2,1)S(1)} %get-tuple-element.23.packed), channel_id=1, source_target_pairs={{0,16},{16,32},{32,48},{48,64},{64,80},{80,96},{96,112},{112,128},... | collective-permute-start | bytes 860168 | tf_op jit(solution)/shard_map/ppermute | solution.py:437
  7.1 26.0 %all-to-all-start = ((bf16[8,2,136,128]{3,2,1,0:T(8,128)(2,1)}), bf16[8,2,136,128]{3,2,1,0:T(8,128)(2,1)S(1)}, u32[]{:S(2)}, u32[]{:S(2)}) async-start(bf16[8,2,136,128]{3,2,1,0:T(8,128)(2,1)} %bitcast.30), calls=%async_computation | async-start | bytes 1114112 | tf_op jit(solution)/shard_map/all_to_all | solution.py:414
  21.0 35.2 %copy-start = (f32[512]{0:T(512)S(1)}, f32[512]{0:T(512)}, u32[]{:S(2)}) copy-start(f32[512]{0:T(512)} %param.15) | copy-start | bytes 6148
  24.3 7.9 %collective-permute-start.2 = (bf16[136,512]{1,0:T(8,128)(2,1)}, bf16[136,512]{1,0:T(8,128)(2,1)S(1)}, u32[]{:S(2)}, u32[]{:S(2)}) collective-permute-start(bf16[136,512]{1,0:T(8,128)(2,1)} %get-tuple-element.21.near), channel_id=1, source_target_pairs={{0,256},{1,257},{2,258},{3,259},{4,260},{5,261},{6,262},{7,263},{8... | collective-permute-start | bytes 417800 | tf_op jit(solution)/shard_map/ppermute | solution.py:441
  29.8 2.3 %collective-permute-start.1 = (f32[8,136]{1,0:T(8,128)S(1)}, f32[8,136]{1,0:T(8,128)S(1)}, u32[]{:S(2)}, u32[]{:S(2)}) collective-permute-start(f32[8,136]{1,0:T(8,128)S(1)} %get-tuple-element.32), channel_id=1, source_target_pairs={{0,256},{1,257},{2,258},{3,259},{4,260},{5,261},{6,262},{7,263},{8... | collective-permute-start | bytes 13064 | tf_op jit(solution)/shard_map/ppermute | solution.py:441
  33.2 25.2 %collective-permute-start.4 = (bf16[8,136,128]{2,1,0:T(8,128)(2,1)S(1)}, bf16[8,136,128]{2,1,0:T(8,128)(2,1)S(1)}, u32[]{:S(2)}, u32[]{:S(2)}) collective-permute-start(bf16[8,136,128]{2,1,0:T(8,128)(2,1)S(1)} %slice_bitcast_fusion.k0), channel_id=1, source_target_pairs={{0,256},{1,257},{2,258},{3,259},{4,260},{5,261},{6,262},{7,263},{8... | collective-permute-start | bytes 835592 | tf_op jit(solution)/shard_map/ppermute | solution.py:449
  58.4 26.0 %all-to-all-start.2 = ((bf16[8,272,128]{2,1,0:T(8,128)(2,1)}), bf16[8,272,128]{2,1,0:T(8,128)(2,1)S(1)}, u32[]{:S(2)}, u32[]{:S(2)}) async-start(bf16[8,272,128]{2,1,0:T(8,128)(2,1)} %bitcast.14), calls=%async_computation.2 | async-start | bytes 1114112 | tf_op jit(solution)/shard_map/all_to_all | solution.py:414
  68.6 6.5 %collective-permute-start.3 = (bf16[8,136,128]{2,1,0:T(8,128)(2,1)S(1)}, bf16[8,136,128]{2,1,0:T(8,128)(2,1)S(1)}, u32[]{:S(2)}, u32[]{:S(2)}) collective-permute-start(bf16[8,136,128]{2,1,0:T(8,128)(2,1)S(1)} %slice_bitcast_fusion.k0), channel_id=1, source_target_pairs={{0,16},{16,0},{1,17},{17,1},{2,18},{18,2},{3,19},{19,3},{4,20},{20... | collective-permute-start | bytes 835592 | tf_op jit(solution)/shard_map/ppermute | solution.py:418
  73.1 3.5 %collective-permute-start.5 = (bf16[8,136,128]{2,1,0:T(8,128)(2,1)S(1)}, bf16[8,136,128]{2,1,0:T(8,128)(2,1)S(1)}, u32[]{:S(2)}, u32[]{:S(2)}) collective-permute-start(bf16[8,136,128]{2,1,0:T(8,128)(2,1)S(1)} %collective-permute-done.4.k2), channel_id=1, source_target_pairs={{0,16},{16,0},{1,17},{17,1},{2,18},{18,2},{3,19},{19,3},{4,20},{20... | collective-permute-start | bytes 835592 | tf_op jit(solution)/shard_map/ppermute | solution.py:418
  84.4 8.5 %collective-permute-start.6 = (bf16[8,272,128]{2,1,0:T(8,128)(2,1)S(1)}, bf16[8,272,128]{2,1,0:T(8,128)(2,1)S(1)}, u32[]{:S(2)}, u32[]{:S(2)}) collective-permute-start(bf16[8,272,128]{2,1,0:T(8,128)(2,1)S(1)} %all-to-all-done.2), channel_id=1, source_target_pairs={{0,16},{16,0},{1,17},{17,1},{2,18},{18,2},{3,19},{19,3},{4,20},{20... | collective-permute-start | bytes 1671176 | tf_op jit(solution)/shard_map/ppermute | solution.py:418

commit v11 on v10

--- a/solution.py
+++ b/solution.py
@@ -41,12 +41,12 @@
 
 
 def head_lanes(head):
-    return pl.ds(pl.multiple_of(head * HD, HD), HD)
+    return slice(head * HD, (head + 1) * HD)
 
 
 def early_kernel(
     packed, gs, res, taps_in, long_in, partial, feat, res_out, edge, taps_out, long_out,
-    gs_v, ext, prod, copies, sems,
+    gs_v, exts, prods, all_copies, sems,
 ):
     rows, chans = gs.shape
     loads = [(taps_in, taps_out), (long_in, long_out), (gs, gs_v), (res, res_out)]
@@ -58,11 +58,12 @@
     tiles = rows // 8
     pairs = [(tile, group) for group in range(long_in.shape[0] // 8) for tile in range(group, tiles)]
     top = lax.broadcasted_iota(jnp.int32, (rows, HD), 0) < 2
-    ext[0:8, :] = jnp.zeros((8, HD), jnp.float32)
-    prod[0:8, :] = jnp.zeros((8, HD), jnp.float32)
-
-    def one_head(head, carry):
+
+    def one_head(head):
         lanes = head_lanes(head)
+        ext, prod, copies = exts.at[head], prods.at[head], all_copies.at[head]
+        ext[0:8, :] = jnp.zeros((8, HD), jnp.float32)
+        prod[0:8, :] = jnp.zeros((8, HD), jnp.float32)
         taps = taps_out[:, :, lanes]
 
         def feature(index, raw):
@@ -78,9 +79,9 @@
         shift_copies(prod, copies)
         totals = lag_sums(long_out[:, lanes], copies, 8, pairs)
         partial[:, lanes] = jnp.concatenate(totals, axis=0)
-        return carry
-
-    lax.fori_loop(0, chans // HD, one_head, 0)
+
+    for head in range(chans // HD):
+        one_head(head)
 
 
 def in_hbm(*arrays):
@@ -89,6 +90,7 @@
 
 def early(packed, gs, res, taps, long_taps):
     rows, chans = gs.shape
+    heads = chans // HD
     hbm = pl.BlockSpec(memory_space=pltpu.HBM)
     vmem = pl.BlockSpec(memory_space=pltpu.VMEM)
     return pl.pallas_call(
@@ -105,9 +107,9 @@
         ],
         scratch_shapes=[
             pltpu.VMEM((rows, chans), jnp.bfloat16),
-            pltpu.VMEM((rows + 8, HD), jnp.float32),
-            pltpu.VMEM((rows + 8, HD), jnp.float32),
-            pltpu.VMEM((8, rows + 8, HD), jnp.float32),
+            pltpu.VMEM((heads, rows + 8, HD), jnp.float32),
+            pltpu.VMEM((heads, rows + 8, HD), jnp.float32),
+            pltpu.VMEM((heads, 8, rows + 8, HD), jnp.float32),
             pltpu.SemaphoreType.DMA((4,)),
         ],
         compiler_params=pltpu.CompilerParams(vmem_limit_bytes=32 << 20),
@@ -116,17 +118,18 @@
     )(packed, *in_hbm(gs, res, taps, long_taps))
 
 
-def late_kernel(halo, partial, feat, res, edge, taps_in, long_in, stream, squares, ext, prod, copies):
+def late_kernel(halo, partial, feat, res, edge, taps_in, long_in, stream, squares, exts, prods, all_copies):
     rows, chans = res.shape
     tiles = rows // 8
     pairs = [(tile, group) for group in range(long_in.shape[0] // 8) for tile in range(min(group + 2, tiles))]
     inside = lax.broadcasted_iota(jnp.int32, (rows, HD), 0) < rows - 6
-    prod[0:8, :] = jnp.zeros((8, HD), jnp.float32)
-    prod[rows + 8 :, :] = jnp.zeros((8, HD), jnp.float32)
     total = jnp.zeros((8, rows), jnp.float32)
 
     def one_head(head, total):
         lanes = head_lanes(head)
+        ext, prod, copies = exts.at[head], prods.at[head], all_copies.at[head]
+        prod[0:8, :] = jnp.zeros((8, HD), jnp.float32)
+        prod[rows + 8 :, :] = jnp.zeros((8, HD), jnp.float32)
         taps = taps_in[:, :, lanes]
 
         def feature(index, begin):
@@ -155,12 +158,14 @@
         )
         return total
 
-    total = lax.fori_loop(0, chans // HD, one_head, total)
+    for head in range(chans // HD):
+        total = one_head(head, total)
     squares[...] = total
 
 
 def late(halo, partial, feat, res, edge, taps, long_taps):
     rows, chans = res.shape
+    heads = chans // HD
     vmem = pl.BlockSpec(memory_space=pltpu.VMEM)
     return pl.pallas_call(
         late_kernel,
@@ -171,9 +176,9 @@
             jax.ShapeDtypeStruct((8, rows), jnp.float32),
         ],
         scratch_shapes=[
-            pltpu.VMEM((rows + 8, HD), jnp.float32),
-            pltpu.VMEM((rows + 16, HD), jnp.float32),
-            pltpu.VMEM((8, rows + 16, HD), jnp.float32),
+            pltpu.VMEM((heads, rows + 8, HD), jnp.float32),
+            pltpu.VMEM((heads, rows + 16, HD), jnp.float32),
+            pltpu.VMEM((heads, 8, rows + 16, HD), jnp.float32),
         ],
         compiler_params=pltpu.CompilerParams(vmem_limit_bytes=32 << 20),
         cost_estimate=pl.CostEstimate(flops=30_000_000_000, bytes_accessed=2_000_000, transcendentals=0),
@@ -438,10 +443,12 @@
     early_parts = early(last, gate_second, residual, short_taps, long_taps)
     stream, squares = late(halo, *early_parts)
 
-    far_stream, far_squares = [lax.ppermute(value, "zh", [(0, 1)]) for value in (stream, squares)]
+    far_squares = lax.ppermute(squares, "zh", [(0, 1)])
+    far_squares, sent = lax.optimization_barrier((far_squares, stream))
+    far_stream = lax.ppermute(sent, "zh", [(0, 1)])
     squares = jnp.concatenate([squares[0:1], far_squares[0:1]], axis=1)
     squares = jnp.broadcast_to(squares, (16, 1, 2 * rows))
-    blocks, squares, far_stream = lax.optimization_barrier((blocks, squares, far_stream))
+    blocks, squares = lax.optimization_barrier((blocks, squares))
     gathered = exchange(squares, CHAN_AXES)
     packed = normalize(width, gathered, stream, far_stream, norm_gain.reshape(1, chans))
     keys_near = blocks[:, 0]

time: 103 us -> 105 us (1.019)
  waiting for transfers between devices: 6.07 us -> 20.7 us
  blocking collectives: 22.2 us -> 8.56 us
    all_to_all x2 -> x3, waiting for transfers between devices: 3.58 us -> 18.5 us  [exchange(): return lax.all_to_all(value, axes, 0, 0, tiled=True)]
    all_to_all x2 -> x1, blocking collectives: 22.2 us -> 8.56 us  [exchange(): return lax.all_to_all(value, axes, 0, 0, tiled=True)]
    all_to_all x2 -> x3, starting transfers between devices: 21.2 us -> 21.5 us  [exchange(): return lax.all_to_all(value, axes, 0, 0, tiled=True)]
  transfers between devices with their start and end apart: 9 -> 10, of which waited for: 4 -> 5; matrix products, arithmetic and copies ran while one was open for 0% -> 0% of each run, Pallas kernels for 16% -> 16%
where the time goes in v11:
time: 105 us; the launch traced here: 104 us
  starting transfers between devices  53.7 us (51%)
  waiting for transfers between devices  20.7 us (20%)
  Pallas kernels  18.9 us (18%)
  blocking collectives  8.56 us (8%)
  local copies, waits for them, and re-layouts  1.43 us (1%)
    all_to_all x3, starting transfers between devices, exchange(): return lax.all_to_all(value, axes, 0, 0, tiled=True)  21.5 us
    all_to_all x3, waiting for transfers between devices, exchange(): return lax.all_to_all(value, axes, 0, 0, tiled=True)  18.5 us
    ppermute x3, starting transfers between devices, swap_cores(): return lax.ppermute(value, 'c', [(0, 1), (1, 0)])  11.5 us
    ppermute x1, starting transfers between devices, shards(): keys_far = lax.ppermute(keys_near, 'zh', [(0, 1)])  9.36 us
    all_to_all x1, blocking collectives, exchange(): return lax.all_to_all(value, axes, 0, 0, tiled=True)  8.56 us
    ppermute x1, starting transfers between devices, shards(): far_squares = lax.ppermute(squares, 'zh', [(0, 1)])  5.44 us
    pallas_call x1, Pallas kernels, score(): pl.pallas_call(score_kernel, in_specs=[pl.BlockSpec(memory_space=pltpu.SM...  5.18 us
    ppermute x1, starting transfers between devices, shards(): lax.ppermute(last, ROWS_AXES, [(source, source + 1) for source in range(c...  4.59 us
  transfers between devices with their start and end apart: 10, of which 5 were waited for; matrix products, arithmetic and copies ran while one was open for 0% of the time, Pallas kernels for 16%

profile of v11, /device:TPU:1, one launch (start us, length us, event | category | flops | bytes accessed | tf_op | source)
XLA Modules:
  0.0 104.2 jit_solution(6438226176204093674)
XLA Ops:
  0.6 1.9 %pack.1 = (bf16[280,512]{1,0:T(8,128)(2,1)S(1)}, bf16[2,4,2,136,128]{4,3,2,1,0:T(8,128)(2,1)}) custom-call(bf16[136,512]{1,0:T(8,128)(2,1)} %gf.1, bf16[136,512]{1,0:T(8,128)(2,1)} %hv.1, bf16[136,512]{1,0:T(8,128)(2,1)} %gs.3, bf16[136,512]{1,0:T(8,128)(2,1)} %keys.1, bf16[136,512]{1,0:T(8,128)(2,1)} %queries.1), custom_call_target="tpu_custom_call" | custom-call | bytes 600000 | tf_op jit(solution)/shard_map/pack/pallas_call | solution.py:222
  2.5 4.6 %collective-permute-start = (bf16[280,512]{1,0:T(8,128)(2,1)S(1)}, bf16[280,512]{1,0:T(8,128)(2,1)S(1)}, u32[]{:S(2)}, u32[]{:S(2)}) collective-permute-start(bf16[280,512]{1,0:T(8,128)(2,1)S(1)} %get-tuple-element.24.packed), channel_id=1, source_target_pairs={{0,16},{16,32},{32,48},{48,64},{64,80},{80,96},{96,112},{112,128},... | collective-permute-start | bytes 860168 | tf_op jit(solution)/shard_map/ppermute | solution.py:442
  7.2 11.1 %all-to-all-start = ((bf16[8,2,136,128]{3,2,1,0:T(8,128)(2,1)}), bf16[8,2,136,128]{3,2,1,0:T(8,128)(2,1)S(1)}, u32[]{:S(2)}, u32[]{:S(2)}) async-start(bf16[8,2,136,128]{3,2,1,0:T(8,128)(2,1)} %bitcast.30), calls=%async_computation | async-start | bytes 1114112 | tf_op jit(solution)/shard_map/all_to_all | solution.py:419
  18.3 2.7 %early.1 = (f32[136,512]{1,0:T(8,128)S(1)}, f32[136,512]{1,0:T(8,128)S(1)}, bf16[136,512]{1,0:T(8,128)(2,1)S(1)}, f32[3,8,512]{2,1,0:T(8,128)S(1)}, f32[3,3,512]...) custom-call(bf16[280,512]{1,0:T(8,128)(2,1)S(1)} %get-tuple-element.24.packed, bf16[136,512]{1,0:T(8,128)(2,1)} %gs.3, ...), custom_call_target="tpu_custom_call" | custom-call | flops 20000000 | bytes 2000000 | tf_op jit(solution)/shard_map/early/pallas_call | solution.py:96
  21.0 2.8 %late.1 = (bf16[136,512]{1,0:T(8,128)(2,1)}, f32[8,136]{1,0:T(8,128)S(1)}) custom-call(bf16[280,512]{1,0:T(8,128)(2,1)S(1)} %collective-permute-done.halo, f32[136,512]{1,0:T(8,128)S(1)} %get-tuple-element.25.partial, f32[136,512]{1,0:T(8,128)S(1)} %get-tuple-element.26.feat, bf16[136,512]{1,0:T(8,128)(2,1)S(1)} %get-tuple-element.27.res, ...), custom_call_target="tpu_custom_call" | custom-call | flops 30000001024 | bytes 2000000 | tf_op jit(solution)/shard_map/late/pallas_call | solution.py:170
  23.8 5.4 %collective-permute-start.1 = (f32[8,136]{1,0:T(8,128)S(1)}, f32[8,136]{1,0:T(8,128)S(1)}, u32[]{:S(2)}, u32[]{:S(2)}) collective-permute-start(f32[8,136]{1,0:T(8,128)S(1)} %get-tuple-element.33), channel_id=1, source_target_pairs={{0,256},{1,257},{2,258},{3,259},{4,260},{5,261},{6,262},{7,263},{8... | collective-permute-start | bytes 13064 | tf_op jit(solution)/shard_map/ppermute | solution.py:446
  29.3 0.8 collective-permute-done.1
  30.2 3.0 %all-to-all-done = bf16[8,2,136,128]{3,2,1,0:T(8,128)(2,1)S(1)} async-done(((bf16[8,2,136,128]{3,2,1,0:T(8,128)(2,1)}), bf16[8,2,136,128]{3,2,1,0:T(8,128)(2,1)S(1)}, u32[]{:S(2)}, u32[]{:S(2)}) %all-to-all-start) | async-done | bytes 557088 | tf_op jit(solution)/shard_map/all_to_all | solution.py:419
  33.8 9.4 %collective-permute-start.4 = (bf16[8,136,128]{2,1,0:T(8,128)(2,1)S(1)}, bf16[8,136,128]{2,1,0:T(8,128)(2,1)S(1)}, u32[]{:S(2)}, u32[]{:S(2)}) collective-permute-start(bf16[8,136,128]{2,1,0:T(8,128)(2,1)S(1)} %slice_bitcast_fusion.k0), channel_id=1, source_target_pairs={{0,256},{1,257},{2,258},{3,259},{4,260},{5,261},{6,262},{7,263},{8... | collective-permute-start | bytes 835592 | tf_op jit(solution)/shard_map/ppermute | solution.py:456
  43.1 1.3 %collective-permute-start.3 = (bf16[136,512]{1,0:T(8,128)(2,1)}, bf16[136,512]{1,0:T(8,128)(2,1)S(1)}, u32[]{:S(2)}, u32[]{:S(2)}) collective-permute-start(bf16[136,512]{1,0:T(8,128)(2,1)} %get-tuple-element.37.near), channel_id=1, source_target_pairs={{0,256},{1,257},{2,258},{3,259},{4,260},{5,261},{6,262},{7,263},{8... | collective-permute-start | bytes 417800 | tf_op jit(solution)/shard_map/ppermute | solution.py:448
  44.5 6.9 %all-to-all-start.1 = ((f32[16,1,272]{2,1,0:T(1,128)}), f32[16,1,272]{2,1,0:T(1,128)S(1)}, u32[]{:S(2)}, u32[]{:S(2)}) async-start(f32[16,1,272]{2,1,0:T(1,128)} %broadcast_in_dim.3), calls=%async_computation.1 | async-start | bytes 49152 | tf_op jit(solution)/shard_map/all_to_all | solution.py:419
  51.3 12.9 %all-to-all-done.1.gathered = f32[16,1,272]{2,1,0:T(1,128)S(1)} async-done(((f32[16,1,272]{2,1,0:T(1,128)}), f32[16,1,272]{2,1,0:T(1,128)S(1)}, u32[]{:S(2)}, u32[]{:S(2)}) %all-to-all-start.1) | async-done | bytes 17440 | tf_op jit(solution)/shard_map/all_to_all | solution.py:419
  64.2 2.2 %normalize.1 = bf16[2,4,2,136,128]{4,3,2,1,0:T(8,128)(2,1)} custom-call(f32[16,1,272]{2,1,0:T(1,128)S(1)} %all-to-all-done.1.gathered, bf16[136,512]{1,0:T(8,128)(2,1)} %get-tuple-element.37.near, bf16[136,512]{1,0:T(8,128)(2,1)S(1)} %collective-permute-done.3.far, f32[1,512]{1,0:T(1,128)S(1)} %bitcast.29), custom_call_target="tpu_custom_call" | custom-call | flops 1000000 | bytes 800000 | tf_op jit(solution)/shard_map/normalize/pallas_call | solution.py:263
  66.3 3.5 %all-to-all-start.2 = ((bf16[8,272,128]{2,1,0:T(8,128)(2,1)}), bf16[8,272,128]{2,1,0:T(8,128)(2,1)S(1)}, u32[]{:S(2)}, u32[]{:S(2)}) async-start(bf16[8,272,128]{2,1,0:T(8,128)(2,1)} %bitcast.14), calls=%async_computation.2 | async-start | bytes 1114112 | tf_op jit(solution)/shard_map/all_to_all | solution.py:419
  70.0 4.4 %collective-permute-start.2 = (bf16[8,136,128]{2,1,0:T(8,128)(2,1)S(1)}, bf16[8,136,128]{2,1,0:T(8,128)(2,1)S(1)}, u32[]{:S(2)}, u32[]{:S(2)}) collective-permute-start(bf16[8,136,128]{2,1,0:T(8,128)(2,1)S(1)} %slice_bitcast_fusion.k0), channel_id=1, source_target_pairs={{0,16},{16,0},{1,17},{17,1},{2,18},{18,2},{3,19},{19,3},{4,20},{20... | collective-permute-start | bytes 835592 | tf_op jit(solution)/shard_map/ppermute | solution.py:423
  74.4 1.9 %collective-permute-start.5 = (bf16[8,136,128]{2,1,0:T(8,128)(2,1)S(1)}, bf16[8,136,128]{2,1,0:T(8,128)(2,1)S(1)}, u32[]{:S(2)}, u32[]{:S(2)}) collective-permute-start(bf16[8,136,128]{2,1,0:T(8,128)(2,1)S(1)} %collective-permute-done.4.k2), channel_id=1, source_target_pairs={{0,16},{16,0},{1,17},{17,1},{2,18},{18,2},{3,19},{19,3},{4,20},{20... | collective-permute-start | bytes 835592 | tf_op jit(solution)/shard_map/ppermute | solution.py:423
  76.4 1.5 %collective-permute-done.5.k3 = bf16[8,136,128]{2,1,0:T(8,128)(2,1)S(1)} collective-permute-done((bf16[8,136,128]{2,1,0:T(8,128)(2,1)S(1)}, bf16[8,136,128]{2,1,0:T(8,128)(2,1)S(1)}, u32[]{:S(2)}, u32[]{:S(2)}) %collective-permute-start.5) | collective-permute-done | bytes 278560 | tf_op jit(solution)/shard_map/ppermute | solution.py:423
  77.8 5.2 %score.1 = (bf16[544,4352]{1,0:T(8,128)(2,1)}, f32[544,128]{1,0:T(8,128)S(1)}) custom-call(s32[10]{0:T(128)S(1)} %broadcast_multiply_fusion.place, bf16[544,128]{1,0:T(8,128)(2,1)S(1)} %bitcast.28, bf16[8,136,128]{2,1,0:T(8,128)(2,1)S(1)} %slice_bitcast_fusion.k0, bf16[8,136,128]{2,1,0:T(8,128)(2,1)S(1)} %collective-permute-done.2.k1, ...), custom_call_target="tpu_custom_call" | custom-call | flops 606076928 | bytes 8000000 | tf_op jit(solution)/shard_map/score/pallas_call | solution.py:331
  83.0 2.7 %all-to-all-done.2 = bf16[8,272,128]{2,1,0:T(8,128)(2,1)S(1)} async-done(((bf16[8,272,128]{2,1,0:T(8,128)(2,1)}), bf16[8,272,128]{2,1,0:T(8,128)(2,1)S(1)}, u32[]{:S(2)}, u32[]{:S(2)}) %all-to-all-start.2) | async-done | bytes 557088 | tf_op jit(solution)/shard_map/all_to_all | solution.py:419
  85.7 5.2 %collective-permute-start.6 = (bf16[8,272,128]{2,1,0:T(8,128)(2,1)S(1)}, bf16[8,272,128]{2,1,0:T(8,128)(2,1)S(1)}, u32[]{:S(2)}, u32[]{:S(2)}) collective-permute-start(bf16[8,272,128]{2,1,0:T(8,128)(2,1)S(1)} %all-to-all-done.2), channel_id=1, source_target_pairs={{0,16},{16,0},{1,17},{17,1},{2,18},{18,2},{3,19},{19,3},{4,20},{20... | collective-permute-start | bytes 1671176 | tf_op jit(solution)/shard_map/ppermute | solution.py:423
  90.9 3.3 %attend_own.1 = (f32[544,128]{1,0:T(8,128)S(1)}, bf16[544,2176]{1,0:T(8,128)(2,1)S(1)}) custom-call(bf16[544,4352]{1,0:T(8,128)(2,1)} %get-tuple-element.39.weights_in, bf16[2176,128]{1,0:T(8,128)(2,1)S(1)} %bitcast.25), custom_call_target="tpu_custom_call" | custom-call | flops 303038464 | bytes 5500000 | tf_op jit(solution)/shard_map/attend_own/pallas_call | solution.py:385
  94.2 0.8 attend_other.1
  95.0 8.6 %all_to_all.20 = bf16[4,136,128]{2,1,0:T(8,128)(2,1)S(1)} all-to-all(bf16[4,136,128]{2,1,0:T(8,128)(2,1)S(1)} %bitcast.27), channel_id=1, replica_groups=mesh['zh'=2,'s'=2,'h'=4,'c'=2,'x'=4,'zl'=4] {'h'}, dimensions={0} | all-to-all | bytes 278528 | tf_op jit(solution)/shard_map/all_to_all | solution.py:419
  103.6 0.7 copy_bitcast_fusion
  (15 shorter events, 0.9 us)
Async XLA Ops:
  2.5 18.5 %collective-permute-start = (bf16[280,512]{1,0:T(8,128)(2,1)S(1)}, bf16[280,512]{1,0:T(8,128)(2,1)S(1)}, u32[]{:S(2)}, u32[]{:S(2)}) collective-permute-start(bf16[280,512]{1,0:T(8,128)(2,1)S(1)} %get-tuple-element.24.packed), channel_id=1, source_target_pairs={{0,16},{16,32},{32,48},{48,64},{64,80},{80,96},{96,112},{112,128},... | collective-permute-start | bytes 860168 | tf_op jit(solution)/shard_map/ppermute | solution.py:442
  7.2 26.0 %all-to-all-start = ((bf16[8,2,136,128]{3,2,1,0:T(8,128)(2,1)}), bf16[8,2,136,128]{3,2,1,0:T(8,128)(2,1)S(1)}, u32[]{:S(2)}, u32[]{:S(2)}) async-start(bf16[8,2,136,128]{3,2,1,0:T(8,128)(2,1)} %bitcast.30), calls=%async_computation | async-start | bytes 1114112 | tf_op jit(solution)/shard_map/all_to_all | solution.py:419
  21.0 43.2 %copy-start = (f32[512]{0:T(512)S(1)}, f32[512]{0:T(512)}, u32[]{:S(2)}) copy-start(f32[512]{0:T(512)} %param.15) | copy-start | bytes 6148
  23.8 6.2 %collective-permute-start.1 = (f32[8,136]{1,0:T(8,128)S(1)}, f32[8,136]{1,0:T(8,128)S(1)}, u32[]{:S(2)}, u32[]{:S(2)}) collective-permute-start(f32[8,136]{1,0:T(8,128)S(1)} %get-tuple-element.33), channel_id=1, source_target_pairs={{0,256},{1,257},{2,258},{3,259},{4,260},{5,261},{6,262},{7,263},{8... | collective-permute-start | bytes 13064 | tf_op jit(solution)/shard_map/ppermute | solution.py:446
  33.8 32.6 %collective-permute-start.4 = (bf16[8,136,128]{2,1,0:T(8,128)(2,1)S(1)}, bf16[8,136,128]{2,1,0:T(8,128)(2,1)S(1)}, u32[]{:S(2)}, u32[]{:S(2)}) collective-permute-start(bf16[8,136,128]{2,1,0:T(8,128)(2,1)S(1)} %slice_bitcast_fusion.k0), channel_id=1, source_target_pairs={{0,256},{1,257},{2,258},{3,259},{4,260},{5,261},{6,262},{7,263},{8... | collective-permute-start | bytes 835592 | tf_op jit(solution)/shard_map/ppermute | solution.py:456
  43.1 8.2 %collective-permute-start.3 = (bf16[136,512]{1,0:T(8,128)(2,1)}, bf16[136,512]{1,0:T(8,128)(2,1)S(1)}, u32[]{:S(2)}, u32[]{:S(2)}) collective-permute-start(bf16[136,512]{1,0:T(8,128)(2,1)} %get-tuple-element.37.near), channel_id=1, source_target_pairs={{0,256},{1,257},{2,258},{3,259},{4,260},{5,261},{6,262},{7,263},{8... | collective-permute-start | bytes 417800 | tf_op jit(solution)/shard_map/ppermute | solution.py:448
  44.5 19.7 %all-to-all-start.1 = ((f32[16,1,272]{2,1,0:T(1,128)}), f32[16,1,272]{2,1,0:T(1,128)S(1)}, u32[]{:S(2)}, u32[]{:S(2)}) async-start(f32[16,1,272]{2,1,0:T(1,128)} %broadcast_in_dim.3), calls=%async_computation.1 | async-start | bytes 49152 | tf_op jit(solution)/shard_map/all_to_all | solution.py:419
  66.3 19.3 %all-to-all-start.2 = ((bf16[8,272,128]{2,1,0:T(8,128)(2,1)}), bf16[8,272,128]{2,1,0:T(8,128)(2,1)S(1)}, u32[]{:S(2)}, u32[]{:S(2)}) async-start(bf16[8,272,128]{2,1,0:T(8,128)(2,1)} %bitcast.14), calls=%async_computation.2 | async-start | bytes 1114112 | tf_op jit(solution)/shard_map/all_to_all | solution.py:419
  70.0 6.4 %collective-permute-start.2 = (bf16[8,136,128]{2,1,0:T(8,128)(2,1)S(1)}, bf16[8,136,128]{2,1,0:T(8,128)(2,1)S(1)}, u32[]{:S(2)}, u32[]{:S(2)}) collective-permute-start(bf16[8,136,128]{2,1,0:T(8,128)(2,1)S(1)} %slice_bitcast_fusion.k0), channel_id=1, source_target_pairs={{0,16},{16,0},{1,17},{17,1},{2,18},{18,2},{3,19},{19,3},{4,20},{20... | collective-permute-start | bytes 835592 | tf_op jit(solution)/shard_map/ppermute | solution.py:423
  74.4 3.5 %collective-permute-start.5 = (bf16[8,136,128]{2,1,0:T(8,128)(2,1)S(1)}, bf16[8,136,128]{2,1,0:T(8,128)(2,1)S(1)}, u32[]{:S(2)}, u32[]{:S(2)}) collective-permute-start(bf16[8,136,128]{2,1,0:T(8,128)(2,1)S(1)} %collective-permute-done.4.k2), channel_id=1, source_target_pairs={{0,16},{16,0},{1,17},{17,1},{2,18},{18,2},{3,19},{19,3},{4,20},{20... | collective-permute-start | bytes 835592 | tf_op jit(solution)/shard_map/ppermute | solution.py:423
  85.7 8.5 %collective-permute-start.6 = (bf16[8,272,128]{2,1,0:T(8,128)(2,1)S(1)}, bf16[8,272,128]{2,1,0:T(8,128)(2,1)S(1)}, u32[]{:S(2)}, u32[]{:S(2)}) collective-permute-start(bf16[8,272,128]{2,1,0:T(8,128)(2,1)S(1)} %all-to-all-done.2), channel_id=1, source_target_pairs={{0,16},{16,0},{1,17},{17,1},{2,18},{18,2},{3,19},{19,3},{4,20},{20... | collective-permute-start | bytes 1671176 | tf_op jit(solution)/shard_map/ppermute | solution.py:423
